TPU v7x, 32 devices: a whole 2x2x4 slice. The times are simulated.
32 devices in a mesh: tok: 16 (over z, x, core), head: 2 (over y).
Axes of the slice: x: 2, y: 2, z: 4, core: 2. Of those that a mesh axis runs over, the one named last changes fastest.
Arguments:
- hidden: bfloat16 [4096, 1536], P(('tok', 'head')), may hold values from -6 to 6
- attn_gain: float32 [1536], replicated, may hold values from 0.1 to 1.9
- w_qkv: bfloat16 [1536, 2560], P(None, 'head'), may hold values from -11 to 11
- kv_cache: bfloat16 [4096, 1024], P('tok', 'head'), may hold values from -38 to 38
- page_table: int32 [256], replicated, may hold values from 0 to 255, each once
- lengths: int32 [64], replicated, may hold values from 1 to 256, as said below
- request_group: int32 [64], replicated, may hold values from 0 to 1
- key_mask: int32 [4096], replicated, may hold values 0 or 1
- o_weight: bfloat16 [1536, 1536], replicated, may hold values from -3.5 to 3.5
- moe_gain: float32 [1536], replicated, may hold values from 0.1 to 1.9
- router: bfloat16 [1536, 16], replicated, may hold values from -151 to 151
- routes: int32 [4096, 8], P(('tok', 'head')), may hold values from 0 to 15, all different within a row; in each aligned block of 128 rows (0 to 127, 128 to 255, ...) at most 96 rows name the same one
- w_gate_up: bfloat16 [16, 1536, 1024], P('tok'), may hold values from -0.21875 to 0.21875
- w_down: bfloat16 [16, 512, 1536], P('tok'), may hold values from -0.5 to 0.5
Outputs:
- attn_branch: bfloat16 [4096, 1536], P(('tok', 'head'))
- layer_out: bfloat16 [4096, 1536], P(('tok', 'head'))
Inputs may be any that keep to these rules, and one draw needn't show every extreme that they name: `page_table`: each page appears once. The lengths sum to 4096; the largest is exactly 256. `routes`: the 8 experts of a token differ. Among the rows of one device no expert is named more than 96 times, and in every draw some expert is named exactly 96 times among some device's rows.
All inputs are finite; a program needn't handle non-finite values.
Results may differ from a plain program's by a relative error of at most 0.015.
Values may be sent and summed in bfloat16 or wider, within the bound.
No kernel may reach another device: no remote copies, remote signals or barrier semaphores. Data moves between devices by JAX's collectives and lax.ppermute only.
A program may use at most 192 MiB of HBM per device.

v0:
```python
import jax
import jax.numpy as jnp
from jax import lax
from jax.sharding import PartitionSpec as P

D = 1536
HEADS = 24
KVH = 8
HD = 64
FFE = 512
TOPK = 8
PREFIX = 2048
GROUPS = 2
PAGE = 16


EPSILON = 1e-06
ROPE_BASE = 10000.0
MASKED = -1e30


def shifted(array, axis, by):
    count = lax.axis_size(axis)
    pairs = [(i, i + by) for i in range(count) if 0 <= i + by < count]
    return lax.ppermute(array, axis, pairs)


def rms_scale(states, gain_vec):
    widened = states.astype(jnp.float32)
    return (
        widened
        * lax.rsqrt(jnp.mean(widened * widened, axis=-1, keepdims=True) + EPSILON)
        * gain_vec
    )


def rotate(states, position):
    half_dim = states.shape[-1] // 2
    inv_freq = ROPE_BASE ** (-2.0 * jnp.arange(half_dim, dtype=jnp.float32) / (2 * half_dim))
    angles = position[:, None] * inv_freq[None, :]
    cosine = jnp.cos(angles)[:, None, :]
    sine_part = jnp.sin(angles)[:, None, :]
    lower_half = states[..., :half_dim]
    upper_half = states[..., half_dim:]
    return jnp.concatenate(
        [
            lower_half * cosine - upper_half * sine_part,
            upper_half * cosine + lower_half * sine_part,
        ],
        axis=-1,
    )


def token_info(token_ids, lengths, request_group):
    starts = jnp.cumsum(lengths) - lengths
    request = jnp.sum((starts[None, :] <= token_ids[:, None]).astype(jnp.int32), axis=1) - 1
    member = request[:, None] == jnp.arange(starts.shape[0], dtype=jnp.int32)[None, :]
    start_of = jnp.sum(jnp.where(member, starts[None, :], 0), axis=1)
    group_of = jnp.sum(jnp.where(member, request_group[None, :], 0), axis=1)
    return (request, start_of, group_of)


def page_groups(page_table):
    n_pages = page_table.shape[0]
    slot_group = jnp.arange(n_pages, dtype=jnp.int32) // (n_pages // GROUPS)
    member = page_table[:, None] == jnp.arange(n_pages, dtype=jnp.int32)[None, :]
    return jnp.sum(jnp.where(member, slot_group[:, None], 0), axis=0)


def absorb(carry, queries, keys_values, allowed_keys):
    running, denominator, numerator = carry
    scores = jnp.einsum(
        "tgqd,ngd->tgqn", queries, keys_values[:, :, 0], preferred_element_type=jnp.float32
    ) * HD ** (-0.5)
    allowed = allowed_keys[:, None, None, :]
    scores = jnp.where(allowed, scores, MASKED)
    new_running = jnp.maximum(running, jnp.max(scores, axis=-1))
    weights = jnp.where(allowed, jnp.exp(scores - new_running[..., None]), 0.0)
    rescale = jnp.exp(running - new_running)
    denominator = denominator * rescale + jnp.sum(weights, axis=-1)
    numerator = numerator * rescale[..., None] + jnp.einsum(
        "tgqn,ngd->tgqd",
        weights.astype(jnp.bfloat16),
        keys_values[:, :, 1],
        preferred_element_type=jnp.float32,
    )
    return (new_running, denominator, numerator)


def absorb_blocks(carry, queries, keys_values, allowed_keys):
    key_count = keys_values.shape[0]
    width_block = min(key_count, 1024)
    for offset in range(0, key_count, width_block):
        carry = absorb(
            carry,
            queries,
            keys_values[offset : offset + width_block],
            allowed_keys[:, offset : offset + width_block],
        )
    return carry


def per_device(
    hidden,
    attn_gain,
    w_qkv,
    kv_cache,
    page_table,
    lengths,
    request_group,
    key_mask,
    o_weight,
    moe_gain,
    router,
    routes,
    w_gate_up,
    w_down,
):
    n_tok = lax.axis_size("tok")
    n_head = lax.axis_size("head")
    tok_dev = hidden.shape[0]
    row_tokens = tok_dev * n_head
    group_heads = HEADS // KVH
    kv_dev = w_qkv.shape[1] // ((group_heads + 2) * HD)
    heads_dev = kv_dev * group_heads
    row_index = lax.axis_index("tok")
    head_index = lax.axis_index("head")
    row_states = lax.all_gather(hidden, "head", axis=0, tiled=True)
    normed = rms_scale(row_states, attn_gain).astype(jnp.bfloat16)
    projected = jnp.dot(normed, w_qkv, preferred_element_type=jnp.float32).reshape(
        row_tokens, kv_dev, group_heads + 2, HD
    )
    row_first = row_index * row_tokens
    own_index = row_first + jnp.arange(row_tokens, dtype=jnp.int32)
    own_request, own_start, own_group = token_info(own_index, lengths, request_group)
    position = (PREFIX + own_index - own_start).astype(jnp.float32)
    queries = (
        rotate(projected[:, :, :group_heads].reshape(row_tokens, heads_dev, HD), position)
        .reshape(row_tokens, kv_dev, group_heads, HD)
        .astype(jnp.bfloat16)
    )
    keys_rot = rotate(projected[:, :, group_heads], position)
    values_raw = projected[:, :, group_heads + 1]
    own_kv = (
        jnp.stack([keys_rot, values_raw], axis=2)
        .astype(jnp.bfloat16)
        .reshape(row_tokens, kv_dev * 2 * HD)
    )
    prior_kv = shifted(own_kv, "tok", 1)
    window = jnp.concatenate([prior_kv, own_kv], axis=0).reshape(2 * row_tokens, kv_dev, 2, HD)
    window_pos = row_first - row_tokens + jnp.arange(2 * row_tokens, dtype=jnp.int32)
    window_request = token_info(jnp.maximum(window_pos, 0), lengths, request_group)[0]
    mask_padded = jnp.concatenate([jnp.zeros((row_tokens,), jnp.int32), key_mask])
    window_mask = lax.dynamic_slice_in_dim(mask_padded, row_first, 2 * row_tokens)
    suffix_allowed = (
        ((window_pos >= 0) & (window_mask == 1))[None, :]
        & (window_request[None, :] == own_request[:, None])
        & (window_pos[None, :] <= own_index[:, None])
    )
    page_group = page_groups(page_table)
    n_pages = page_table.shape[0]
    start_carry = (
        jnp.full((row_tokens, kv_dev, group_heads), MASKED, jnp.float32),
        jnp.zeros((row_tokens, kv_dev, group_heads), jnp.float32),
        jnp.zeros((row_tokens, kv_dev, group_heads, HD), jnp.float32),
    )
    piece = lax.all_gather(kv_cache, "tok", axis=0, tiled=True)
    key_count = piece.shape[0]
    page_of = jnp.arange(key_count, dtype=jnp.int32) // PAGE
    member = page_of[:, None] == jnp.arange(n_pages, dtype=jnp.int32)[None, :]
    piece_group = jnp.sum(jnp.where(member, page_group[None, :], 0), axis=1)
    allowed_keys = own_group[:, None] == piece_group[None, :]
    carry = absorb_blocks(
        start_carry, queries, piece.reshape(key_count, kv_dev, 2, HD), allowed_keys
    )
    running, denominator, numerator = absorb_blocks(carry, queries, window, suffix_allowed)
    context = (
        (numerator / denominator[..., None])
        .astype(jnp.bfloat16)
        .reshape(row_tokens, heads_dev * HD)
    )
    rows_out = lax.dynamic_slice_in_dim(o_weight, head_index * heads_dev * HD, heads_dev * HD, 0)
    attn_sum = lax.psum_scatter(
        jnp.dot(context, rows_out, preferred_element_type=jnp.float32).astype(jnp.bfloat16),
        "head",
        scatter_dimension=0,
        tiled=True,
    )
    mid_states = (hidden.astype(jnp.float32) + attn_sum.astype(jnp.float32)).astype(jnp.bfloat16)
    mixed = rms_scale(mid_states, moe_gain).astype(jnp.bfloat16)
    logits = jnp.dot(mixed, router, preferred_element_type=jnp.float32)
    experts = router.shape[1]
    route_hits3 = routes[:, :, None] == jnp.arange(experts, dtype=jnp.int32)[None, None, :]
    picked = jnp.sum(jnp.where(route_hits3, logits[:, None, :], 0.0), axis=-1)
    gate_probs = jax.nn.softmax(picked, axis=-1)
    exp_dev = w_gate_up.shape[0]
    capacity = min(tok_dev, 3 * tok_dev * TOPK // (2 * experts))
    flat_routes = routes.reshape(-1)
    route_hits = (flat_routes[:, None] == jnp.arange(experts, dtype=jnp.int32)[None, :]).astype(
        jnp.int32
    )
    slot_index = jnp.sum(jnp.cumsum(route_hits, axis=0) * route_hits, axis=1) - 1
    target = flat_routes * capacity + slot_index
    source = jnp.repeat(mixed, TOPK, axis=0)
    outgoing = jnp.zeros((experts * capacity, D), jnp.bfloat16).at[target].set(source)
    outgoing = outgoing.reshape(n_tok, exp_dev, capacity, D)
    joined = jnp.einsum(
        "sxcd,xdf->sxcf",
        lax.all_to_all(outgoing, "tok", split_axis=0, concat_axis=0, tiled=True),
        w_gate_up,
        preferred_element_type=jnp.float32,
    )
    activated = (jax.nn.silu(joined[..., :FFE]) * joined[..., FFE:]).astype(jnp.bfloat16)
    result = jnp.einsum(
        "sxcf,xfd->sxcd", activated, w_down, preferred_element_type=jnp.float32
    ).astype(jnp.bfloat16)
    returned = lax.all_to_all(result, "tok", split_axis=0, concat_axis=0, tiled=True)
    back_rows = returned.reshape(experts * capacity, D)
    picked_rows = back_rows[target].astype(jnp.float32).reshape(tok_dev, TOPK, D)
    routed_sum = jnp.sum(picked_rows * gate_probs[:, :, None], axis=1)
    layer_out = (mid_states.astype(jnp.float32) + routed_sum).astype(jnp.bfloat16)
    return (attn_sum, layer_out)


def solution(mesh):
    return jax.shard_map(
        per_device,
        mesh=mesh,
        in_specs=(
            P(("tok", "head"), None),
            P(),
            P(None, "head"),
            P("tok", "head"),
            P(),
            P(),
            P(),
            P(),
            P(),
            P(),
            P(),
            P(("tok", "head"), None),
            P("tok", None, None),
            P("tok", None, None),
        ),
        out_specs=(P(("tok", "head"), None), P(("tok", "head"), None)),
        check_vma=False,
    )
```

profile of v0, /device:TPU:11, one launch (start us, length us, event | category | flops | bytes accessed | tf_op | source)
XLA Modules:
  0.0 425.1 jit_solution(12991347437842822446)
XLA Ops:
  13.5 11.1 %all_gather.6 = bf16[256,1536]{1,0:T(8,128)(2,1)S(1)} all-gather(bf16[128,1536]{1,0:T(8,128)(2,1)} %param.14), channel_id=1, replica_groups=mesh['tok'=16,'head'=2] {'head'}, dimensions={0}, use_global_device_ids=true | all-gather | bytes 1179648 | tf_op jit(solution)/shard_map/all_gather | solution.py:128
  25.0 3.9 fusion.111
  30.5 4.5 %collective-permute-start = (bf16[256,512]{0,1:T(8,128)(2,1)}, bf16[256,512]{0,1:T(8,128)(2,1)}, u32[]{:S(2)}, u32[]{:S(2)}) collective-permute-start(bf16[256,512]{0,1:T(8,128)(2,1)} %bitcast.42), channel_id=1, source_target_pairs={{0,2},{2,4},{4,6},{6,8},{8,10},{10,12},{12,14},{14,16},{16,18},{18... | collective-permute-start | bytes 786440 | tf_op jit(solution)/shard_map/ppermute | solution.py:25
  44.8 5.3 %fusion.33 = (f32[256,4,3]{0,2,1:T(4,128)}, f32[4,512,256,3]{2,1,3,0:T(8,128)}) fusion(pred[256,512]{0,1:T(8,128)(4,1)S(1)} %compare_and_fusion, bf16[256,4,3,64]{0,3,2,1:T(8,128)(2,1)S(1)} %bitcast.294, bf16[256,4,2,64]{0,3,1,2:T(8,128)(2,1)} %copy-done.8, bf16[256,4,2,64]{0,3,2,1:T(8,128)(2,1)} %bitcast.43), kind=kOutput, calls=%fused_computation.46 | convolution fusion | flops 206566400 | bytes 7352320 | tf_op jit(solution)/shard_map/tgqd,ngd->tgqn/dot_general | solution.py:72
  50.1 12.2 %all-gather.2.cloned.1.call-done = bf16[4096,512]{0,1:T(8,128)(2,1)} async-done(((bf16[256,512]{0,1:T(8,128)(2,1)}), bf16[4096,512]{0,1:T(8,128)(2,1)}) %all-gather.2.cloned.1.call-update) | async-done | bytes 4194320 | tf_op jit(solution)/shard_map/all_gather | solution.py:167
  62.3 2.7 fusion.158
  65.0 6.6 %bitcast_reduce_fusion.3 = (f32[256,4,3]{0,2,1:T(4,128)S(1)}, f32[4,256,3,1024]{3,1,2,0:T(8,128)}) fusion(pred[256,1024]{1,0:T(8,128)(4,1)S(1)} %copy-done.4, bf16[256,4,3,64]{0,3,2,1:T(8,128)(2,1)S(1)} %bitcast.295, bf16[1024,4,2,64]{0,3,2,1:T(8,128)(2,1)S(1)} %bitcast.308), kind=kOutput, calls=%fused_computation.15 | convolution fusion | flops 412087296 | bytes 13774848 | tf_op jit(solution)/shard_map/tgqd,ngd->tgqn/dot_general | solution.py:72
  73.9 6.5 %bitcast_reduce_fusion.1 = (f32[256,4,3]{0,2,1:T(4,128)S(1)}, f32[4,256,3,1024]{3,1,2,0:T(8,128)}) fusion(pred[256,1024]{1,0:T(8,128)(4,1)S(1)} %copy-done.2, bf16[256,4,3,64]{0,3,2,1:T(8,128)(2,1)S(1)} %bitcast.297, bf16[1024,4,2,64]{0,3,2,1:T(8,128)(2,1)S(1)} %bitcast.304), kind=kOutput, calls=%fused_computation.7 | convolution fusion | flops 412087296 | bytes 13774848 | tf_op jit(solution)/shard_map/tgqd,ngd->tgqn/dot_general | solution.py:72
  80.4 6.7 %bitcast_reduce_fusion.2 = (f32[256,4,3]{0,2,1:T(4,128)S(1)}, f32[4,256,3,1024]{3,1,2,0:T(8,128)}) fusion(pred[256,1024]{1,0:T(8,128)(4,1)S(1)} %copy-done.3, bf16[256,4,3,64]{0,3,2,1:T(8,128)(2,1)S(1)} %bitcast.298, bf16[1024,4,2,64]{0,3,2,1:T(8,128)(2,1)S(1)} %bitcast.306), kind=kOutput, calls=%fused_computation.11 | convolution fusion | flops 412087296 | bytes 13774848 | tf_op jit(solution)/shard_map/tgqd,ngd->tgqn/dot_general | solution.py:72
  90.0 13.1 %fusion.8 = (f32[256,4,3]{0,2,1:T(4,128)}, f32[256,4,3]{0,2,1:T(4,128)}) fusion(f32[4,256,3,1024]{3,1,2,0:T(8,128)} %get-tuple-element.38, f32[256,4,3]{0,2,1:T(4,128)S(1)} %get-tuple-element.26, pred[256,1024]{1,0:T(8,128)(4,1)S(1)} %copy-done.4, f32[256,4,3]{0,2,1:T(4,128)S(1)} %get-tuple-element.12, f32[4,256,3,1024]{3,1,2,0:T(8,128)} %get-tuple-element.36, ...), kind=kLoop, calls=%fused_computation.22 | loop fusion | flops 31451136 | bytes 25739264 | tf_op jit(solution)/shard_map/reduce_sum | solution.py:80
  103.1 10.2 %fusion.12 = (f32[256,4,3]{0,2,1:T(4,128)}, f32[256,4,3]{0,2,1:T(4,128)}) fusion(f32[4,256,3,1024]{3,1,2,0:T(8,128)} %get-tuple-element.34, f32[256,4,3]{0,2,1:T(4,128)S(1)} %get-tuple-element.11, pred[256,1024]{1,0:T(8,128)(4,1)S(1)} %copy-done.2, f32[256,4,3]{0,2,1:T(4,128)S(1)} %get-tuple-element.10, f32[4,256,3,1024]{3,1,2,0:T(8,128)S(1)} %get-tuple-element.32, ...), kind=kLoop, calls=%fused_computation.26 | loop fusion | flops 31451136 | bytes 25739264 | tf_op jit(solution)/shard_map/reduce_sum | solution.py:80
  114.2 6.4 %fusion.98 = f32[256,4,3,64]{0,3,2,1:T(8,128)S(1)} fusion(f32[4,256,3,1024]{3,1,2,0:T(8,128)} %get-tuple-element.38, f32[256,4,3]{0,2,1:T(4,128)S(1)} %get-tuple-element.26, pred[256,1024]{1,0:T(8,128)(4,1)S(1)} %copy-done.4, bf16[1024,4,2,64]{0,3,2,1:T(8,128)(2,1)S(1)} %bitcast.309, f32[256,4,3]{0,2,1:T(4,128)S(1)} %get-tuple-element.8, ...), kind=kOutput, calls=%fused_computation.87 | convolution fusion | flops 418775040 | bytes 14462976 | tf_op jit(solution)/shard_map/tgqn,ngd->tgqd/dot_general | solution.py:81
  120.6 6.4 %fusion.92 = f32[256,4,3,64]{0,3,2,1:T(8,128)S(1)} fusion(f32[256,4,3,64]{0,3,2,1:T(8,128)S(1)} %fusion.98, f32[4,256,3,1024]{3,1,2,0:T(8,128)} %get-tuple-element.36, f32[256,4,3]{0,2,1:T(4,128)S(1)} %get-tuple-element.12, pred[256,1024]{1,0:T(8,128)(4,1)S(1)} %copy-done.3, bf16[1024,4,2,64]{0,3,2,1:T(8,128)(2,1)S(1)} %bitcast.307, ...), kind=kOutput, calls=%fused_computation.85 | convolution fusion | flops 418775040 | bytes 15237120 | tf_op jit(solution)/shard_map/tgqn,ngd->tgqd/dot_general | solution.py:81
  127.0 6.7 %fusion.86 = f32[256,4,3,64]{0,3,2,1:T(8,128)S(1)} fusion(f32[256,4,3,64]{0,3,2,1:T(8,128)S(1)} %fusion.92, f32[4,256,3,1024]{3,1,2,0:T(8,128)} %get-tuple-element.34, f32[256,4,3]{0,2,1:T(4,128)S(1)} %get-tuple-element.11, pred[256,1024]{1,0:T(8,128)(4,1)S(1)} %copy-done.2, bf16[1024,4,2,64]{0,3,2,1:T(8,128)(2,1)S(1)} %bitcast.305, ...), kind=kOutput, calls=%fused_computation.83 | convolution fusion | flops 418775040 | bytes 15237120 | tf_op jit(solution)/shard_map/tgqn,ngd->tgqd/dot_general | solution.py:81
  133.7 3.1 fusion.80
  145.1 9.3 %reduce-window.20 = s32[16,8,128]{2,1,0:T(8,128)} reduce-window(s32[16,8,128]{2,1,0:T(8,128)} %fusion.128, s32[]{:T(128)} %constant.43.clone.1), window={size=1x1x128 pad=0_0x0_0x127_0}, to_apply=%region_19.20 | reduce-window | flops 2080768 | bytes 131076 | tf_op jit(solution)/shard_map/reduce-window.1
  163.6 8.6 %scatter_custom_fusion = bf16[1536,1536]{1,0:T(8,128)(2,1)} fusion(s32[1024]{0:T(1024)S(1)} %bitcast.315, bf16[]{:T(256)} %constant.106.clone.1, bf16[128,1536]{1,0:T(8,128)(2,1)} %fusion.109), kind=kCustom, calls=%fused_computation.57 | custom fusion | bytes 5111810 | tf_op jit(solution)/shard_map/scatter | solution.py:205
  172.2 110.4 %all_to_all.10 = bf16[16,1,96,1536]{3,2,1,0:T(8,128)(2,1)S(1)} all-to-all(bf16[16,1,96,1536]{3,2,1,0:T(8,128)(2,1)} %bitcast.293), channel_id=1, replica_groups=mesh['tok'=16,'head'=2] {'tok'}, dimensions={0} | all-to-all | bytes 9437184 | tf_op jit(solution)/shard_map/all_to_all | solution.py:209
  282.6 5.4 %fusion.45 = f32[16,1,96,1024]{3,2,0,1:T(8,128)S(1)} fusion(bf16[1,1536,1024]{2,1,0:T(8,128)(2,1)S(1)} %copy-done, bf16[16,1,96,1536]{3,2,1,0:T(8,128)(2,1)S(1)} %all_to_all.10), kind=kOutput, calls=%fused_computation.61 | convolution fusion | flops 4831838208 | bytes 14155776 | tf_op jit(solution)/shard_map/sxcd,xdf->sxcf/dot_general | solution.py:207
  288.1 4.3 %convert_bitcast_fusion = bf16[16,1,96,1536]{3,2,1,0:T(8,128)(2,1)} fusion(bf16[1,512,1536]{2,1,0:T(8,128)(2,1)S(1)} %copy-done.21, f32[16,1,96,1024]{3,2,0,1:T(8,128)S(1)} %fusion.45), kind=kOutput, calls=%fused_computation.49 | convolution fusion | flops 2422996992 | bytes 12582912 | tf_op jit(solution)/shard_map/sxcf,xfd->sxcd/dot_general | solution.py:214
  292.3 5.1 %all-to-all-start.1 = ((bf16[16,1,96,1536]{3,2,1,0:T(8,128)(2,1)}), bf16[16,1,96,1536]{3,2,1,0:T(8,128)(2,1)}, u32[]{:S(2)}, u32[]{:S(2)}) async-start(bf16[16,1,96,1536]{3,2,1,0:T(8,128)(2,1)} %convert_bitcast_fusion), calls=%async_computation.2 | async-start | bytes 9437184 | tf_op jit(solution)/shard_map/all_to_all | solution.py:217
  299.5 101.7 %all-to-all-done.1 = bf16[16,1,96,1536]{3,2,1,0:T(8,128)(2,1)} async-done(((bf16[16,1,96,1536]{3,2,1,0:T(8,128)(2,1)}), bf16[16,1,96,1536]{3,2,1,0:T(8,128)(2,1)}, u32[]{:S(2)}, u32[]{:S(2)}) %all-to-all-start.1) | async-done | bytes 4718624 | tf_op jit(solution)/shard_map/all_to_all | solution.py:217
  401.1 10.2 %gather_fusion = bf16[1024,1536]{1,0:T(8,128)(2,1)} fusion(bf16[1536,1536]{1,0:T(8,128)(2,1)} %bitcast.74, s32[1024]{0:T(1024)S(1)} %broadcast_clamp_fusion), kind=kCustom, calls=%fused_computation | custom fusion | bytes 6295552 | tf_op jit(solution)/shard_map/gather | solution.py:219
  411.3 4.7 %fusion.16 = f32[128,1536]{1,0:T(8,128)S(1)} fusion(bf16[1024,1536]{1,0:T(8,128)(2,1)} %gather_fusion, f32[128,8]{1,0:T(8,128)} %copy.95), kind=kLoop, calls=%fused_computation.31 | loop fusion | flops 4521984 | bytes 3936256 | tf_op jit(solution)/shard_map/reduce_sum | solution.py:220
  (128 shorter events, 45.2 us)
Async XLA Ops:
  7.2 275.5 %copy-start = (bf16[1,1536,1024]{2,1,0:T(8,128)(2,1)S(1)}, bf16[1,1536,1024]{2,1,0:T(8,128)(2,1)}, u32[]{:S(2)}) copy-start(bf16[1,1536,1024]{2,1,0:T(8,128)(2,1)} %param.26) | copy-start | bytes 9437188
  7.2 55.1 %all-gather.2.cloned.1.call-start = ((), (), s32[]{:S(2)}) async-start(), calls=%async_computation.3 | async-start | bytes 4456448 | tf_op jit(solution)/shard_map/all_gather | solution.py:167
  9.2 151.2 %reduce-scatter.2.cloned.1.call-start = ((), (), s32[]{:S(2)}) async-start(), calls=%async_computation.4 | async-start | bytes 1179648 | tf_op jit(solution)/shard_map/reduce_scatter | solution.py:183
  13.5 23.1 %copy-start.20 = (s32[256]{0:T(256)S(1)}, s32[256]{0:T(256)}, u32[]{:S(2)}) copy-start(s32[256]{0:T(256)} %param.18) | copy-start | bytes 3076
  28.9 13.7 %copy-start.16 = (s32[4096]{0:T(1024)S(1)}, s32[4096]{0:T(1024)}, u32[]{:S(2)}) copy-start(s32[4096]{0:T(1024)} %param.21) | copy-start | bytes 49156
  30.5 13.7 %collective-permute-start = (bf16[256,512]{0,1:T(8,128)(2,1)}, bf16[256,512]{0,1:T(8,128)(2,1)}, u32[]{:S(2)}, u32[]{:S(2)}) collective-permute-start(bf16[256,512]{0,1:T(8,128)(2,1)} %bitcast.42), channel_id=1, source_target_pairs={{0,2},{2,4},{4,6},{6,8},{8,10},{10,12},{12,14},{14,16},{16,18},{18... | collective-permute-start | bytes 786440 | tf_op jit(solution)/shard_map/ppermute | solution.py:25
  65.0 6.7 %copy-start.6 = (bf16[1024,512]{0,1:T(8,128)(2,1)}, bf16[1024,512]{0,1:T(8,128)(2,1)S(1)}, u32[]{:S(2)}) copy-start(bf16[1024,512]{0,1:T(8,128)(2,1)S(1)} %get-tuple-element.16) | copy-start | bytes 3145732
  65.0 6.7 %copy-start.1 = (pred[256,1024]{1,0:T(8,128)(4,1)S(1)}, pred[256,1024]{1,0:T(8,128)(4,1)}, u32[]{:S(2)}) copy-start(pred[256,1024]{1,0:T(8,128)(4,1)} %get-tuple-element.18) | copy-start | bytes 786436
  71.6 15.4 %copy-start.13 = (f32[256,4,3]{0,2,1:T(4,128)}, f32[256,4,3]{0,2,1:T(4,128)S(1)}, u32[]{:S(2)}) copy-start(f32[256,4,3]{0,2,1:T(4,128)S(1)} %get-tuple-element.37) | copy-start | bytes 36868
  73.8 6.6 %copy-start.3 = (pred[256,1024]{1,0:T(8,128)(4,1)S(1)}, pred[256,1024]{1,0:T(8,128)(4,1)}, u32[]{:S(2)}) copy-start(pred[256,1024]{1,0:T(8,128)(4,1)} %get-tuple-element.17) | copy-start | bytes 786436
  73.8 13.9 %slice-start = ((s8[6291456]{0:T(1024)(128)(4,1)}), s8[4194304]{0:T(1024)(128)(4,1)S(1)}, s32[]{:S(2)}) async-start(s8[6291456]{0:T(1024)(128)(4,1)} %bitcast.299), calls=%async_computation.5 | async-start | bytes 8388608
  80.4 6.7 %copy-start.17 = (f32[256,4,3]{0,2,1:T(4,128)S(1)}, f32[256,4,3]{0,2,1:T(4,128)}, u32[]{:S(2)}) copy-start(f32[256,4,3]{0,2,1:T(4,128)} %get-tuple-element.29) | copy-start | bytes 36868
  80.4 7.3 %slice-start.1 = ((s8[6291456]{0:T(1024)(128)(4,1)}), s8[2097152]{0:T(1024)(128)(4,1)S(1)}, s32[]{:S(2)}) async-start(s8[6291456]{0:T(1024)(128)(4,1)} %bitcast.299), calls=%async_computation.6 | async-start | bytes 4194304
  80.4 7.3 %copy-start.11 = (pred[256,512]{0,1:T(8,128)(4,1)S(1)}, pred[256,512]{0,1:T(8,128)(4,1)}, u32[]{:S(2)}) copy-start(pred[256,512]{0,1:T(8,128)(4,1)} %copy-done.10) | copy-start | bytes 393220
  103.1 10.2 %copy-start.14 = (f32[256,4,3]{0,2,1:T(4,128)S(1)}, f32[256,4,3]{0,2,1:T(4,128)}, u32[]{:S(2)}) copy-start(f32[256,4,3]{0,2,1:T(4,128)} %copy-done.13) | copy-start | bytes 36868
  103.1 11.0 %copy-start.7 = (bf16[1024,512]{0,1:T(8,128)(2,1)S(1)}, bf16[1024,512]{0,1:T(8,128)(2,1)}, u32[]{:S(2)}) copy-start(bf16[1024,512]{0,1:T(8,128)(2,1)} %copy-done.6) | copy-start | bytes 3145732
  127.0 12.5 %slice-start.2 = ((s8[4718592]{0:T(1024)(128)(4,1)}), s8[524288]{0:T(1024)(128)(4,1)S(1)}, s32[]{:S(2)}) async-start(s8[4718592]{0:T(1024)(128)(4,1)} %bitcast.319), calls=%async_computation.7 | async-start | bytes 1048576
  133.7 3.2 copy-start.9
  133.7 3.2 copy-start.12
  133.7 5.8 %slice-start.3 = ((s8[4718592]{0:T(1024)(128)(4,1)}), s8[4194304]{0:T(1024)(128)(4,1)S(1)}, s32[]{:S(2)}) async-start(s8[4718592]{0:T(1024)(128)(4,1)} %bitcast.319), calls=%async_computation.8 | async-start | bytes 8388608
  136.9 23.6 %copy-start.5 = (bf16[128,1536]{1,0:T(8,128)(2,1)S(1)}, bf16[128,1536]{1,0:T(8,128)(2,1)}, u32[]{:S(2)}) copy-start(bf16[128,1536]{1,0:T(8,128)(2,1)} %param.14) | copy-start | bytes 1179652
  282.6 5.4 %copy-start.21 = (bf16[1,512,1536]{2,1,0:T(8,128)(2,1)S(1)}, bf16[1,512,1536]{2,1,0:T(8,128)(2,1)}, u32[]{:S(2)}) copy-start(bf16[1,512,1536]{2,1,0:T(8,128)(2,1)} %param.27) | copy-start | bytes 4718596
  292.3 6.3 %copy-start.15 = (s32[128,8]{0,1:T(8,128)S(1)}, s32[128,8]{0,1:T(8,128)}, u32[]{:S(2)}) copy-start(s32[128,8]{0,1:T(8,128)} %param.25) | copy-start | bytes 12292
  292.3 108.8 %all-to-all-start.1 = ((bf16[16,1,96,1536]{3,2,1,0:T(8,128)(2,1)}), bf16[16,1,96,1536]{3,2,1,0:T(8,128)(2,1)}, u32[]{:S(2)}, u32[]{:S(2)}) async-start(bf16[16,1,96,1536]{3,2,1,0:T(8,128)(2,1)} %convert_bitcast_fusion), calls=%async_computation.2 | async-start | bytes 9437184 | tf_op jit(solution)/shard_map/all_to_all | solution.py:217
  (6 other events, 7.3 us)
Sparse Core Ops, SparseCore 0:
  10.2 52.0 all-gather.1
  141.3 17.7 reduce-scatter.1
where the time goes:
time: 430 us; the launch traced here: 425 us
  blocking collectives  122 us (28%)
  waiting for transfers between devices  114 us (27%)
  matrix products  69 us (16%)
  other arithmetic  58.6 us (14%)
  local copies, waits for them, and re-layouts  37.7 us (9%)
  between operations  14.8 us (3%)
  starting transfers between devices  9.63 us (2%)
    all_to_all x1, blocking collectives, per_device(): lax.all_to_all(outgoing, 'tok', split_axis=0, concat_axis=0, tiled=True)  110 us
    all_to_all x1, waiting for transfers between devices, per_device(): lax.all_to_all(result, 'tok', split_axis=0, concat_axis=0, tiled=True)  102 us
    dot_general x5, matrix products, absorb(): jnp.einsum('tgqd,ngd->tgqn', queries, keys_values[:, :, 0], preferred_ele...  27.3 us
    reduce_sum x3, other arithmetic, absorb(): denominator = denominator * rescale + jnp.sum(weights, axis=-1)  25.6 us
    dot_general x5, matrix products, absorb(): jnp.einsum('tgqn,ngd->tgqd', weights.astype(jnp.bfloat16), keys_values[:,...  25.2 us
    all_gather x1, waiting for transfers between devices, per_device(): piece = lax.all_gather(kv_cache, 'tok', axis=0, tiled=True)  12.2 us
    another operation x6, other arithmetic  11.7 us
    all_gather x1, blocking collectives, per_device(): row_states = lax.all_gather(hidden, 'head', axis=0, tiled=True)  11.1 us
  transfers between devices with their start and end apart: 4, of which 2 were waited for; matrix products, arithmetic and copies ran while one was open for 10% of the time, Pallas kernels for 0%

commit v1 on v0

--- a/solution.py
+++ b/solution.py
@@ -1,6 +1,8 @@
 import jax
 import jax.numpy as jnp
 from jax import lax
+from jax.experimental import pallas as pl
+from jax.experimental.pallas import tpu as pltpu
 from jax.sharding import PartitionSpec as P
 
 D = 1536
@@ -98,6 +100,87 @@
             allowed_keys[:, offset : offset + width_block],
         )
     return carry
+
+
+LANES = 128
+
+
+def crossed(array, axis, flip):
+    count = lax.axis_size(axis)
+    return lax.ppermute(array, axis, [(i, i ^ flip) for i in range(count)])
+
+
+def spread(own, axis):
+    count = lax.axis_size(axis)
+    slots = {0: own}
+    bit = count // 2
+    while bit:
+        for d in sorted(slots):
+            slots[d | bit] = crossed(slots[d], axis, bit)
+        bit //= 2
+    return slots
+
+
+def folded(parts, axis):
+    count = lax.axis_size(axis)
+    parts = dict(parts)
+    bit = 1
+    while bit < count:
+        for d in sorted(parts, reverse=True):
+            if d & bit:
+                came = crossed(parts.pop(d).astype(jnp.bfloat16), axis, bit)
+                parts[d ^ bit] = parts[d ^ bit].astype(jnp.float32) + came.astype(jnp.float32)
+        bit *= 2
+    return parts[0]
+
+
+def expert_kernel(count, experts_here, where_ref, *refs):
+    state_refs = refs[:count]
+    hits_ref, router_ref, up_ref, down_ref = refs[count : count + 4]
+    out_refs = refs[count + 4 :]
+    me = where_ref[0]
+    rows = state_refs[0].shape[0]
+    states = jnp.concatenate([ref[...] for ref in state_refs], axis=0)
+    hits = jnp.concatenate(
+        [
+            hits_ref[pl.ds(pl.multiple_of(where_ref[1 + i] * rows, rows), rows), :]
+            for i in range(count)
+        ],
+        axis=0,
+    )
+    logits = jnp.dot(states, router_ref[...], preferred_element_type=jnp.float32)
+    hit = hits.astype(jnp.float32) > 0.0
+    logits = jnp.where(hit, logits, MASKED)
+    peak = jnp.max(logits, axis=-1, keepdims=True)
+    shares = jnp.where(hit, jnp.exp(logits - peak), 0.0)
+    total = jnp.sum(shares, axis=-1, keepdims=True)
+    lane = lax.broadcasted_iota(jnp.int32, shares.shape, 1)
+    result = None
+    for x in range(experts_here):
+        mine = jnp.sum(jnp.where(lane == me * experts_here + x, shares, 0.0), axis=-1, keepdims=True)
+        gate = mine / total
+        joined = jnp.dot(states, up_ref[x], preferred_element_type=jnp.float32)
+        lead = joined[:, :FFE]
+        activated = (lead / (1.0 + jnp.exp(-lead)) * joined[:, FFE:]).astype(jnp.bfloat16)
+        part = gate * jnp.dot(activated, down_ref[x], preferred_element_type=jnp.float32)
+        result = part if result is None else result + part
+    for i in range(count):
+        out_refs[i][...] = result[i * rows : (i + 1) * rows].astype(jnp.bfloat16)
+
+
+def run_experts(slots, offsets, me, hits, router, w_gate_up, w_down):
+    count = len(offsets)
+    where = jnp.stack([me] + [me ^ d for d in offsets]).astype(jnp.int32)
+    vmem = pl.BlockSpec(memory_space=pltpu.VMEM)
+    outs = pl.pallas_call(
+        lambda *refs: expert_kernel(count, w_gate_up.shape[0], *refs),
+        out_shape=[jax.ShapeDtypeStruct(slots[d].shape, jnp.bfloat16) for d in offsets],
+        in_specs=[pl.BlockSpec(memory_space=pltpu.SMEM)] + [vmem] * (count + 4),
+        out_specs=[vmem] * count,
+        compiler_params=pltpu.CompilerParams(vmem_limit_bytes=56 << 20),
+        name="experts",
+    )(where, *[slots[d] for d in offsets], hits, router, w_gate_up, w_down)
+    return dict(zip(offsets, outs))
 
 
 def per_device(
@@ -188,36 +271,29 @@
     )
     mid_states = (hidden.astype(jnp.float32) + attn_sum.astype(jnp.float32)).astype(jnp.bfloat16)
     mixed = rms_scale(mid_states, moe_gain).astype(jnp.bfloat16)
-    logits = jnp.dot(mixed, router, preferred_element_type=jnp.float32)
     experts = router.shape[1]
-    route_hits3 = routes[:, :, None] == jnp.arange(experts, dtype=jnp.int32)[None, None, :]
-    picked = jnp.sum(jnp.where(route_hits3, logits[:, None, :], 0.0), axis=-1)
-    gate_probs = jax.nn.softmax(picked, axis=-1)
-    exp_dev = w_gate_up.shape[0]
-    capacity = min(tok_dev, 3 * tok_dev * TOPK // (2 * experts))
-    flat_routes = routes.reshape(-1)
-    route_hits = (flat_routes[:, None] == jnp.arange(experts, dtype=jnp.int32)[None, :]).astype(
-        jnp.int32
-    )
-    slot_index = jnp.sum(jnp.cumsum(route_hits, axis=0) * route_hits, axis=1) - 1
-    target = flat_routes * capacity + slot_index
-    source = jnp.repeat(mixed, TOPK, axis=0)
-    outgoing = jnp.zeros((experts * capacity, D), jnp.bfloat16).at[target].set(source)
-    outgoing = outgoing.reshape(n_tok, exp_dev, capacity, D)
-    joined = jnp.einsum(
-        "sxcd,xdf->sxcf",
-        lax.all_to_all(outgoing, "tok", split_axis=0, concat_axis=0, tiled=True),
-        w_gate_up,
-        preferred_element_type=jnp.float32,
-    )
-    activated = (jax.nn.silu(joined[..., :FFE]) * joined[..., FFE:]).astype(jnp.bfloat16)
-    result = jnp.einsum(
-        "sxcf,xfd->sxcd", activated, w_down, preferred_element_type=jnp.float32
+    lanes = -(-experts // LANES) * LANES
+    all_routes = lax.all_gather(routes, "tok", axis=0, tiled=True)
+    hits = jnp.any(
+        all_routes[:, :, None] == jnp.arange(lanes, dtype=jnp.int32)[None, None, :], axis=1
     ).astype(jnp.bfloat16)
-    returned = lax.all_to_all(result, "tok", split_axis=0, concat_axis=0, tiled=True)
-    back_rows = returned.reshape(experts * capacity, D)
-    picked_rows = back_rows[target].astype(jnp.float32).reshape(tok_dev, TOPK, D)
-    routed_sum = jnp.sum(picked_rows * gate_probs[:, :, None], axis=1)
+    wide_router = jnp.pad(router, ((0, 0), (0, lanes - experts)))
+    slots = spread(mixed, "tok")
+    together = min(4, n_tok)
+    parts = {}
+    for first in range(0, n_tok, together):
+        parts.update(
+            run_experts(
+                slots,
+                list(range(first, first + together)),
+                row_index,
+                hits,
+                wide_router,
+                w_gate_up,
+                w_down,
+            )
+        )
+    routed_sum = folded(parts, "tok").astype(jnp.float32)
     layer_out = (mid_states.astype(jnp.float32) + routed_sum).astype(jnp.bfloat16)
     return (attn_sum, layer_out)
 

time: 430 us -> 313 us (0.73)
  the two profiles are of different devices: /device:TPU:11 before, /device:TPU:0 now
where the time goes in v1:
time: 313 us; the launch traced here: 309 us
  waiting for transfers between devices  89.7 us (29%)
  matrix products  52.4 us (17%)
  other arithmetic  48.2 us (15%)
  blocking collectives  42.8 us (14%)
  Pallas kernels  30.4 us (10%)
  starting transfers between devices  20.8 us (7%)
  between operations  15 us (5%)
  local copies, waits for them, and re-layouts  9.79 us (3%)
    ppermute x30, waiting for transfers between devices, crossed(): return lax.ppermute(array, axis, [(i, i ^ flip) for i in range(count)])  45.3 us
    pallas_call x4, Pallas kernels, run_experts(): pl.pallas_call(lambda *refs: expert_kernel(count, w_gate_up.shape[0], *re...  30.4 us
    all_gather x1, blocking collectives, per_device(): all_routes = lax.all_gather(routes, 'tok', axis=0, tiled=True)  29.8 us
    all_gather x1, waiting for transfers between devices, per_device(): piece = lax.all_gather(kv_cache, 'tok', axis=0, tiled=True)  28.5 us
    dot_general x5, matrix products, absorb(): jnp.einsum('tgqn,ngd->tgqd', weights.astype(jnp.bfloat16), keys_values[:,...  24.6 us
    dot_general x5, matrix products, absorb(): jnp.einsum('tgqd,ngd->tgqn', queries, keys_values[:, :, 0], preferred_ele...  22.2 us
    reduce_sum x3, other arithmetic, absorb(): denominator = denominator * rescale + jnp.sum(weights, axis=-1)  21.9 us
    ppermute x30, starting transfers between devices, crossed(): return lax.ppermute(array, axis, [(i, i ^ flip) for i in range(count)])  18.7 us
  transfers between devices with their start and end apart: 33, of which 9 were waited for; matrix products, arithmetic and copies ran while one was open for 12% of the time, Pallas kernels for 10%

profile of v1, /device:TPU:0, one launch (start us, length us, event | category | flops | bytes accessed | tf_op | source)
XLA Modules:
  0.0 309.0 jit_solution(3944818054002989364)
XLA Ops:
  11.6 13.0 %all_gather.9 = bf16[256,1536]{1,0:T(8,128)(2,1)S(1)} all-gather(bf16[128,1536]{1,0:T(8,128)(2,1)} %param.14), channel_id=1, replica_groups=mesh['tok'=16,'head'=2] {'head'}, dimensions={0}, use_global_device_ids=true | all-gather | bytes 1179648 | tf_op jit(solution)/shard_map/all_gather | solution.py:211
  25.1 3.9 %fusion.95 = f32[256,1280]{0,1:T(8,128)S(1)} fusion(bf16[1536,1280]{1,0:T(8,128)(2,1)} %param.16, bf16[256,1536]{1,0:T(8,128)(2,1)S(1)} %all_gather.9, f32[1536]{0:T(1024)} %param.15, f32[256]{0:T(256)S(1)} %add_rsqrt_fusion), kind=kOutput, calls=%fused_computation.82 | convolution fusion | flops 1008205824 | bytes 6036480 | tf_op jit(solution)/shard_map/dot_general | solution.py:213
  34.3 4.7 %fusion.33 = (f32[256,4,3]{0,2,1:T(4,128)S(1)}, f32[4,512,256,3]{2,1,3,0:T(8,128)}) fusion(pred[256,512]{0,1:T(8,128)(4,1)S(1)} %compare_and_fusion, bf16[256,4,3,64]{0,3,2,1:T(8,128)(2,1)S(1)} %bitcast.251, bf16[256,4,2,64]{0,3,1,2:T(8,128)(2,1)S(1)} %maximum_convert_fusion, bf16[256,4,2,64]{0,3,2,1:T(8,128)(2,1)} %bitcast.43), kind=kOutput, calls=%fused_computation.44 | convolution fusion | flops 206566400 | bytes 7352320 | tf_op jit(solution)/shard_map/tgqd,ngd->tgqn/dot_general | solution.py:74
  39.0 28.5 %all-gather.2.cloned.1.call-done = bf16[4096,512]{0,1:T(8,128)(2,1)} async-done(((bf16[256,512]{0,1:T(8,128)(2,1)}), bf16[4096,512]{0,1:T(8,128)(2,1)}) %all-gather.2.cloned.1.call-update) | async-done | bytes 4194320 | tf_op jit(solution)/shard_map/all_gather | solution.py:250
  70.2 6.6 %bitcast_reduce_fusion.3 = (f32[256,4,3]{0,2,1:T(4,128)S(1)}, f32[4,256,3,1024]{3,1,2,0:T(8,128)}) fusion(pred[256,1024]{1,0:T(8,128)(4,1)S(1)} %get-tuple-element.52, bf16[256,4,3,64]{0,3,2,1:T(8,128)(2,1)S(1)} %bitcast.252, bf16[1024,4,2,64]{0,3,2,1:T(8,128)(2,1)S(1)} %bitcast.265), kind=kOutput, calls=%fused_computation.13 | convolution fusion | flops 412087296 | bytes 13774848 | tf_op jit(solution)/shard_map/tgqd,ngd->tgqn/dot_general | solution.py:74
  81.2 6.6 %bitcast_reduce_fusion.2 = (f32[256,4,3]{0,2,1:T(4,128)S(1)}, f32[4,256,3,1024]{3,1,2,0:T(8,128)}) fusion(pred[256,1024]{1,0:T(8,128)(4,1)S(1)} %get-tuple-element.49, bf16[256,4,3,64]{0,3,2,1:T(8,128)(2,1)S(1)} %bitcast.255, bf16[1024,4,2,64]{0,3,2,1:T(8,128)(2,1)S(1)} %bitcast.263), kind=kOutput, calls=%fused_computation.9 | convolution fusion | flops 412087296 | bytes 13774848 | tf_op jit(solution)/shard_map/tgqd,ngd->tgqn/dot_general | solution.py:74
  89.7 12.6 %fusion.8 = (f32[256,4,3]{0,2,1:T(4,128)S(1)}, f32[256,4,3]{0,2,1:T(4,128)S(1)}) fusion(f32[4,256,3,1024]{3,1,2,0:T(8,128)} %get-tuple-element.70, f32[256,4,3]{0,2,1:T(4,128)S(1)} %get-tuple-element.58, pred[256,1024]{1,0:T(8,128)(4,1)S(1)} %get-tuple-element.52, f32[256,4,3]{0,2,1:T(4,128)S(1)} %get-tuple-element.44, ...), kind=kLoop, calls=%fused_computation.20 | loop fusion | flops 31451136 | bytes 25739264 | tf_op jit(solution)/shard_map/reduce_sum | solution.py:82
  102.2 7.6 %fusion.12 = (f32[256,4,3]{0,2,1:T(4,128)S(1)}, f32[256,4,3]{0,2,1:T(4,128)S(1)}) fusion(f32[4,256,3,1024]{3,1,2,0:T(8,128)S(1)} %get-tuple-element.66, f32[256,4,3]{0,2,1:T(4,128)S(1)} %get-tuple-element.43, pred[256,1024]{1,0:T(8,128)(4,1)S(1)} %get-tuple-element.51, f32[256,4,3]{0,2,1:T(4,128)S(1)} %get-tuple-element.42, ...), kind=kLoop, calls=%fused_computation.24 | loop fusion | flops 31451136 | bytes 25739264 | tf_op jit(solution)/shard_map/reduce_sum | solution.py:82
  109.9 6.6 %fusion.82 = f32[256,4,3,64]{0,3,2,1:T(8,128)S(1)} fusion(f32[4,256,3,1024]{3,1,2,0:T(8,128)} %get-tuple-element.70, f32[256,4,3]{0,2,1:T(4,128)S(1)} %get-tuple-element.58, pred[256,1024]{1,0:T(8,128)(4,1)S(1)} %get-tuple-element.52, bf16[1024,4,2,64]{0,3,2,1:T(8,128)(2,1)} %bitcast.266, f32[256,4,3]{0,2,1:T(4,128)S(1)} %get-tuple-element.40, ...), kind=kOutput, calls=%fused_computation.72 | convolution fusion | flops 418775040 | bytes 14467072 | tf_op jit(solution)/shard_map/tgqn,ngd->tgqd/dot_general | solution.py:83
  116.6 7.0 %fusion.76 = f32[256,4,3,64]{0,3,2,1:T(8,128)S(1)} fusion(f32[256,4,3,64]{0,3,2,1:T(8,128)S(1)} %fusion.82, f32[4,256,3,1024]{3,1,2,0:T(8,128)} %get-tuple-element.68, f32[256,4,3]{0,2,1:T(4,128)S(1)} %get-tuple-element.44, pred[256,1024]{1,0:T(8,128)(4,1)S(1)} %get-tuple-element.49, bf16[1024,4,2,64]{0,3,2,1:T(8,128)(2,1)S(1)} %bitcast.264, ...), kind=kOutput, calls=%fused_computation.70 | convolution fusion | flops 418775040 | bytes 15237120 | tf_op jit(solution)/shard_map/tgqn,ngd->tgqd/dot_general | solution.py:83
  130.0 4.6 %fusion.88 = bf16[256,4,3,64]{0,3,2,1:T(8,128)(2,1)S(1)} fusion(f32[256,4,3,64]{0,3,2,1:T(8,128)S(1)} %fusion.64, f32[4,512,256,3]{2,1,3,0:T(8,128)} %get-tuple-element.62, f32[256,4,3]{0,2,1:T(4,128)S(1)} %get-tuple-element.41, pred[256,512]{0,1:T(8,128)(4,1)S(1)} %compare_and_fusion, f32[256,4,3]{0,2,1:T(4,128)S(1)} %get-tuple-element.36, ...), kind=kOutput, calls=%fused_computation.77 | convolution fusion | flops 210305024 | bytes 8151040 | tf_op jit(solution)/shard_map/tgqn,ngd->tgqd/dot_general | solution.py:83
  136.4 15.8 %reduce-scatter.2.cloned.1.call-done = bf16[128,1536]{1,0:T(8,128)(2,1)} async-done(((bf16[256,1536]{1,0:T(8,128)(2,1)}), bf16[128,1536]{1,0:T(8,128)(2,1)}) %reduce-scatter.2.cloned.1.call-update) | async-done | bytes 393232 | tf_op jit(solution)/shard_map/reduce_scatter | solution.py:266
  160.0 29.8 %all_gather.11 = s32[2048,8]{0,1:T(8,128)S(1)} all-gather(s32[128,8]{0,1:T(8,128)S(1)} %copy-done.27), channel_id=1, replica_groups=mesh['tok'=16,'head'=2] {'tok'}, dimensions={0}, use_global_device_ids=true | all-gather | bytes 69632 | tf_op jit(solution)/shard_map/all_gather | solution.py:276
  190.8 11.6 %fusion.16 = pred[2048,128]{1,0:T(8,128)(4,1)S(1)} fusion(s32[2048,8]{1,0:T(8,128)S(1)} %copy.58), kind=kLoop, calls=%fused_computation.29 | loop fusion | flops 3932160 | bytes 327680 | tf_op jit(solution)/shard_map/reduce_or | solution.py:277
  207.2 7.6 %experts.4 = (bf16[128,1536]{1,0:T(8,128)(2,1)}, bf16[128,1536]{1,0:T(8,128)(2,1)}, bf16[128,1536]{1,0:T(8,128)(2,1)}, bf16[128,1536]{1,0:T(8,128)(2,1)}) custom-call(s32[5]{0:T(128)} %stack.76.refs_0_, bf16[128,1536]{1,0:T(8,128)(2,1)} %copy-done.9, bf16[128,1536]{1,0:T(8,128)(2,1)} %collective-permute-done.1.refs_2_, ...), custom_call_target="tpu_custom_call" | custom-call | tf_op jit(solution)/shard_map/experts/pallas_call | solution.py:175
  218.1 7.6 %experts.5 = (bf16[128,1536]{1,0:T(8,128)(2,1)}, bf16[128,1536]{1,0:T(8,128)(2,1)}, bf16[128,1536]{1,0:T(8,128)(2,1)}, bf16[128,1536]{1,0:T(8,128)(2,1)}) custom-call(s32[5]{0:T(128)} %stack.81.refs_0_, bf16[128,1536]{1,0:T(8,128)(2,1)} %copy-done.12, bf16[128,1536]{1,0:T(8,128)(2,1)} %collective-permute-done.8.refs_2_, bf16[128,1536]{1,0:T(8,128)(2,1)} %copy-done.15, ...), custom_call_target="tpu_custom_call" | custom-call | tf_op jit(solution)/shard_map/experts/pallas_call | solution.py:175
  229.7 7.6 %experts.6 = (bf16[128,1536]{1,0:T(8,128)(2,1)}, bf16[128,1536]{1,0:T(8,128)(2,1)}, bf16[128,1536]{1,0:T(8,128)(2,1)}, bf16[128,1536]{1,0:T(8,128)(2,1)}) custom-call(s32[5]{0:T(128)} %stack.86.refs_0_, bf16[128,1536]{1,0:T(8,128)(2,1)} %copy-done.10, bf16[128,1536]{1,0:T(8,128)(2,1)} %copy-done.17, bf16[128,1536]{1,0:T(8,128)(2,1)} %copy-done.13, ...), custom_call_target="tpu_custom_call" | custom-call | tf_op jit(solution)/shard_map/experts/pallas_call | solution.py:175
  238.2 7.6 %experts.7 = (bf16[128,1536]{1,0:T(8,128)(2,1)}, bf16[128,1536]{1,0:T(8,128)(2,1)}, bf16[128,1536]{1,0:T(8,128)(2,1)}, bf16[128,1536]{1,0:T(8,128)(2,1)}) custom-call(s32[5]{0:T(128)} %stack.91.refs_0_, bf16[128,1536]{1,0:T(8,128)(2,1)} %copy-done.11, bf16[128,1536]{1,0:T(8,128)(2,1)} %copy-done.16, bf16[128,1536]{1,0:T(8,128)(2,1)} %copy-done.14, ...), custom_call_target="tpu_custom_call" | custom-call | tf_op jit(solution)/shard_map/experts/pallas_call | solution.py:175
  251.3 9.2 %collective-permute-done.28 = bf16[128,1536]{1,0:T(8,128)(2,1)S(1)} collective-permute-done((bf16[128,1536]{1,0:T(8,128)(2,1)S(1)}, bf16[128,1536]{1,0:T(8,128)(2,1)S(1)}, u32[]{:S(2)}, u32[]{:S(2)}) %collective-permute-start.28) | collective-permute-done | bytes 393248 | tf_op jit(solution)/shard_map/ppermute | solution.py:110
  263.8 8.8 %collective-permute-done.13 = bf16[128,1536]{1,0:T(8,128)(2,1)S(1)} collective-permute-done((bf16[128,1536]{1,0:T(8,128)(2,1)S(1)}, bf16[128,1536]{1,0:T(8,128)(2,1)S(1)}, u32[]{:S(2)}, u32[]{:S(2)}) %collective-permute-start.13) | collective-permute-done | bytes 393248 | tf_op jit(solution)/shard_map/ppermute | solution.py:110
  274.8 4.5 %collective-permute-done.21 = bf16[128,1536]{1,0:T(8,128)(2,1)S(1)} collective-permute-done((bf16[128,1536]{1,0:T(8,128)(2,1)S(1)}, bf16[128,1536]{1,0:T(8,128)(2,1)S(1)}, u32[]{:S(2)}, u32[]{:S(2)}) %collective-permute-start.21) | collective-permute-done | bytes 393248 | tf_op jit(solution)/shard_map/ppermute | solution.py:110
  279.3 9.6 %collective-permute-done.29 = bf16[128,1536]{1,0:T(8,128)(2,1)S(1)} collective-permute-done((bf16[128,1536]{1,0:T(8,128)(2,1)S(1)}, bf16[128,1536]{1,0:T(8,128)(2,1)S(1)}, u32[]{:S(2)}, u32[]{:S(2)}) %collective-permute-start.29) | collective-permute-done | bytes 393248 | tf_op jit(solution)/shard_map/ppermute | solution.py:110
  289.1 4.0 %collective-permute-done.14 = bf16[128,1536]{1,0:T(8,128)(2,1)S(1)} collective-permute-done((bf16[128,1536]{1,0:T(8,128)(2,1)S(1)}, bf16[128,1536]{1,0:T(8,128)(2,1)S(1)}, u32[]{:S(2)}, u32[]{:S(2)}) %collective-permute-start.14) | collective-permute-done | bytes 393248 | tf_op jit(solution)/shard_map/ppermute | solution.py:110
  293.1 7.7 %collective-permute-done.30 = bf16[128,1536]{1,0:T(8,128)(2,1)S(1)} collective-permute-done((bf16[128,1536]{1,0:T(8,128)(2,1)S(1)}, bf16[128,1536]{1,0:T(8,128)(2,1)S(1)}, u32[]{:S(2)}, u32[]{:S(2)}) %collective-permute-start.30) | collective-permute-done | bytes 393248 | tf_op jit(solution)/shard_map/ppermute | solution.py:110
  (191 shorter events, 60.9 us)
Async XLA Ops:
  7.2 60.3 %all-gather.2.cloned.1.call-start = ((), (), s32[]{:S(2)}) async-start(), calls=%async_computation.1 | async-start | bytes 4456448 | tf_op jit(solution)/shard_map/all_gather | solution.py:250
  9.0 143.1 %reduce-scatter.2.cloned.1.call-start = ((), (), s32[]{:S(2)}) async-start(), calls=%async_computation.2 | async-start | bytes 1179648 | tf_op jit(solution)/shard_map/reduce_scatter | solution.py:266
  154.5 36.0 %collective-permute-start.2 = (bf16[128,1536]{1,0:T(8,128)(2,1)S(1)}, bf16[128,1536]{1,0:T(8,128)(2,1)}, u32[]{:S(2)}, u32[]{:S(2)}) collective-permute-start(bf16[128,1536]{1,0:T(8,128)(2,1)S(1)} %fusion.93.refs_1_), channel_id=1, source_target_pairs={{0,4},{2,6},{4,0},{6,2},{8,12},{10,14},{12,8},{14,10},{16,20},{18,... | collective-permute-start | bytes 1179656 | tf_op jit(solution)/shard_map/ppermute | solution.py:110
  156.1 34.6 %collective-permute-start.7 = (bf16[128,1536]{1,0:T(8,128)(2,1)S(1)}, bf16[128,1536]{1,0:T(8,128)(2,1)S(1)}, u32[]{:S(2)}, u32[]{:S(2)}) collective-permute-start(bf16[128,1536]{1,0:T(8,128)(2,1)S(1)} %fusion.93.refs_1_), channel_id=1, source_target_pairs={{0,8},{2,10},{4,12},{6,14},{8,0},{10,2},{12,4},{14,6},{16,24},{18,... | collective-permute-start | bytes 1179656 | tf_op jit(solution)/shard_map/ppermute | solution.py:110
  157.6 33.1 %collective-permute-start.15 = (bf16[128,1536]{1,0:T(8,128)(2,1)S(1)}, bf16[128,1536]{1,0:T(8,128)(2,1)S(1)}, u32[]{:S(2)}, u32[]{:S(2)}) collective-permute-start(bf16[128,1536]{1,0:T(8,128)(2,1)S(1)} %fusion.93.refs_1_), channel_id=1, source_target_pairs={{0,16},{2,18},{4,20},{6,22},{8,24},{10,26},{12,28},{14,30},{16,0},... | collective-permute-start | bytes 1179656 | tf_op jit(solution)/shard_map/ppermute | solution.py:110
  190.1 15.3 %collective-permute-start.1 = (bf16[128,1536]{1,0:T(8,128)(2,1)S(1)}, bf16[128,1536]{1,0:T(8,128)(2,1)}, u32[]{:S(2)}, u32[]{:S(2)}) collective-permute-start(bf16[128,1536]{1,0:T(8,128)(2,1)S(1)} %fusion.93.refs_1_), channel_id=1, source_target_pairs={{0,2},{2,0},{4,6},{6,4},{8,10},{10,8},{12,14},{14,12},{16,18},{18,... | collective-permute-start | bytes 1179656 | tf_op jit(solution)/shard_map/ppermute | solution.py:110
  190.5 16.7 %collective-permute-start.3 = (bf16[128,1536]{1,0:T(8,128)(2,1)}, bf16[128,1536]{1,0:T(8,128)(2,1)}, u32[]{:S(2)}, u32[]{:S(2)}) collective-permute-start(bf16[128,1536]{1,0:T(8,128)(2,1)} %collective-permute-done.2.refs_3_), channel_id=1, source_target_pairs={{0,2},{2,0},{4,6},{6,4},{8,10},{10,8},{12,14},{14,12},{16,18},{18,... | collective-permute-start | bytes 1179656 | tf_op jit(solution)/shard_map/ppermute | solution.py:110
  190.7 16.3 %collective-permute-start.9 = (bf16[128,1536]{1,0:T(8,128)(2,1)S(1)}, bf16[128,1536]{1,0:T(8,128)(2,1)S(1)}, u32[]{:S(2)}, u32[]{:S(2)}) collective-permute-start(bf16[128,1536]{1,0:T(8,128)(2,1)S(1)} %collective-permute-done.7.refs_1_), channel_id=1, source_target_pairs={{0,4},{2,6},{4,0},{6,2},{8,12},{10,14},{12,8},{14,10},{16,20},{18,... | collective-permute-start | bytes 1179656 | tf_op jit(solution)/shard_map/ppermute | solution.py:110
  190.7 24.4 %collective-permute-start.22 = (bf16[128,1536]{1,0:T(8,128)(2,1)S(1)}, bf16[128,1536]{1,0:T(8,128)(2,1)S(1)}, u32[]{:S(2)}, u32[]{:S(2)}) collective-permute-start(bf16[128,1536]{1,0:T(8,128)(2,1)S(1)} %collective-permute-done.15.refs_1_), channel_id=1, source_target_pairs={{0,8},{2,10},{4,12},{6,14},{8,0},{10,2},{12,4},{14,6},{16,24},{18,... | collective-permute-start | bytes 1179656 | tf_op jit(solution)/shard_map/ppermute | solution.py:110
  205.0 12.5 %collective-permute-start.8 = (bf16[128,1536]{1,0:T(8,128)(2,1)S(1)}, bf16[128,1536]{1,0:T(8,128)(2,1)}, u32[]{:S(2)}, u32[]{:S(2)}) collective-permute-start(bf16[128,1536]{1,0:T(8,128)(2,1)S(1)} %collective-permute-done.7.refs_1_), channel_id=1, source_target_pairs={{0,2},{2,0},{4,6},{6,4},{8,10},{10,8},{12,14},{14,12},{16,18},{18,... | collective-permute-start | bytes 1179656 | tf_op jit(solution)/shard_map/ppermute | solution.py:110
  205.4 12.1 %collective-permute-start.17 = (bf16[128,1536]{1,0:T(8,128)(2,1)S(1)}, bf16[128,1536]{1,0:T(8,128)(2,1)S(1)}, u32[]{:S(2)}, u32[]{:S(2)}) collective-permute-start(bf16[128,1536]{1,0:T(8,128)(2,1)S(1)} %collective-permute-done.15.refs_1_), channel_id=1, source_target_pairs={{0,4},{2,6},{4,0},{6,2},{8,12},{10,14},{12,8},{14,10},{16,20},{18,... | collective-permute-start | bytes 1179656 | tf_op jit(solution)/shard_map/ppermute | solution.py:110
  217.5 19.8 %collective-permute-start.23 = (bf16[128,1536]{1,0:T(8,128)(2,1)S(1)}, bf16[128,1536]{1,0:T(8,128)(2,1)S(1)}, u32[]{:S(2)}, u32[]{:S(2)}) collective-permute-start(bf16[128,1536]{1,0:T(8,128)(2,1)S(1)} %collective-permute-done.22.refs_1_), channel_id=1, source_target_pairs={{0,2},{2,0},{4,6},{6,4},{8,10},{10,8},{12,14},{14,12},{16,18},{18,... | collective-permute-start | bytes 1179656 | tf_op jit(solution)/shard_map/ppermute | solution.py:110
  225.7 20.0 %collective-permute-start.12 = (bf16[128,1536]{1,0:T(8,128)(2,1)}, bf16[128,1536]{1,0:T(8,128)(2,1)S(1)}, u32[]{:S(2)}, u32[]{:S(2)}) collective-permute-start(bf16[128,1536]{1,0:T(8,128)(2,1)} %get-tuple-element.25), channel_id=1, source_target_pairs={{0,2},{2,0},{4,6},{6,4},{8,10},{10,8},{12,14},{14,12},{16,18},{18,... | collective-permute-start | bytes 1179656 | tf_op jit(solution)/shard_map/ppermute | solution.py:110
  227.7 61.5 %collective-permute-start.4 = (bf16[128,1536]{1,0:T(8,128)(2,1)}, bf16[128,1536]{1,0:T(8,128)(2,1)S(1)}, u32[]{:S(2)}, u32[]{:S(2)}) collective-permute-start(bf16[128,1536]{1,0:T(8,128)(2,1)} %get-tuple-element.19), channel_id=1, source_target_pairs={{0,2},{2,0},{4,6},{6,4},{8,10},{10,8},{12,14},{14,12},{16,18},{18,... | collective-permute-start | bytes 1179656 | tf_op jit(solution)/shard_map/ppermute | solution.py:110
  228.1 61.0 %collective-permute-start.6 = (bf16[128,1536]{1,0:T(8,128)(2,1)S(1)}, bf16[128,1536]{1,0:T(8,128)(2,1)S(1)}, u32[]{:S(2)}, u32[]{:S(2)}) collective-permute-start(bf16[128,1536]{1,0:T(8,128)(2,1)S(1)} %add_convert_fusion.6), channel_id=1, source_target_pairs={{0,4},{2,6},{4,0},{6,2},{8,12},{10,14},{12,8},{14,10},{16,20},{18,... | collective-permute-start | bytes 1179656 | tf_op jit(solution)/shard_map/ppermute | solution.py:110
  237.3 25.1 %collective-permute-start.11 = (bf16[128,1536]{1,0:T(8,128)(2,1)}, bf16[128,1536]{1,0:T(8,128)(2,1)S(1)}, u32[]{:S(2)}, u32[]{:S(2)}) collective-permute-start(bf16[128,1536]{1,0:T(8,128)(2,1)} %get-tuple-element.23), channel_id=1, source_target_pairs={{0,2},{2,0},{4,6},{6,4},{8,10},{10,8},{12,14},{14,12},{16,18},{18,... | collective-permute-start | bytes 1179656 | tf_op jit(solution)/shard_map/ppermute | solution.py:110
  237.4 11.9 %collective-permute-start.20 = (bf16[128,1536]{1,0:T(8,128)(2,1)}, bf16[128,1536]{1,0:T(8,128)(2,1)S(1)}, u32[]{:S(2)}, u32[]{:S(2)}) collective-permute-start(bf16[128,1536]{1,0:T(8,128)(2,1)} %get-tuple-element.29), channel_id=1, source_target_pairs={{0,2},{2,0},{4,6},{6,4},{8,10},{10,8},{12,14},{14,12},{16,18},{18,... | collective-permute-start | bytes 1179656 | tf_op jit(solution)/shard_map/ppermute | solution.py:110
  249.3 11.2 %collective-permute-start.28 = (bf16[128,1536]{1,0:T(8,128)(2,1)S(1)}, bf16[128,1536]{1,0:T(8,128)(2,1)S(1)}, u32[]{:S(2)}, u32[]{:S(2)}) collective-permute-start(bf16[128,1536]{1,0:T(8,128)(2,1)S(1)} %add_convert_fusion.2), channel_id=1, source_target_pairs={{0,4},{2,6},{4,0},{6,2},{8,12},{10,14},{12,8},{14,10},{16,20},{18,... | collective-permute-start | bytes 1179656 | tf_op jit(solution)/shard_map/ppermute | solution.py:110
  251.2 23.5 %collective-permute-start.19 = (bf16[128,1536]{1,0:T(8,128)(2,1)}, bf16[128,1536]{1,0:T(8,128)(2,1)S(1)}, u32[]{:S(2)}, u32[]{:S(2)}) collective-permute-start(bf16[128,1536]{1,0:T(8,128)(2,1)} %get-tuple-element.27), channel_id=1, source_target_pairs={{0,2},{2,0},{4,6},{6,4},{8,10},{10,8},{12,14},{14,12},{16,18},{18,... | collective-permute-start | bytes 1179656 | tf_op jit(solution)/shard_map/ppermute | solution.py:110
  260.5 12.1 %collective-permute-start.13 = (bf16[128,1536]{1,0:T(8,128)(2,1)S(1)}, bf16[128,1536]{1,0:T(8,128)(2,1)S(1)}, u32[]{:S(2)}, u32[]{:S(2)}) collective-permute-start(bf16[128,1536]{1,0:T(8,128)(2,1)S(1)} %add_convert_fusion.5), channel_id=1, source_target_pairs={{0,4},{2,6},{4,0},{6,2},{8,12},{10,14},{12,8},{14,10},{16,20},{18,... | collective-permute-start | bytes 1179656 | tf_op jit(solution)/shard_map/ppermute | solution.py:110
  262.4 16.9 %collective-permute-start.21 = (bf16[128,1536]{1,0:T(8,128)(2,1)S(1)}, bf16[128,1536]{1,0:T(8,128)(2,1)S(1)}, u32[]{:S(2)}, u32[]{:S(2)}) collective-permute-start(bf16[128,1536]{1,0:T(8,128)(2,1)S(1)} %add_convert_fusion.3), channel_id=1, source_target_pairs={{0,4},{2,6},{4,0},{6,2},{8,12},{10,14},{12,8},{14,10},{16,20},{18,... | collective-permute-start | bytes 1179656 | tf_op jit(solution)/shard_map/ppermute | solution.py:110
  272.6 16.3 %collective-permute-start.29 = (bf16[128,1536]{1,0:T(8,128)(2,1)S(1)}, bf16[128,1536]{1,0:T(8,128)(2,1)S(1)}, u32[]{:S(2)}, u32[]{:S(2)}) collective-permute-start(bf16[128,1536]{1,0:T(8,128)(2,1)S(1)} %add_convert_fusion.1), channel_id=1, source_target_pairs={{0,8},{2,10},{4,12},{6,14},{8,0},{10,2},{12,4},{14,6},{16,24},{18,... | collective-permute-start | bytes 1179656 | tf_op jit(solution)/shard_map/ppermute | solution.py:110
  274.7 18.4 %collective-permute-start.14 = (bf16[128,1536]{1,0:T(8,128)(2,1)S(1)}, bf16[128,1536]{1,0:T(8,128)(2,1)S(1)}, u32[]{:S(2)}, u32[]{:S(2)}) collective-permute-start(bf16[128,1536]{1,0:T(8,128)(2,1)S(1)} %add_convert_fusion.4), channel_id=1, source_target_pairs={{0,8},{2,10},{4,12},{6,14},{8,0},{10,2},{12,4},{14,6},{16,24},{18,... | collective-permute-start | bytes 1179656 | tf_op jit(solution)/shard_map/ppermute | solution.py:110
  289.0 11.8 %collective-permute-start.30 = (bf16[128,1536]{1,0:T(8,128)(2,1)S(1)}, bf16[128,1536]{1,0:T(8,128)(2,1)S(1)}, u32[]{:S(2)}, u32[]{:S(2)}) collective-permute-start(bf16[128,1536]{1,0:T(8,128)(2,1)S(1)} %add_convert_fusion), channel_id=1, source_target_pairs={{0,16},{2,18},{4,20},{6,22},{8,24},{10,26},{12,28},{14,30},{16,0},... | collective-permute-start | bytes 1179656 | tf_op jit(solution)/shard_map/ppermute | solution.py:110
  (42 other events, 807.3 us)
Sparse Core Ops, SparseCore 0:
  10.7 56.7 all-gather.1
  136.5 15.5 reduce-scatter.1

commit v2 on v1

v2 whole, which is shorter than its diff:
```python
import functools

import jax
import jax.numpy as jnp
from jax import lax
from jax.experimental import pallas as pl
from jax.experimental.pallas import tpu as pltpu
from jax.sharding import PartitionSpec as P

D = 1536
HEADS = 24
KVH = 8
HD = 64
FFE = 512
TOPK = 8
PREFIX = 2048
GROUPS = 2
PAGE = 16
QPG = HEADS // KVH
BLOCK = 64


EPSILON = 1e-06
ROPE_BASE = 10000.0
MASKED = -1e30

LANES = 128


def crossed(array, axis, flip):
    count = lax.axis_size(axis)
    return lax.ppermute(array, axis, [(i, i ^ flip) for i in range(count)])


def spread(own, axis):
    count = lax.axis_size(axis)
    slots = {0: own}
    bit = count // 2
    while bit:
        for d in sorted(slots):
            slots[d | bit] = crossed(slots[d], axis, bit)
        bit //= 2
    return slots


def folded(parts, axis):
    count = lax.axis_size(axis)
    parts = dict(parts)
    bit = 1
    while bit < count:
        for d in sorted(parts, reverse=True):
            if d & bit:
                came = crossed(parts.pop(d).astype(jnp.bfloat16), axis, bit)
                parts[d ^ bit] = parts[d ^ bit].astype(jnp.float32) + came.astype(jnp.float32)
        bit *= 2
    return parts[0]


VMEM = pl.BlockSpec(memory_space=pltpu.VMEM)
SMEM = pl.BlockSpec(memory_space=pltpu.SMEM)
PARAMS = pltpu.CompilerParams(vmem_limit_bytes=56 << 20)


def token_info(token_ids, lengths, request_group):
    ends = jnp.cumsum(lengths)
    starts = ends - lengths
    member = (starts[None, :] <= token_ids[:, None]) & (token_ids[:, None] < ends[None, :])
    request = jnp.sum(
        jnp.where(member, jnp.arange(lengths.shape[0], dtype=jnp.int32)[None, :], 0), axis=1
    )
    start_of = jnp.sum(jnp.where(member, starts[None, :], 0), axis=1)
    group_of = jnp.sum(jnp.where(member, request_group[None, :], 0), axis=1)
    return (request, start_of, group_of)


def ranks(group_of):
    count = group_of.shape[0]
    order = group_of * count + jnp.arange(count, dtype=jnp.int32)
    rank = jnp.sum((order[None, :] < order[:, None]).astype(jnp.int32), axis=1)
    return rank, jnp.sum((group_of == 0).astype(jnp.int32))


def arranged(values, rank):
    count = rank.shape[0]
    place = rank[None, :] == jnp.arange(count, dtype=jnp.int32)[:, None]
    return jnp.sum(jnp.where(place, values[None, :], 0), axis=1)


def project_kernel(slots, kv_dev, rank_ref, gain_ref, weight_ref, cos_ref, sin_ref, *refs):
    state_refs = refs[:slots]
    query_ref, kv_ref = refs[slots:]
    states = jnp.concatenate([ref[...] for ref in state_refs], axis=0).astype(jnp.float32)
    rows = states.shape[0]
    scale = lax.rsqrt(jnp.mean(states * states, axis=-1, keepdims=True) + EPSILON)
    normed = (states * scale * gain_ref[...]).astype(jnp.bfloat16)
    place = rank_ref[...] == lax.broadcasted_iota(jnp.int32, (rows, rows), 0)
    normed = jnp.dot(
        place.astype(jnp.bfloat16), normed, preferred_element_type=jnp.float32
    ).astype(jnp.bfloat16)
    projected = jnp.dot(normed, weight_ref[...], preferred_element_type=jnp.float32)
    cosine = cos_ref[...]
    sine = sin_ref[...]
    lane = lax.broadcasted_iota(jnp.int32, (rows, LANES), 1)
    low = lane < HD
    first = lane % HD < HD // 2

    def tile(number):
        return projected[:, number * LANES : (number + 1) * LANES]

    @functools.cache
    def turned(number):
        plain = tile(number)
        partner = jnp.where(
            first, pltpu.roll(plain, LANES - HD // 2, 1), pltpu.roll(plain, HD // 2, 1)
        )
        return plain * cosine + partner * sine

    for j in range(kv_dev):
        unit = j * (QPG + 2)
        for i in range(QPG):
            query = turned((unit + i) // 2)
            if (unit + i) % 2:
                query = pltpu.roll(query, HD, 1)
            query_ref[j, i] = jnp.where(low, query * HD ** (-0.5), 0.0).astype(jnp.bfloat16)
        key, value = turned((unit + QPG) // 2), tile((unit + QPG + 1) // 2)
        if (unit + QPG) % 2:
            key, value = pltpu.roll(key, HD, 1), pltpu.roll(value, HD, 1)
        kv_ref[:, j * LANES : (j + 1) * LANES] = jnp.where(low, key, value).astype(jnp.bfloat16)


def scored(queries, keys):
    return lax.dot_general(
        queries, keys, (((1,), (1,)), ((), ())), preferred_element_type=jnp.float32
    )


def attend_kernel(
    shards,
    kv_dev,
    slots,
    scalar_ref,
    place_ref,
    query_ref,
    prior_ref,
    own_ref,
    row_request_ref,
    row_id_ref,
    key_request_ref,
    key_id_ref,
    rank_ref,
    *refs,
):
    shard_refs = refs[:shards]
    out_refs = refs[shards : shards + slots]
    pool_ref, peak_ref, total_ref, sum_ref, arrived = refs[shards + slots :]
    me = scalar_ref[0]
    in_first = scalar_ref[1]
    rows = query_ref.shape[2]
    blocks = rows // BLOCK
    shard_pages = shard_refs[0].shape[0] // PAGE

    for d in range(shards):
        def start(j, carry, d=d):
            page = (me ^ d) * shard_pages + j
            pltpu.make_async_copy(
                shard_refs[d].at[pl.ds(pl.multiple_of(j * PAGE, PAGE), PAGE), :],
                pool_ref.at[pl.ds(pl.multiple_of(place_ref[page] * PAGE, PAGE), PAGE), :],
                arrived,
            ).start()
            return carry

        lax.fori_loop(0, shard_pages, start, 0)

    def near(b, carry):
        at = pl.ds(pl.multiple_of(b * BLOCK, BLOCK), BLOCK)
        request = row_request_ref[at, :]
        ident = row_id_ref[at, :]
        allowed = (key_request_ref[...] == request) & (key_id_ref[...] <= ident)
        allowed = jnp.concatenate([allowed.astype(jnp.float32)] * QPG, axis=0) > 0.0
        for j in range(kv_dev):
            queries = query_ref[j, :, at, :].reshape(QPG * BLOCK, LANES)
            columns = slice(j * LANES, (j + 1) * LANES)
            keys = jnp.concatenate([prior_ref[:, columns], own_ref[:, columns]], axis=0)
            scores = jnp.where(allowed, scored(queries, keys), MASKED)
            peak = jnp.max(scores, axis=-1, keepdims=True)
            weights = jnp.where(allowed, jnp.exp(scores - peak), 0.0)
            total = jnp.sum(weights, axis=-1, keepdims=True)
            mixed = jnp.dot(
                weights.astype(jnp.bfloat16), keys, preferred_element_type=jnp.float32
            )
            shape = (QPG, BLOCK, LANES)
            peak_ref[j, :, at, :] = jnp.broadcast_to(peak, mixed.shape).reshape(shape)
            total_ref[j, :, at, :] = jnp.broadcast_to(total, mixed.shape).reshape(shape)
            sum_ref[j, :, at, :] = mixed.reshape(shape)
        return carry

    lax.fori_loop(0, blocks, near, 0)
    pltpu.make_async_copy(pool_ref, pool_ref, arrived).wait()

    group_rows = pool_ref.shape[0] // GROUPS
    full = (in_first + BLOCK - 1) // BLOCK
    skip = in_first // BLOCK

    def far(item, carry):
        group = (item >= full).astype(jnp.int32)
        b = jnp.where(item < full, item, item - full + skip)
        at = pl.ds(pl.multiple_of(b * BLOCK, BLOCK), BLOCK)
        keys_at = pl.ds(pl.multiple_of(group * group_rows, group_rows), group_rows)
        line = lax.broadcasted_iota(jnp.int32, (QPG, BLOCK, LANES), 1) + b * BLOCK
        chosen = (line >= in_first) == (group == 1)
        shape = (QPG, BLOCK, LANES)
        for j in range(kv_dev):
            queries = query_ref[j, :, at, :].reshape(QPG * BLOCK, LANES)
            keys = pool_ref[keys_at, j * LANES : (j + 1) * LANES]
            scores = scored(queries, keys)
            here = jnp.max(scores, axis=-1, keepdims=True)
            weights = jnp.exp(scores - here)
            total = jnp.sum(weights, axis=-1, keepdims=True)
            mixed = jnp.dot(
                weights.astype(jnp.bfloat16), keys, preferred_element_type=jnp.float32
            ).reshape(shape)
            here = jnp.broadcast_to(here, (QPG * BLOCK, LANES)).reshape(shape)
            total = jnp.broadcast_to(total, (QPG * BLOCK, LANES)).reshape(shape)
            before = peak_ref[j, :, at, :]
            peak = jnp.maximum(before, here)
            keep, gain = jnp.exp(before - peak), jnp.exp(here - peak)
            joint_total = total_ref[j, :, at, :] * keep + total * gain
            joint_sum = sum_ref[j, :, at, :] * keep + mixed * gain
            total_ref[j, :, at, :] = jnp.where(chosen, joint_total, total_ref[j, :, at, :])
            sum_ref[j, :, at, :] = jnp.where(chosen, joint_sum, sum_ref[j, :, at, :])
        return carry

    lax.fori_loop(0, full + blocks - skip, far, 0)

    back = (rank_ref[...] == lax.broadcasted_iota(jnp.int32, (rows, rows), 1)).astype(jnp.bfloat16)
    lane = lax.broadcasted_iota(jnp.int32, (rows, LANES), 1)
    piece = rows // slots
    heads = [
        sum_ref[j, i] / total_ref[j, i] for j in range(kv_dev) for i in range(QPG)
    ]
    for h in range(0, len(heads), 2):
        pair = pltpu.roll(heads[h], HD, 1)
        if h + 1 < len(heads):
            pair = jnp.where(lane < HD, pair, heads[h + 1])
        pair = jnp.dot(
            back, pair.astype(jnp.bfloat16), preferred_element_type=jnp.float32
        ).astype(jnp.bfloat16)
        width = min(LANES, len(heads) * HD - h * HD)
        for k in range(slots):
            out_refs[k][:, h * HD : h * HD + width] = pair[k * piece : (k + 1) * piece, :width]


def close_kernel(slots, scalar_ref, hidden_ref, weight_ref, gain_ref, *refs):
    context_refs = refs[:slots]
    branch_ref, mid_ref, mixed_ref = refs[slots:]
    width = context_refs[0].shape[1]
    total = None
    for k in range(slots):
        first = pl.multiple_of((scalar_ref[0] ^ k) * width, width)
        part = jnp.dot(
            context_refs[k][...],
            weight_ref[pl.ds(first, width), :],
            preferred_element_type=jnp.float32,
        )
        total = part if total is None else total + part
    branch = total.astype(jnp.bfloat16)
    branch_ref[...] = branch
    mid = (hidden_ref[...].astype(jnp.float32) + branch.astype(jnp.float32)).astype(jnp.bfloat16)
    mid_ref[...] = mid
    wide = mid.astype(jnp.float32)
    scale = lax.rsqrt(jnp.mean(wide * wide, axis=-1, keepdims=True) + EPSILON)
    mixed_ref[...] = (wide * scale * gain_ref[...]).astype(jnp.bfloat16)


def expert_kernel(count, experts_here, where_ref, *refs):
    state_refs = refs[:count]
    routes_ref, router_ref, up_ref, down_ref = refs[count : count + 4]
    out_refs = refs[count + 4 :]
    me = where_ref[0]
    rows = state_refs[0].shape[0]
    lanes = router_ref.shape[1]
    states = jnp.concatenate([ref[...] for ref in state_refs], axis=0)
    lane = lax.broadcasted_iota(jnp.int32, (rows, lanes), 1)
    hits = []
    for i in range(count):
        first = pl.multiple_of(where_ref[1 + i] * TOPK, TOPK)
        routes = jnp.transpose(routes_ref[pl.ds(first, TOPK), :].astype(jnp.float32)).astype(jnp.int32)
        hit = jnp.zeros((rows, lanes), jnp.float32)
        for k in range(TOPK):
            hit = jnp.where(lane == routes[:, k : k + 1], 1.0, hit)
        hits.append(hit)
    hit = jnp.concatenate(hits, axis=0) > 0.0
    logits = jnp.dot(states, router_ref[...], preferred_element_type=jnp.float32)
    logits = jnp.where(hit, logits, MASKED)
    peak = jnp.max(logits, axis=-1, keepdims=True)
    shares = jnp.where(hit, jnp.exp(logits - peak), 0.0)
    total = jnp.sum(shares, axis=-1, keepdims=True)
    lane = lax.broadcasted_iota(jnp.int32, shares.shape, 1)
    result = None
    for x in range(experts_here):
        mine = jnp.sum(jnp.where(lane == me * experts_here + x, shares, 0.0), axis=-1, keepdims=True)
        gate = mine / total
        joined = jnp.dot(states, up_ref[x], preferred_element_type=jnp.float32)
        lead = joined[:, :FFE]
        activated = (lead / (1.0 + jnp.exp(-lead)) * joined[:, FFE:]).astype(jnp.bfloat16)
        part = gate * jnp.dot(activated, down_ref[x], preferred_element_type=jnp.float32)
        result = part if result is None else result + part
    for i in range(count):
        out_refs[i][...] = result[i * rows : (i + 1) * rows].astype(jnp.bfloat16)


def run_experts(slots, offsets, me, routes, router, w_gate_up, w_down):
    count = len(offsets)
    where = jnp.stack([me] + [me ^ d for d in offsets]).astype(jnp.int32)
    outs = pl.pallas_call(
        functools.partial(expert_kernel, count, w_gate_up.shape[0]),
        out_shape=[jax.ShapeDtypeStruct(slots[d].shape, jnp.bfloat16) for d in offsets],
        in_specs=[SMEM] + [VMEM] * (count + 4),
        out_specs=[VMEM] * count,
        compiler_params=PARAMS,
        name="experts",
    )(where, *[slots[d] for d in offsets], routes, router, w_gate_up, w_down)
    return dict(zip(offsets, outs))


def per_device(
    hidden,
    attn_gain,
    w_qkv,
    kv_cache,
    page_table,
    lengths,
    request_group,
    key_mask,
    o_weight,
    moe_gain,
    router,
    routes,
    w_gate_up,
    w_down,
):
    n_tok = lax.axis_size("tok")
    n_head = lax.axis_size("head")
    tok_dev = hidden.shape[0]
    row_tokens = tok_dev * n_head
    kv_dev = w_qkv.shape[1] // ((QPG + 2) * HD)
    row_index = lax.axis_index("tok")
    head_index = lax.axis_index("head")

    states = spread(hidden, "head")
    shards = spread(kv_cache, "tok")

    within = jnp.arange(tok_dev, dtype=jnp.int32)
    row_offset = jnp.concatenate(
        [(head_index ^ k).astype(jnp.int32) * tok_dev + within for k in range(n_head)]
    )
    own_ids = row_index * row_tokens + row_offset
    prior_ids = own_ids - row_tokens
    own_request, own_start, own_group = token_info(own_ids, lengths, request_group)
    prior_request, _, prior_group = token_info(prior_ids, lengths, request_group)
    rank, in_first = ranks(own_group)
    prior_rank, _ = ranks(prior_group)
    token_mask = jnp.concatenate([jnp.zeros((row_tokens,), jnp.int32), key_mask])
    window = lax.dynamic_slice_in_dim(token_mask, row_index * row_tokens, 2 * row_tokens)
    window = window.reshape(2 * n_head, tok_dev)
    flipped = [(head_index ^ k) for k in range(n_head)]
    prior_mask = jnp.concatenate([window[f] for f in flipped])
    own_mask = jnp.concatenate([window[n_head + f] for f in flipped])
    ids = arranged(own_ids, rank)
    request = arranged(own_request, rank)
    position = (PREFIX + arranged(own_ids - own_start, rank)).astype(jnp.float32)
    key_request = jnp.concatenate(
        [
            arranged(jnp.where(prior_mask == 1, prior_request, -1), prior_rank),
            arranged(jnp.where(own_mask == 1, own_request, -1), rank),
        ]
    )
    key_ids = jnp.concatenate([arranged(prior_ids, prior_rank), ids])
    half = HD // 2
    inv_freq = ROPE_BASE ** (-2.0 * jnp.arange(half, dtype=jnp.float32) / HD)
    angles = position[:, None] * jnp.tile(inv_freq, LANES // half)[None, :]
    sign = jnp.where(jnp.arange(LANES, dtype=jnp.int32) % HD < half, -1.0, 1.0)
    cosine = jnp.cos(angles)
    sine = jnp.sin(angles) * sign[None, :]
    n_pages = page_table.shape[0]
    pages = jnp.arange(n_pages, dtype=jnp.int32)
    place = jnp.sum(
        jnp.where(page_table[:, None] == pages[None, :], pages[:, None], 0), axis=0
    )
    experts = router.shape[1]
    wide_router = jnp.pad(router, ((0, 0), (0, -experts % LANES)))
    all_routes = lax.all_gather(routes.T, "tok", axis=0, tiled=True)
    all_routes, place, key_request, key_ids, wide_router, cosine, sine = lax.optimization_barrier(
        (all_routes, place, key_request, key_ids, wide_router, cosine, sine)
    )

    columns = w_qkv.shape[1]
    queries, own_kv = pl.pallas_call(
        functools.partial(project_kernel, n_head, kv_dev),
        out_shape=[
            jax.ShapeDtypeStruct((kv_dev, QPG, row_tokens, LANES), jnp.bfloat16),
            jax.ShapeDtypeStruct((row_tokens, kv_dev * LANES), jnp.bfloat16),
        ],
        in_specs=[VMEM] * (5 + n_head),
        out_specs=[VMEM] * 2,
        compiler_params=PARAMS,
        name="project",
    )(
        rank[None, :],
        attn_gain[None, :],
        jnp.pad(w_qkv, ((0, 0), (0, -columns % LANES))),
        cosine,
        sine,
        *[states[k] for k in range(n_head)],
    )
    prior_kv = lax.ppermute(own_kv, "tok", [(i, i + 1) for i in range(n_tok - 1)])
    pool_rows = kv_cache.shape[0] * n_tok
    contexts = pl.pallas_call(
        functools.partial(attend_kernel, n_tok, kv_dev, n_head),
        out_shape=[jax.ShapeDtypeStruct((tok_dev, kv_dev * QPG * HD), jnp.bfloat16)] * n_head,
        in_specs=[SMEM] * 2 + [VMEM] * 8 + [pl.BlockSpec(memory_space=pl.ANY)] * n_tok,
        out_specs=[VMEM] * n_head,
        scratch_shapes=[pltpu.VMEM((pool_rows, kv_cache.shape[1]), jnp.bfloat16)]
        + [pltpu.VMEM((kv_dev, QPG, row_tokens, LANES), jnp.float32)] * 3
        + [pltpu.SemaphoreType.DMA],
        compiler_params=PARAMS,
        name="attend",
    )(
        jnp.stack([row_index, in_first]).astype(jnp.int32),
        place,
        queries,
        prior_kv,
        own_kv,
        request[:, None],
        ids[:, None],
        key_request[None, :],
        key_ids[None, :],
        rank[:, None],
        *[shards[d] for d in range(n_tok)],
    )
    context_slots = [contexts[0]] + [crossed(contexts[k], "head", k) for k in range(1, n_head)]
    attn_sum, mid_states, mixed = pl.pallas_call(
        functools.partial(close_kernel, n_head),
        out_shape=[jax.ShapeDtypeStruct(hidden.shape, jnp.bfloat16)] * 3,
        in_specs=[SMEM] + [VMEM] * (3 + n_head),
        out_specs=[VMEM] * 3,
        compiler_params=PARAMS,
        name="close",
    )(
        head_index.astype(jnp.int32)[None],
        hidden,
        o_weight,
        moe_gain[None, :],
        *context_slots,
    )

    slots = spread(mixed, "tok")
    together = min(4, n_tok)
    parts = {}
    for first in range(0, n_tok, together):
        parts.update(
            run_experts(
                slots,
                list(range(first, first + together)),
                row_index,
                all_routes,
                wide_router,
                w_gate_up,
                w_down,
            )
        )
    routed_sum = folded(parts, "tok").astype(jnp.float32)
    layer_out = (mid_states.astype(jnp.float32) + routed_sum).astype(jnp.bfloat16)
    return (attn_sum, layer_out)


def solution(mesh):
    return jax.shard_map(
        per_device,
        mesh=mesh,
        in_specs=(
            P(("tok", "head"), None),
            P(),
            P(None, "head"),
            P("tok", "head"),
            P(),
            P(),
            P(),
            P(),
            P(),
            P(),
            P(),
            P(("tok", "head"), None),
            P("tok", None, None),
            P("tok", None, None),
        ),
        out_specs=(P(("tok", "head"), None), P(("tok", "head"), None)),
        check_vma=False,
    )
```

time: 313 us -> 248 us (0.79); the launches traced: 309 us -> 248 us
  matrix products: 52.4 us -> 0 us
  other arithmetic: 48.2 us -> 12.1 us
  Pallas kernels: 30.4 us -> 61.4 us
  starting transfers between devices: 20.8 us -> 35.6 us
  between operations: 15 us -> 1.16 us
  blocking collectives: 42.8 us -> 29.5 us
  waiting for transfers between devices: 89.7 us -> 95.9 us
    dot_general x12 -> x0, matrix products: 52.4 us -> none  [the longest x5 24.6 us: absorb(): jnp.einsum('tgqn,ngd->tgqd', weights.astype(jnp.bfloat16), keys_values[:,...]
    ppermute x30 -> x47, waiting for transfers between devices: 45.3 us -> 95.9 us  [crossed(): return lax.ppermute(array, axis, [(i, i ^ flip) for i in range(count)])]
    pallas_call x4 -> x7, Pallas kernels: 30.4 us -> 61.4 us  [the longest x4 30.4 us: run_experts(): pl.pallas_call(functools.partial(expert_kernel, count, w_gate_up.shape[0]...]
    all_gather x1 -> x0, waiting for transfers between devices: 28.5 us -> none  [per_device(): piece = lax.all_gather(kv_cache, 'tok', axis=0, tiled=True)]
    reduce_sum x9 -> x4, other arithmetic: 25.2 us -> 2.06 us  [the longest x1 1.33 us: per_device(): jnp.sum(jnp.where(page_table[:, None] == pages[None, :], pages[:, None],...]
    reduce_scatter x1 -> x0, waiting for transfers between devices: 15.8 us -> none  [per_device(): lax.psum_scatter(jnp.dot(context, rows_out, preferred_element_type=jnp.fl...]
    ppermute x30 -> x47, starting transfers between devices: 18.7 us -> 33.4 us  [crossed(): return lax.ppermute(array, axis, [(i, i ^ flip) for i in range(count)])]
    all_gather x2 -> x1, blocking collectives: 42.8 us -> 29.5 us  [per_device(): all_routes = lax.all_gather(routes.T, 'tok', axis=0, tiled=True)]
  transfers between devices with their start and end apart: 33 -> 48, of which waited for: 9 -> 14; matrix products, arithmetic and copies ran while one was open for 12% -> 9% of each run, Pallas kernels for 10% -> 14%
where the time goes in v2:
time: 248 us
  waiting for transfers between devices  95.9 us (39%)
  Pallas kernels  61.4 us (25%)
  starting transfers between devices  35.6 us (14%)
  blocking collectives  29.5 us (12%)
  local copies, waits for them, and re-layouts  12.8 us (5%)
  other arithmetic  12.1 us (5%)
    ppermute x47, waiting for transfers between devices, crossed(): return lax.ppermute(array, axis, [(i, i ^ flip) for i in range(count)])  95.9 us
    ppermute x47, starting transfers between devices, crossed(): return lax.ppermute(array, axis, [(i, i ^ flip) for i in range(count)])  33.4 us
    pallas_call x4, Pallas kernels, run_experts(): pl.pallas_call(functools.partial(expert_kernel, count, w_gate_up.shape[0]...  30.4 us
    all_gather x1, blocking collectives, per_device(): all_routes = lax.all_gather(routes.T, 'tok', axis=0, tiled=True)  29.5 us
    pallas_call x1, Pallas kernels, per_device(): pl.pallas_call(functools.partial(attend_kernel, n_tok, kv_dev, n_head), o...  21.3 us
    pallas_call x1, Pallas kernels, per_device(): pl.pallas_call(functools.partial(project_kernel, n_head, kv_dev), out_sha...  5.34 us
  transfers between devices with their start and end apart: 48, of which 14 were waited for; matrix products, arithmetic and copies ran while one was open for 9% of the time, Pallas kernels for 14%

profile of v2, /device:TPU:0, one launch (start us, length us, event | category | flops | bytes accessed | tf_op | source)
XLA Modules:
  0.0 248.4 jit_solution(2786449240202731568)
XLA Ops:
  1.1 2.6 %collective-permute-start.3 = (bf16[256,512]{1,0:T(8,128)(2,1)}, bf16[256,512]{1,0:T(8,128)(2,1)S(1)}, u32[]{:S(2)}, u32[]{:S(2)}) collective-permute-start(bf16[256,512]{1,0:T(8,128)(2,1)} %refs_0_.3), channel_id=1, source_target_pairs={{0,4},{2,6},{4,0},{6,2},{8,12},{10,14},{12,8},{14,10},{16,20},{18,... | collective-permute-start | bytes 786440 | tf_op jit(solution)/shard_map/ppermute | solution.py:32
  5.3 2.6 %collective-permute-start.9 = (bf16[256,512]{1,0:T(8,128)(2,1)}, bf16[256,512]{1,0:T(8,128)(2,1)S(1)}, u32[]{:S(2)}, u32[]{:S(2)}) collective-permute-start(bf16[256,512]{1,0:T(8,128)(2,1)} %refs_0_.3), channel_id=1, source_target_pairs={{0,16},{2,18},{4,20},{6,22},{8,24},{10,26},{12,28},{14,30},{16,0},... | collective-permute-start | bytes 786440 | tf_op jit(solution)/shard_map/ppermute | solution.py:32
  16.7 3.4 %collective-permute-done.9.refs_8_ = bf16[256,512]{1,0:T(8,128)(2,1)S(1)} collective-permute-done((bf16[256,512]{1,0:T(8,128)(2,1)}, bf16[256,512]{1,0:T(8,128)(2,1)S(1)}, u32[]{:S(2)}, u32[]{:S(2)}) %collective-permute-start.9) | collective-permute-done | bytes 262176 | tf_op jit(solution)/shard_map/ppermute | solution.py:32
  27.1 29.5 %all_gather.3.refs_4_ = s32[128,128]{1,0:T(8,128)} all-gather(s32[8,128]{1,0:T(8,128)} %bitcast.42), channel_id=1, replica_groups=mesh['tok'=16,'head'=2] {'tok'}, dimensions={0}, use_global_device_ids=true | all-gather | bytes 69632 | tf_op jit(solution)/shard_map/all_gather | solution.py:392
  59.1 5.3 %project.1 = (bf16[4,3,256,128]{3,2,1,0:T(8,128)(2,1)}, bf16[256,512]{1,0:T(8,128)(2,1)}) custom-call(s32[1,256]{1,0:T(1,128)} %bitcast.36, f32[1,1536]{1,0:T(1,128)} %broadcast_in_dim.187.gain_ref, bf16[1536,1280]{1,0:T(8,128)(2,1)} %weight_ref.2, f32[256,128]{1,0:T(8,128)} %get-tuple-element.33.cos_ref, f32[256,128]{1,0:T(8,128)} %get-tuple-element.34.sin_ref, ...), custom_call_target="tpu_custom_call" | custom-call | tf_op jit(solution)/shard_map/project/pallas_call | solution.py:398
  64.5 2.3 collective-permute-start.1
  73.0 21.3 %attend.1 = (bf16[128,768]{1,0:T(8,128)(2,1)}, bf16[128,768]{1,0:T(8,128)(2,1)}) custom-call(s32[2]{0:T(128)} %pad_add_fusion.2.scalar_ref, s32[256]{0:T(256)} %select_reduce_fusion.6.place_ref, bf16[4,3,256,128]{3,2,1,0:T(8,128)(2,1)} %get-tuple-element.35.query_ref, bf16[256,512]{1,0:T(8,128)(2,1)} %copy-done.31, ...), custom_call_target="tpu_custom_call" | custom-call | tf_op jit(solution)/shard_map/attend/pallas_call | solution.py:418
  96.4 5.0 %collective-permute-done.17.refs_1_ = bf16[128,768]{1,0:T(8,128)(2,1)S(1)} collective-permute-done((bf16[128,768]{1,0:T(8,128)(2,1)}, bf16[128,768]{1,0:T(8,128)(2,1)S(1)}, u32[]{:S(2)}, u32[]{:S(2)}) %collective-permute-start.17) | collective-permute-done | bytes 196640 | tf_op jit(solution)/shard_map/ppermute | solution.py:32
  102.1 4.4 %close.1 = (bf16[128,1536]{1,0:T(8,128)(2,1)}, bf16[128,1536]{1,0:T(8,128)(2,1)}, bf16[128,1536]{1,0:T(8,128)(2,1)}) custom-call(s32[1]{0:T(128)} %bitcast.scalar_ref, bf16[128,1536]{1,0:T(8,128)(2,1)} %hidden_ref.1, bf16[1536,1536]{1,0:T(8,128)(2,1)} %weight_ref.3, f32[1,1536]{1,0:T(1,128)} %broadcast_in_dim.169.gain_ref, ...), custom_call_target="tpu_custom_call" | custom-call | tf_op jit(solution)/shard_map/close/pallas_call | solution.py:442
  106.5 3.2 %collective-permute-start.32 = (bf16[128,1536]{1,0:T(8,128)(2,1)}, bf16[128,1536]{1,0:T(8,128)(2,1)S(1)}, u32[]{:S(2)}, u32[]{:S(2)}) collective-permute-start(bf16[128,1536]{1,0:T(8,128)(2,1)} %get-tuple-element.43.refs_0_), channel_id=1, source_target_pairs={{0,16},{2,18},{4,20},{6,22},{8,24},{10,26},{12,28},{14,30},{16,0},... | collective-permute-start | bytes 1179656 | tf_op jit(solution)/shard_map/ppermute | solution.py:32
  110.2 16.8 %collective-permute-done.32.refs_0_ = bf16[128,1536]{1,0:T(8,128)(2,1)S(1)} collective-permute-done((bf16[128,1536]{1,0:T(8,128)(2,1)}, bf16[128,1536]{1,0:T(8,128)(2,1)S(1)}, u32[]{:S(2)}, u32[]{:S(2)}) %collective-permute-start.32) | collective-permute-done | bytes 393248 | tf_op jit(solution)/shard_map/ppermute | solution.py:32
  130.3 8.8 %collective-permute-done.34.refs_2_ = bf16[128,1536]{1,0:T(8,128)(2,1)S(1)} collective-permute-done((bf16[128,1536]{1,0:T(8,128)(2,1)S(1)}, bf16[128,1536]{1,0:T(8,128)(2,1)S(1)}, u32[]{:S(2)}, u32[]{:S(2)}) %collective-permute-start.34) | collective-permute-done | bytes 393248 | tf_op jit(solution)/shard_map/ppermute | solution.py:32
  139.6 6.0 %collective-permute-done.26.refs_2_ = bf16[128,1536]{1,0:T(8,128)(2,1)S(1)} collective-permute-done((bf16[128,1536]{1,0:T(8,128)(2,1)S(1)}, bf16[128,1536]{1,0:T(8,128)(2,1)S(1)}, u32[]{:S(2)}, u32[]{:S(2)}) %collective-permute-start.26) | collective-permute-done | bytes 393248 | tf_op jit(solution)/shard_map/ppermute | solution.py:32
  146.5 7.6 %experts.4 = (bf16[128,1536]{1,0:T(8,128)(2,1)}, bf16[128,1536]{1,0:T(8,128)(2,1)}, bf16[128,1536]{1,0:T(8,128)(2,1)}, bf16[128,1536]{1,0:T(8,128)(2,1)}) custom-call(s32[5]{0:T(128)} %stack.77.where_ref, bf16[128,1536]{1,0:T(8,128)(2,1)} %get-tuple-element.43.refs_0_, bf16[128,1536]{1,0:T(8,128)(2,1)} %copy-done.17, bf16[128,1536]{1,0:T(8,128)(2,1)} %copy-done.16, ...), custom_call_target="tpu_custom_call" | custom-call | tf_op jit(solution)/shard_map/experts/pallas_call | solution.py:315
  156.6 7.6 %experts.6 = (bf16[128,1536]{1,0:T(8,128)(2,1)}, bf16[128,1536]{1,0:T(8,128)(2,1)}, bf16[128,1536]{1,0:T(8,128)(2,1)}, bf16[128,1536]{1,0:T(8,128)(2,1)}) custom-call(s32[5]{0:T(128)} %stack.87.where_ref, bf16[128,1536]{1,0:T(8,128)(2,1)} %copy-done.10, bf16[128,1536]{1,0:T(8,128)(2,1)} %copy-done.14, bf16[128,1536]{1,0:T(8,128)(2,1)} %copy-done.13, ...), custom_call_target="tpu_custom_call" | custom-call | tf_op jit(solution)/shard_map/experts/pallas_call | solution.py:315
  165.0 7.6 %experts.5 = (bf16[128,1536]{1,0:T(8,128)(2,1)}, bf16[128,1536]{1,0:T(8,128)(2,1)}, bf16[128,1536]{1,0:T(8,128)(2,1)}, bf16[128,1536]{1,0:T(8,128)(2,1)}) custom-call(s32[5]{0:T(128)} %stack.82.where_ref, bf16[128,1536]{1,0:T(8,128)(2,1)} %copy-done.9, bf16[128,1536]{1,0:T(8,128)(2,1)} %copy-done.15, bf16[128,1536]{1,0:T(8,128)(2,1)} %copy-done.11, ...), custom_call_target="tpu_custom_call" | custom-call | tf_op jit(solution)/shard_map/experts/pallas_call | solution.py:315
  175.8 7.6 %experts.7 = (bf16[128,1536]{1,0:T(8,128)(2,1)}, bf16[128,1536]{1,0:T(8,128)(2,1)}, bf16[128,1536]{1,0:T(8,128)(2,1)}, bf16[128,1536]{1,0:T(8,128)(2,1)}) custom-call(s32[5]{0:T(128)} %stack.92.where_ref, bf16[128,1536]{1,0:T(8,128)(2,1)} %copy-done.8, bf16[128,1536]{1,0:T(8,128)(2,1)} %copy-done.18, bf16[128,1536]{1,0:T(8,128)(2,1)} %copy-done.12, ...), custom_call_target="tpu_custom_call" | custom-call | tf_op jit(solution)/shard_map/experts/pallas_call | solution.py:315
  189.1 9.8 %collective-permute-done.45 = bf16[128,1536]{1,0:T(8,128)(2,1)S(1)} collective-permute-done((bf16[128,1536]{1,0:T(8,128)(2,1)S(1)}, bf16[128,1536]{1,0:T(8,128)(2,1)S(1)}, u32[]{:S(2)}, u32[]{:S(2)}) %collective-permute-start.45) | collective-permute-done | bytes 393248 | tf_op jit(solution)/shard_map/ppermute | solution.py:32
  202.1 13.6 %collective-permute-done.30 = bf16[128,1536]{1,0:T(8,128)(2,1)S(1)} collective-permute-done((bf16[128,1536]{1,0:T(8,128)(2,1)S(1)}, bf16[128,1536]{1,0:T(8,128)(2,1)S(1)}, u32[]{:S(2)}, u32[]{:S(2)}) %collective-permute-start.30) | collective-permute-done | bytes 393248 | tf_op jit(solution)/shard_map/ppermute | solution.py:32
  216.2 1.8 collective-permute-start.31
  218.0 5.4 %collective-permute-done.38 = bf16[128,1536]{1,0:T(8,128)(2,1)S(1)} collective-permute-done((bf16[128,1536]{1,0:T(8,128)(2,1)S(1)}, bf16[128,1536]{1,0:T(8,128)(2,1)S(1)}, u32[]{:S(2)}, u32[]{:S(2)}) %collective-permute-start.38) | collective-permute-done | bytes 393248 | tf_op jit(solution)/shard_map/ppermute | solution.py:32
  223.4 8.6 %collective-permute-done.46 = bf16[128,1536]{1,0:T(8,128)(2,1)S(1)} collective-permute-done((bf16[128,1536]{1,0:T(8,128)(2,1)S(1)}, bf16[128,1536]{1,0:T(8,128)(2,1)S(1)}, u32[]{:S(2)}, u32[]{:S(2)}) %collective-permute-start.46) | collective-permute-done | bytes 393248 | tf_op jit(solution)/shard_map/ppermute | solution.py:32
  233.2 5.0 %collective-permute-done.31 = bf16[128,1536]{1,0:T(8,128)(2,1)S(1)} collective-permute-done((bf16[128,1536]{1,0:T(8,128)(2,1)S(1)}, bf16[128,1536]{1,0:T(8,128)(2,1)S(1)}, u32[]{:S(2)}, u32[]{:S(2)}) %collective-permute-start.31) | collective-permute-done | bytes 393248 | tf_op jit(solution)/shard_map/ppermute | solution.py:32
  238.3 9.1 %collective-permute-done.47 = bf16[128,1536]{1,0:T(8,128)(2,1)S(1)} collective-permute-done((bf16[128,1536]{1,0:T(8,128)(2,1)S(1)}, bf16[128,1536]{1,0:T(8,128)(2,1)S(1)}, u32[]{:S(2)}, u32[]{:S(2)}) %collective-permute-start.47) | collective-permute-done | bytes 393248 | tf_op jit(solution)/shard_map/ppermute | solution.py:32
  (199 shorter events, 52.5 us)
Async XLA Ops:
  0.6 22.0 %collective-permute-start.2 = (bf16[256,512]{1,0:T(8,128)(2,1)}, bf16[256,512]{1,0:T(8,128)(2,1)S(1)}, u32[]{:S(2)}, u32[]{:S(2)}) collective-permute-start(bf16[256,512]{1,0:T(8,128)(2,1)} %refs_0_.3), channel_id=1, source_target_pairs={{0,2},{2,0},{4,6},{6,4},{8,10},{10,8},{12,14},{14,12},{16,18},{18,... | collective-permute-start | bytes 786440 | tf_op jit(solution)/shard_map/ppermute | solution.py:32
  3.7 18.9 %collective-permute-start.5 = (bf16[256,512]{1,0:T(8,128)(2,1)}, bf16[256,512]{1,0:T(8,128)(2,1)S(1)}, u32[]{:S(2)}, u32[]{:S(2)}) collective-permute-start(bf16[256,512]{1,0:T(8,128)(2,1)} %refs_0_.3), channel_id=1, source_target_pairs={{0,8},{2,10},{4,12},{6,14},{8,0},{10,2},{12,4},{14,6},{16,24},{18,... | collective-permute-start | bytes 786440 | tf_op jit(solution)/shard_map/ppermute | solution.py:32
  22.6 41.9 %collective-permute-start.6 = (bf16[256,512]{1,0:T(8,128)(2,1)S(1)}, bf16[256,512]{1,0:T(8,128)(2,1)S(1)}, u32[]{:S(2)}, u32[]{:S(2)}) collective-permute-start(bf16[256,512]{1,0:T(8,128)(2,1)S(1)} %collective-permute-done.5.refs_4_), channel_id=1, source_target_pairs={{0,2},{2,0},{4,6},{6,4},{8,10},{10,8},{12,14},{14,12},{16,18},{18,... | collective-permute-start | bytes 786440 | tf_op jit(solution)/shard_map/ppermute | solution.py:32
  22.7 44.1 %collective-permute-start.7 = (bf16[256,512]{1,0:T(8,128)(2,1)S(1)}, bf16[256,512]{1,0:T(8,128)(2,1)S(1)}, u32[]{:S(2)}, u32[]{:S(2)}) collective-permute-start(bf16[256,512]{1,0:T(8,128)(2,1)S(1)} %collective-permute-done.5.refs_4_), channel_id=1, source_target_pairs={{0,4},{2,6},{4,0},{6,2},{8,12},{10,14},{12,8},{14,10},{16,20},{18,... | collective-permute-start | bytes 786440 | tf_op jit(solution)/shard_map/ppermute | solution.py:32
  23.3 43.5 %collective-permute-start.10 = (bf16[256,512]{1,0:T(8,128)(2,1)S(1)}, bf16[256,512]{1,0:T(8,128)(2,1)S(1)}, u32[]{:S(2)}, u32[]{:S(2)}) collective-permute-start(bf16[256,512]{1,0:T(8,128)(2,1)S(1)} %collective-permute-done.9.refs_8_), channel_id=1, source_target_pairs={{0,2},{2,0},{4,6},{6,4},{8,10},{10,8},{12,14},{14,12},{16,18},{18,... | collective-permute-start | bytes 786440 | tf_op jit(solution)/shard_map/ppermute | solution.py:32
  23.4 43.9 %collective-permute-start.11 = (bf16[256,512]{1,0:T(8,128)(2,1)S(1)}, bf16[256,512]{1,0:T(8,128)(2,1)S(1)}, u32[]{:S(2)}, u32[]{:S(2)}) collective-permute-start(bf16[256,512]{1,0:T(8,128)(2,1)S(1)} %collective-permute-done.9.refs_8_), channel_id=1, source_target_pairs={{0,4},{2,6},{4,0},{6,2},{8,12},{10,14},{12,8},{14,10},{16,20},{18,... | collective-permute-start | bytes 786440 | tf_op jit(solution)/shard_map/ppermute | solution.py:32
  26.6 40.9 %collective-permute-start.15 = (bf16[256,512]{1,0:T(8,128)(2,1)S(1)}, bf16[256,512]{1,0:T(8,128)(2,1)S(1)}, u32[]{:S(2)}, u32[]{:S(2)}) collective-permute-start(bf16[256,512]{1,0:T(8,128)(2,1)S(1)} %collective-permute-done.13.refs_12_), channel_id=1, source_target_pairs={{0,4},{2,6},{4,0},{6,2},{8,12},{10,14},{12,8},{14,10},{16,20},{18,... | collective-permute-start | bytes 786440 | tf_op jit(solution)/shard_map/ppermute | solution.py:32
  106.5 20.6 %collective-permute-start.32 = (bf16[128,1536]{1,0:T(8,128)(2,1)}, bf16[128,1536]{1,0:T(8,128)(2,1)S(1)}, u32[]{:S(2)}, u32[]{:S(2)}) collective-permute-start(bf16[128,1536]{1,0:T(8,128)(2,1)} %get-tuple-element.43.refs_0_), channel_id=1, source_target_pairs={{0,16},{2,18},{4,20},{6,22},{8,24},{10,26},{12,28},{14,30},{16,0},... | collective-permute-start | bytes 1179656 | tf_op jit(solution)/shard_map/ppermute | solution.py:32
  109.7 18.8 %collective-permute-start.24 = (bf16[128,1536]{1,0:T(8,128)(2,1)}, bf16[128,1536]{1,0:T(8,128)(2,1)S(1)}, u32[]{:S(2)}, u32[]{:S(2)}) collective-permute-start(bf16[128,1536]{1,0:T(8,128)(2,1)} %get-tuple-element.43.refs_0_), channel_id=1, source_target_pairs={{0,8},{2,10},{4,12},{6,14},{8,0},{10,2},{12,4},{14,6},{16,24},{18,... | collective-permute-start | bytes 1179656 | tf_op jit(solution)/shard_map/ppermute | solution.py:32
  110.2 18.9 %collective-permute-start.19 = (bf16[128,1536]{1,0:T(8,128)(2,1)}, bf16[128,1536]{1,0:T(8,128)(2,1)S(1)}, u32[]{:S(2)}, u32[]{:S(2)}) collective-permute-start(bf16[128,1536]{1,0:T(8,128)(2,1)} %get-tuple-element.43.refs_0_), channel_id=1, source_target_pairs={{0,4},{2,6},{4,0},{6,2},{8,12},{10,14},{12,8},{14,10},{16,20},{18,... | collective-permute-start | bytes 1179656 | tf_op jit(solution)/shard_map/ppermute | solution.py:32
  110.2 18.9 %collective-permute-start.18 = (bf16[128,1536]{1,0:T(8,128)(2,1)}, bf16[128,1536]{1,0:T(8,128)(2,1)S(1)}, u32[]{:S(2)}, u32[]{:S(2)}) collective-permute-start(bf16[128,1536]{1,0:T(8,128)(2,1)} %get-tuple-element.43.refs_0_), channel_id=1, source_target_pairs={{0,2},{2,0},{4,6},{6,4},{8,10},{10,8},{12,14},{14,12},{16,18},{18,... | collective-permute-start | bytes 1179656 | tf_op jit(solution)/shard_map/ppermute | solution.py:32
  129.2 24.9 %collective-permute-start.33 = (bf16[128,1536]{1,0:T(8,128)(2,1)S(1)}, bf16[128,1536]{1,0:T(8,128)(2,1)S(1)}, u32[]{:S(2)}, u32[]{:S(2)}) collective-permute-start(bf16[128,1536]{1,0:T(8,128)(2,1)S(1)} %collective-permute-done.32.refs_0_), channel_id=1, source_target_pairs={{0,2},{2,0},{4,6},{6,4},{8,10},{10,8},{12,14},{14,12},{16,18},{18,... | collective-permute-start | bytes 1179656 | tf_op jit(solution)/shard_map/ppermute | solution.py:32
  139.1 17.5 %collective-permute-start.35 = (bf16[128,1536]{1,0:T(8,128)(2,1)S(1)}, bf16[128,1536]{1,0:T(8,128)(2,1)}, u32[]{:S(2)}, u32[]{:S(2)}) collective-permute-start(bf16[128,1536]{1,0:T(8,128)(2,1)S(1)} %collective-permute-done.34.refs_2_), channel_id=1, source_target_pairs={{0,2},{2,0},{4,6},{6,4},{8,10},{10,8},{12,14},{14,12},{16,18},{18,... | collective-permute-start | bytes 1179656 | tf_op jit(solution)/shard_map/ppermute | solution.py:32
  139.1 25.1 %collective-permute-start.25 = (bf16[128,1536]{1,0:T(8,128)(2,1)S(1)}, bf16[128,1536]{1,0:T(8,128)(2,1)S(1)}, u32[]{:S(2)}, u32[]{:S(2)}) collective-permute-start(bf16[128,1536]{1,0:T(8,128)(2,1)S(1)} %collective-permute-done.24.refs_0_), channel_id=1, source_target_pairs={{0,2},{2,0},{4,6},{6,4},{8,10},{10,8},{12,14},{14,12},{16,18},{18,... | collective-permute-start | bytes 1179656 | tf_op jit(solution)/shard_map/ppermute | solution.py:32
  145.6 26.9 %collective-permute-start.41 = (bf16[128,1536]{1,0:T(8,128)(2,1)S(1)}, bf16[128,1536]{1,0:T(8,128)(2,1)S(1)}, u32[]{:S(2)}, u32[]{:S(2)}) collective-permute-start(bf16[128,1536]{1,0:T(8,128)(2,1)S(1)} %collective-permute-done.39.refs_0_), channel_id=1, source_target_pairs={{0,4},{2,6},{4,0},{6,2},{8,12},{10,14},{12,8},{14,10},{16,20},{18,... | collective-permute-start | bytes 1179656 | tf_op jit(solution)/shard_map/ppermute | solution.py:32
  146.5 18.3 %collective-permute-start.27 = (bf16[128,1536]{1,0:T(8,128)(2,1)S(1)}, bf16[128,1536]{1,0:T(8,128)(2,1)}, u32[]{:S(2)}, u32[]{:S(2)}) collective-permute-start(bf16[128,1536]{1,0:T(8,128)(2,1)S(1)} %collective-permute-done.26.refs_2_), channel_id=1, source_target_pairs={{0,2},{2,0},{4,6},{6,4},{8,10},{10,8},{12,14},{14,12},{16,18},{18,... | collective-permute-start | bytes 1179656 | tf_op jit(solution)/shard_map/ppermute | solution.py:32
  154.1 19.0 %collective-permute-start.22 = (bf16[128,1536]{1,0:T(8,128)(2,1)}, bf16[128,1536]{1,0:T(8,128)(2,1)S(1)}, u32[]{:S(2)}, u32[]{:S(2)}) collective-permute-start(bf16[128,1536]{1,0:T(8,128)(2,1)} %get-tuple-element.49), channel_id=1, source_target_pairs={{0,2},{2,0},{4,6},{6,4},{8,10},{10,8},{12,14},{14,12},{16,18},{18,... | collective-permute-start | bytes 1179656 | tf_op jit(solution)/shard_map/ppermute | solution.py:32
  156.5 76.7 %collective-permute-start.21 = (bf16[128,1536]{1,0:T(8,128)(2,1)}, bf16[128,1536]{1,0:T(8,128)(2,1)S(1)}, u32[]{:S(2)}, u32[]{:S(2)}) collective-permute-start(bf16[128,1536]{1,0:T(8,128)(2,1)} %get-tuple-element.47), channel_id=1, source_target_pairs={{0,2},{2,0},{4,6},{6,4},{8,10},{10,8},{12,14},{14,12},{16,18},{18,... | collective-permute-start | bytes 1179656 | tf_op jit(solution)/shard_map/ppermute | solution.py:32
  164.8 18.6 %collective-permute-start.37 = (bf16[128,1536]{1,0:T(8,128)(2,1)}, bf16[128,1536]{1,0:T(8,128)(2,1)S(1)}, u32[]{:S(2)}, u32[]{:S(2)}) collective-permute-start(bf16[128,1536]{1,0:T(8,128)(2,1)} %get-tuple-element.57), channel_id=1, source_target_pairs={{0,2},{2,0},{4,6},{6,4},{8,10},{10,8},{12,14},{14,12},{16,18},{18,... | collective-permute-start | bytes 1179656 | tf_op jit(solution)/shard_map/ppermute | solution.py:32
  172.6 43.7 %collective-permute-start.36 = (bf16[128,1536]{1,0:T(8,128)(2,1)}, bf16[128,1536]{1,0:T(8,128)(2,1)S(1)}, u32[]{:S(2)}, u32[]{:S(2)}) collective-permute-start(bf16[128,1536]{1,0:T(8,128)(2,1)} %get-tuple-element.55), channel_id=1, source_target_pairs={{0,2},{2,0},{4,6},{6,4},{8,10},{10,8},{12,14},{14,12},{16,18},{18,... | collective-permute-start | bytes 1179656 | tf_op jit(solution)/shard_map/ppermute | solution.py:32
  175.0 26.2 %collective-permute-start.28 = (bf16[128,1536]{1,0:T(8,128)(2,1)}, bf16[128,1536]{1,0:T(8,128)(2,1)S(1)}, u32[]{:S(2)}, u32[]{:S(2)}) collective-permute-start(bf16[128,1536]{1,0:T(8,128)(2,1)} %get-tuple-element.51), channel_id=1, source_target_pairs={{0,2},{2,0},{4,6},{6,4},{8,10},{10,8},{12,14},{14,12},{16,18},{18,... | collective-permute-start | bytes 1179656 | tf_op jit(solution)/shard_map/ppermute | solution.py:32
  188.2 45.0 %collective-permute-start.23 = (bf16[128,1536]{1,0:T(8,128)(2,1)S(1)}, bf16[128,1536]{1,0:T(8,128)(2,1)S(1)}, u32[]{:S(2)}, u32[]{:S(2)}) collective-permute-start(bf16[128,1536]{1,0:T(8,128)(2,1)S(1)} %add_convert_fusion.7), channel_id=1, source_target_pairs={{0,4},{2,6},{4,0},{6,2},{8,12},{10,14},{12,8},{14,10},{16,20},{18,... | collective-permute-start | bytes 1179656 | tf_op jit(solution)/shard_map/ppermute | solution.py:32
  201.2 22.1 %collective-permute-start.38 = (bf16[128,1536]{1,0:T(8,128)(2,1)S(1)}, bf16[128,1536]{1,0:T(8,128)(2,1)S(1)}, u32[]{:S(2)}, u32[]{:S(2)}) collective-permute-start(bf16[128,1536]{1,0:T(8,128)(2,1)S(1)} %add_convert_fusion.4), channel_id=1, source_target_pairs={{0,4},{2,6},{4,0},{6,2},{8,12},{10,14},{12,8},{14,10},{16,20},{18,... | collective-permute-start | bytes 1179656 | tf_op jit(solution)/shard_map/ppermute | solution.py:32
  216.2 22.0 %collective-permute-start.31 = (bf16[128,1536]{1,0:T(8,128)(2,1)S(1)}, bf16[128,1536]{1,0:T(8,128)(2,1)S(1)}, u32[]{:S(2)}, u32[]{:S(2)}) collective-permute-start(bf16[128,1536]{1,0:T(8,128)(2,1)S(1)} %add_convert_fusion.5), channel_id=1, source_target_pairs={{0,8},{2,10},{4,12},{6,14},{8,0},{10,2},{12,4},{14,6},{16,24},{18,... | collective-permute-start | bytes 1179656 | tf_op jit(solution)/shard_map/ppermute | solution.py:32
  (60 other events, 1090.7 us)

commit v3 on v2

--- a/solution.py
+++ b/solution.py
@@ -32,33 +32,39 @@
     return lax.ppermute(array, axis, [(i, i ^ flip) for i in range(count)])
 
 
-def spread(own, axis):
-    count = lax.axis_size(axis)
+def spread(own, axis, bits):
     slots = {0: own}
-    bit = count // 2
-    while bit:
+    for bit in bits:
         for d in sorted(slots):
             slots[d | bit] = crossed(slots[d], axis, bit)
-        bit //= 2
     return slots
 
 
-def folded(parts, axis):
-    count = lax.axis_size(axis)
+def folded(parts, axis, bits):
     parts = dict(parts)
-    bit = 1
-    while bit < count:
+    for bit in bits:
         for d in sorted(parts, reverse=True):
             if d & bit:
                 came = crossed(parts.pop(d).astype(jnp.bfloat16), axis, bit)
                 parts[d ^ bit] = parts[d ^ bit].astype(jnp.float32) + came.astype(jnp.float32)
-        bit *= 2
     return parts[0]
+
+
+def bits_of(count):
+    return [1 << i for i in reversed(range(count.bit_length() - 1))]
 
 
 VMEM = pl.BlockSpec(memory_space=pltpu.VMEM)
 SMEM = pl.BlockSpec(memory_space=pltpu.SMEM)
-PARAMS = pltpu.CompilerParams(vmem_limit_bytes=56 << 20)
+TAIL = 16
+
+
+def params(mib):
+    return pltpu.CompilerParams(vmem_limit_bytes=mib << 20)
+
+
+def pinned(array):
+    return pltpu.with_memory_space_constraint(array, pltpu.VMEM)
 
 
 def token_info(token_ids, lengths, request_group):
@@ -152,12 +158,13 @@
 ):
     shard_refs = refs[:shards]
     out_refs = refs[shards : shards + slots]
-    pool_ref, peak_ref, total_ref, sum_ref, arrived = refs[shards + slots :]
+    routes_ref, pool_ref, peak_ref, total_ref, sum_ref, arrived, told = refs[shards + slots :]
     me = scalar_ref[0]
     in_first = scalar_ref[1]
     rows = query_ref.shape[2]
     blocks = rows // BLOCK
-    shard_pages = shard_refs[0].shape[0] // PAGE
+    shard_rows = shard_refs[0].shape[0] - TAIL
+    shard_pages = shard_rows // PAGE
 
     for d in range(shards):
         def start(j, carry, d=d):
@@ -170,6 +177,11 @@
             return carry
 
         lax.fori_loop(0, shard_pages, start, 0)
+        pltpu.make_async_copy(
+            shard_refs[d].at[shard_rows : shard_rows + TAIL, : routes_ref.shape[1]],
+            routes_ref.at[d * TAIL : (d + 1) * TAIL, :],
+            told,
+        ).start()
 
     def near(b, carry):
         at = pl.ds(pl.multiple_of(b * BLOCK, BLOCK), BLOCK)
@@ -196,6 +208,7 @@
 
     lax.fori_loop(0, blocks, near, 0)
     pltpu.make_async_copy(pool_ref, pool_ref, arrived).wait()
+    pltpu.make_async_copy(routes_ref, routes_ref, told).wait()
 
     group_rows = pool_ref.shape[0] // GROUPS
     full = (in_first + BLOCK - 1) // BLOCK
@@ -272,19 +285,21 @@
     mixed_ref[...] = (wide * scale * gain_ref[...]).astype(jnp.bfloat16)
 
 
-def expert_kernel(count, experts_here, where_ref, *refs):
+def expert_kernel(offsets, parts, where_ref, *refs):
+    count = len(offsets)
     state_refs = refs[:count]
     routes_ref, router_ref, up_ref, down_ref = refs[count : count + 4]
-    out_refs = refs[count + 4 :]
-    me = where_ref[0]
+    swapped = refs[count + 4 : count + 4 + 3 * parts]
+    out_refs = refs[count + 4 + 3 * parts :]
     rows = state_refs[0].shape[0]
     lanes = router_ref.shape[1]
+    experts_here = up_ref.shape[0]
     states = jnp.concatenate([ref[...] for ref in state_refs], axis=0)
     lane = lax.broadcasted_iota(jnp.int32, (rows, lanes), 1)
     hits = []
-    for i in range(count):
-        first = pl.multiple_of(where_ref[1 + i] * TOPK, TOPK)
-        routes = jnp.transpose(routes_ref[pl.ds(first, TOPK), :].astype(jnp.float32)).astype(jnp.int32)
+    for d in offsets:
+        routes = routes_ref[d * TAIL : (d + 1) * TAIL, :].astype(jnp.float32)
+        routes = jnp.transpose(routes).astype(jnp.int32)
         hit = jnp.zeros((rows, lanes), jnp.float32)
         for k in range(TOPK):
             hit = jnp.where(lane == routes[:, k : k + 1], 1.0, hit)
@@ -294,32 +309,45 @@
     logits = jnp.where(hit, logits, MASKED)
     peak = jnp.max(logits, axis=-1, keepdims=True)
     shares = jnp.where(hit, jnp.exp(logits - peak), 0.0)
-    total = jnp.sum(shares, axis=-1, keepdims=True)
+    shares = shares / jnp.sum(shares, axis=-1, keepdims=True)
     lane = lax.broadcasted_iota(jnp.int32, shares.shape, 1)
+
+    def gate_of(expert):
+        return jnp.sum(jnp.where(lane == expert, shares, 0.0), axis=-1, keepdims=True)
+
+    def through(lead, rest, down):
+        activated = (lead / (1.0 + jnp.exp(-lead)) * rest).astype(jnp.bfloat16)
+        return jnp.dot(activated, down, preferred_element_type=jnp.float32)
+
     result = None
     for x in range(experts_here):
-        mine = jnp.sum(jnp.where(lane == me * experts_here + x, shares, 0.0), axis=-1, keepdims=True)
-        gate = mine / total
         joined = jnp.dot(states, up_ref[x], preferred_element_type=jnp.float32)
-        lead = joined[:, :FFE]
-        activated = (lead / (1.0 + jnp.exp(-lead)) * joined[:, FFE:]).astype(jnp.bfloat16)
-        part = gate * jnp.dot(activated, down_ref[x], preferred_element_type=jnp.float32)
+        part = through(joined[:, :FFE], joined[:, FFE:], down_ref[x])
+        part = gate_of(where_ref[0] * experts_here + x) * part
         result = part if result is None else result + part
+    for x in range(experts_here):
+        total = None
+        for k in range(parts):
+            lead_ref, rest_ref, other_ref = swapped[3 * k : 3 * k + 3]
+            lead = jnp.dot(states, lead_ref[x], preferred_element_type=jnp.float32)
+            rest = jnp.dot(states, rest_ref[x], preferred_element_type=jnp.float32)
+            part = through(lead, rest, other_ref[x])
+            total = part if total is None else total + part
+        result = result + gate_of(where_ref[1] * experts_here + x) * total
     for i in range(count):
         out_refs[i][...] = result[i * rows : (i + 1) * rows].astype(jnp.bfloat16)
 
 
-def run_experts(slots, offsets, me, routes, router, w_gate_up, w_down):
+def run_experts(slots, offsets, where, routes, router, w_gate_up, w_down, swapped):
     count = len(offsets)
-    where = jnp.stack([me] + [me ^ d for d in offsets]).astype(jnp.int32)
     outs = pl.pallas_call(
-        functools.partial(expert_kernel, count, w_gate_up.shape[0]),
+        functools.partial(expert_kernel, offsets, len(swapped) // 3),
         out_shape=[jax.ShapeDtypeStruct(slots[d].shape, jnp.bfloat16) for d in offsets],
-        in_specs=[SMEM] + [VMEM] * (count + 4),
+        in_specs=[SMEM] + [VMEM] * (count + 4 + len(swapped)),
         out_specs=[VMEM] * count,
-        compiler_params=PARAMS,
+        compiler_params=params(28),
         name="experts",
-    )(where, *[slots[d] for d in offsets], routes, router, w_gate_up, w_down)
+    )(where, *[slots[d] for d in offsets], routes, router, w_gate_up, w_down, *swapped)
     return dict(zip(offsets, outs))
 
 
@@ -347,8 +375,25 @@
     row_index = lax.axis_index("tok")
     head_index = lax.axis_index("head")
 
-    states = spread(hidden, "head")
-    shards = spread(kv_cache, "tok")
+    states = spread(hidden, "head", bits_of(n_head))
+    told = jnp.pad(
+        routes.T.astype(jnp.bfloat16),
+        ((0, TAIL - TOPK), (0, kv_cache.shape[1] - tok_dev)),
+    )
+    swap = min(2, n_tok // 2)
+    shards = spread(jnp.concatenate([kv_cache, told], axis=0), "tok", bits_of(n_tok))
+
+    share = FFE // n_head
+    lead = lax.dynamic_slice_in_dim(w_gate_up, head_index * share, share, 2)
+    rest = lax.dynamic_slice_in_dim(w_gate_up, FFE + head_index * share, share, 2)
+    down = lax.dynamic_slice_in_dim(w_down, head_index * share, share, 1)
+    lead, rest, down, _ = lax.optimization_barrier(
+        (lead, rest, down, shards[n_tok - 1 - (swap - 1)])
+    )
+    triple = [
+        spread(crossed(w, "tok", swap), "head", bits_of(n_head)) for w in (lead, rest, down)
+    ]
+    swapped = [w[k] for k in range(n_head) for w in triple]
 
     within = jnp.arange(tok_dev, dtype=jnp.int32)
     row_offset = jnp.concatenate(
@@ -389,9 +434,8 @@
     )
     experts = router.shape[1]
     wide_router = jnp.pad(router, ((0, 0), (0, -experts % LANES)))
-    all_routes = lax.all_gather(routes.T, "tok", axis=0, tiled=True)
-    all_routes, place, key_request, key_ids, wide_router, cosine, sine = lax.optimization_barrier(
-        (all_routes, place, key_request, key_ids, wide_router, cosine, sine)
+    place, key_request, key_ids, wide_router, cosine, sine = lax.optimization_barrier(
+        (place, key_request, key_ids, wide_router, cosine, sine)
     )
 
     columns = w_qkv.shape[1]
@@ -403,7 +447,7 @@
         ],
         in_specs=[VMEM] * (5 + n_head),
         out_specs=[VMEM] * 2,
-        compiler_params=PARAMS,
+        compiler_params=params(36),
         name="project",
     )(
         rank[None, :],
@@ -415,15 +459,16 @@
     )
     prior_kv = lax.ppermute(own_kv, "tok", [(i, i + 1) for i in range(n_tok - 1)])
     pool_rows = kv_cache.shape[0] * n_tok
-    contexts = pl.pallas_call(
+    *contexts, all_routes = pl.pallas_call(
         functools.partial(attend_kernel, n_tok, kv_dev, n_head),
-        out_shape=[jax.ShapeDtypeStruct((tok_dev, kv_dev * QPG * HD), jnp.bfloat16)] * n_head,
+        out_shape=[jax.ShapeDtypeStruct((tok_dev, kv_dev * QPG * HD), jnp.bfloat16)] * n_head
+        + [jax.ShapeDtypeStruct((n_tok * TAIL, tok_dev), jnp.bfloat16)],
         in_specs=[SMEM] * 2 + [VMEM] * 8 + [pl.BlockSpec(memory_space=pl.ANY)] * n_tok,
-        out_specs=[VMEM] * n_head,
+        out_specs=[VMEM] * (n_head + 1),
         scratch_shapes=[pltpu.VMEM((pool_rows, kv_cache.shape[1]), jnp.bfloat16)]
         + [pltpu.VMEM((kv_dev, QPG, row_tokens, LANES), jnp.float32)] * 3
-        + [pltpu.SemaphoreType.DMA],
-        compiler_params=PARAMS,
+        + [pltpu.SemaphoreType.DMA] * 2,
+        compiler_params=params(36),
         name="attend",
     )(
         jnp.stack([row_index, in_first]).astype(jnp.int32),
@@ -444,7 +489,7 @@
         out_shape=[jax.ShapeDtypeStruct(hidden.shape, jnp.bfloat16)] * 3,
         in_specs=[SMEM] + [VMEM] * (3 + n_head),
         out_specs=[VMEM] * 3,
-        compiler_params=PARAMS,
+        compiler_params=params(20),
         name="close",
     )(
         head_index.astype(jnp.int32)[None],
@@ -454,22 +499,28 @@
         *context_slots,
     )
 
-    slots = spread(mixed, "tok")
-    together = min(4, n_tok)
+    walk = [bit for bit in bits_of(n_tok) if bit != swap]
+    slots = spread(mixed, "tok", walk)
+    order = sorted(slots)
+    where = jnp.stack([row_index, row_index ^ swap]).astype(jnp.int32)
+    wide_router, w_gate_up, w_down, *swapped = [
+        pinned(w) for w in (wide_router, w_gate_up, w_down, *swapped)
+    ]
     parts = {}
-    for first in range(0, n_tok, together):
+    for first in range(0, len(order), 2):
         parts.update(
             run_experts(
                 slots,
-                list(range(first, first + together)),
-                row_index,
+                order[first : first + 2],
+                where,
                 all_routes,
                 wide_router,
                 w_gate_up,
                 w_down,
+                swapped,
             )
         )
-    routed_sum = folded(parts, "tok").astype(jnp.float32)
+    routed_sum = folded(parts, "tok", walk[::-1]).astype(jnp.float32)
     layer_out = (mid_states.astype(jnp.float32) + routed_sum).astype(jnp.bfloat16)
     return (attn_sum, layer_out)
 

time: 248 us -> 211 us (0.85)
  blocking collectives: 29.5 us -> 0 us
  local copies, waits for them, and re-layouts: 12.8 us -> 33.3 us
  waiting for transfers between devices: 95.9 us -> 81.4 us
  Pallas kernels: 61.4 us -> 47.5 us
    all_gather x1 -> x0, blocking collectives: 29.5 us -> none  [per_device(): all_routes = lax.all_gather(routes.T, 'tok', axis=0, tiled=True)]
    unnamed x73 -> x57, local copies, waits for them, and re-layouts: 2.93 us -> 21.9 us
    ppermute x47 -> x37, waiting for transfers between devices: 95.9 us -> 81.4 us  [crossed(): return lax.ppermute(array, axis, [(i, i ^ flip) for i in range(count)])]
    pallas_call x4, Pallas kernels: 30.4 us -> 22 us  [run_experts(): pl.pallas_call(functools.partial(expert_kernel, offsets, len(swapped) //...]
    dynamic_slice x0 -> x2, local copies, waits for them, and re-layouts: none -> 3.44 us  [the longest x1 2.08 us: per_device(): down = lax.dynamic_slice_in_dim(w_down, head_index * share, share, 1)]
    pallas_call x1, Pallas kernels: 5.34 us -> 2.66 us  [per_device(): pl.pallas_call(functools.partial(project_kernel, n_head, kv_dev), out_sha...]
    pallas_call x1, Pallas kernels: 4.37 us -> 1.73 us  [per_device(): pl.pallas_call(functools.partial(close_kernel, n_head), out_shape=[jax.Sh...]
    another operation x5 -> x1, local copies, waits for them, and re-layouts: 3.27 us -> 0.74 us  [the longest x4 2.53 us: run_experts(): where = jnp.stack([me] + [me ^ d for d in offsets]).astype(jnp.int32)]
  transfers between devices with their start and end apart: 48 -> 38, of which waited for: 14 -> 12; matrix products, arithmetic and copies ran while one was open for 9% -> 11% of each run, Pallas kernels for 14% -> 23%
where the time goes in v3:
time: 211 us; the launch traced here: 210 us
  waiting for transfers between devices  81.4 us (39%)
  Pallas kernels  47.5 us (23%)
  starting transfers between devices  35.1 us (17%)
  local copies, waits for them, and re-layouts  33.3 us (16%)
  other arithmetic  11.8 us (6%)
    ppermute x37, waiting for transfers between devices, crossed(): return lax.ppermute(array, axis, [(i, i ^ flip) for i in range(count)])  81.4 us
    ppermute x37, starting transfers between devices, crossed(): return lax.ppermute(array, axis, [(i, i ^ flip) for i in range(count)])  33.1 us
    pallas_call x4, Pallas kernels, run_experts(): pl.pallas_call(functools.partial(expert_kernel, offsets, len(swapped) //...  22 us
    unnamed x57, local copies, waits for them, and re-layouts  21.9 us
    pallas_call x1, Pallas kernels, per_device(): pl.pallas_call(functools.partial(attend_kernel, n_tok, kv_dev, n_head), o...  21.1 us
  transfers between devices with their start and end apart: 38, of which 12 were waited for; matrix products, arithmetic and copies ran while one was open for 11% of the time, Pallas kernels for 23%

profile of v3, /device:TPU:0, one launch (start us, length us, event | category | flops | bytes accessed | tf_op | source)
XLA Modules:
  0.0 209.9 jit_solution(4963429715427333508)
XLA Ops:
  2.8 2.6 %collective-permute-start.3 = (bf16[272,512]{1,0:T(8,128)(2,1)S(1)}, bf16[272,512]{1,0:T(8,128)(2,1)}, u32[]{:S(2)}, u32[]{:S(2)}) collective-permute-start(bf16[272,512]{1,0:T(8,128)(2,1)S(1)} %fusion.1.refs_0_), channel_id=1, source_target_pairs={{0,4},{2,6},{4,0},{6,2},{8,12},{10,14},{12,8},{14,10},{16,20},{18,... | collective-permute-start | bytes 835592 | tf_op jit(solution)/shard_map/ppermute | solution.py:32
  7.0 2.6 %collective-permute-start.9 = (bf16[272,512]{1,0:T(8,128)(2,1)S(1)}, bf16[272,512]{1,0:T(8,128)(2,1)}, u32[]{:S(2)}, u32[]{:S(2)}) collective-permute-start(bf16[272,512]{1,0:T(8,128)(2,1)S(1)} %fusion.1.refs_0_), channel_id=1, source_target_pairs={{0,16},{2,18},{4,20},{6,22},{8,24},{10,26},{12,28},{14,30},{16,0},... | collective-permute-start | bytes 835592 | tf_op jit(solution)/shard_map/ppermute | solution.py:32
  29.7 2.0 collective-permute-done.13.refs_12_
  32.8 2.1 %copy-done.3 = bf16[1536,1280]{1,0:T(8,128)(2,1)S(1)} copy-done((bf16[1536,1280]{1,0:T(8,128)(2,1)S(1)}, bf16[1536,1280]{1,0:T(8,128)(2,1)}, u32[]{:S(2)}) %copy-start.3) | copy-done | bytes 3932184
  38.7 2.7 %project.1 = (bf16[4,3,256,128]{3,2,1,0:T(8,128)(2,1)S(1)}, bf16[256,512]{1,0:T(8,128)(2,1)}) custom-call(s32[1,256]{1,0:T(1,128)S(1)} %bitcast.23, f32[1,1536]{1,0:T(1,128)S(1)} %broadcast_in_dim.187.gain_ref, bf16[1536,1280]{1,0:T(8,128)(2,1)S(1)} %copy-done.3, f32[256,128]{1,0:T(8,128)S(1)} %copy-done.16, f32[256,128]{1,0:T(8,128)S(1)} %copy-done.15, ...), custom_call_target="tpu_custom_call" | custom-call | tf_op jit(solution)/shard_map/project/pallas_call | solution.py:442
  48.0 2.1 constant_dynamic-slice_fusion
  64.1 21.1 %attend.1 = (bf16[128,768]{1,0:T(8,128)(2,1)S(1)}, bf16[128,768]{1,0:T(8,128)(2,1)S(1)}, bf16[256,128]{1,0:T(8,128)(2,1)S(1)}) custom-call(s32[2]{0:T(128)S(1)} %pad_add_fusion.2.scalar_ref, s32[256]{0:T(256)S(1)} %copy-done.26, bf16[4,3,256,128]{3,2,1,0:T(8,128)(2,1)S(1)} %copy-done.11, bf16[256,512]{1,0:T(8,128)(2,1)} %collective-permute-done.1.prior_ref, ...), custom_call_target="tpu_custom_call" | custom-call | tf_op jit(solution)/shard_map/attend/pallas_call | solution.py:462
  87.5 5.4 %collective-permute-done.17.refs_1_ = bf16[128,768]{1,0:T(8,128)(2,1)S(1)} collective-permute-done((bf16[128,768]{1,0:T(8,128)(2,1)S(1)}, bf16[128,768]{1,0:T(8,128)(2,1)S(1)}, u32[]{:S(2)}, u32[]{:S(2)}) %collective-permute-start.17) | collective-permute-done | bytes 196640 | tf_op jit(solution)/shard_map/ppermute | solution.py:32
  93.0 2.3 %copy-done.2 = bf16[1536,1536]{1,0:T(8,128)(2,1)S(1)} copy-done((bf16[1536,1536]{1,0:T(8,128)(2,1)S(1)}, bf16[1536,1536]{1,0:T(8,128)(2,1)}, u32[]{:S(2)}) %copy-start.2) | copy-done | bytes 4718616
  97.8 2.7 %collective-permute-start.30 = (bf16[128,1536]{1,0:T(8,128)(2,1)}, bf16[128,1536]{1,0:T(8,128)(2,1)S(1)}, u32[]{:S(2)}, u32[]{:S(2)}) collective-permute-start(bf16[128,1536]{1,0:T(8,128)(2,1)} %get-tuple-element.38.refs_0_), channel_id=1, source_target_pairs={{0,16},{2,18},{4,20},{6,22},{8,24},{10,26},{12,28},{14,30},{16,0},... | collective-permute-start | bytes 1179656 | tf_op jit(solution)/shard_map/ppermute | solution.py:32
  105.5 12.7 %collective-permute-done.30.refs_0_ = bf16[128,1536]{1,0:T(8,128)(2,1)S(1)} collective-permute-done((bf16[128,1536]{1,0:T(8,128)(2,1)}, bf16[128,1536]{1,0:T(8,128)(2,1)S(1)}, u32[]{:S(2)}, u32[]{:S(2)}) %collective-permute-start.30) | collective-permute-done | bytes 393248 | tf_op jit(solution)/shard_map/ppermute | solution.py:32
  119.0 2.0 collective-permute-start.26
  121.0 10.0 %collective-permute-done.33.refs_0_ = bf16[128,1536]{1,0:T(8,128)(2,1)} collective-permute-done((bf16[128,1536]{1,0:T(8,128)(2,1)S(1)}, bf16[128,1536]{1,0:T(8,128)(2,1)}, u32[]{:S(2)}, u32[]{:S(2)}) %collective-permute-start.33) | collective-permute-done | bytes 393248 | tf_op jit(solution)/shard_map/ppermute | solution.py:32
  131.0 7.5 %collective-permute-done.26.refs_0_ = bf16[128,1536]{1,0:T(8,128)(2,1)} collective-permute-done((bf16[128,1536]{1,0:T(8,128)(2,1)}, bf16[128,1536]{1,0:T(8,128)(2,1)}, u32[]{:S(2)}, u32[]{:S(2)}) %collective-permute-start.26) | collective-permute-done | bytes 393248 | tf_op jit(solution)/shard_map/ppermute | solution.py:32
  139.2 13.0 %collective-permute-done.24.refs_11_ = bf16[1,256,1536]{2,1,0:T(8,128)(2,1)} collective-permute-done((bf16[1,256,1536]{2,1,0:T(8,128)(2,1)}, bf16[1,256,1536]{2,1,0:T(8,128)(2,1)}, u32[]{:S(2)}, u32[]{:S(2)}) %collective-permute-start.24) | collective-permute-done | bytes 786464 | tf_op jit(solution)/shard_map/ppermute | solution.py:32
  154.5 5.6 %experts.7 = (bf16[128,1536]{1,0:T(8,128)(2,1)S(1)}, bf16[128,1536]{1,0:T(8,128)(2,1)S(1)}) custom-call(s32[2]{0:T(128)S(1)} %pad_add_fusion.3.where_ref, bf16[128,1536]{1,0:T(8,128)(2,1)} %collective-permute-done.33.refs_0_, bf16[128,1536]{1,0:T(8,128)(2,1)} %collective-permute-done.34.refs_1_, bf16[256,128]{1,0:T(8,128)(2,1)S(1)} %copy-done.9, ...), custom_call_target="tpu_custom_call" | custom-call | tf_op jit(solution)/shard_map/experts/pallas_call | solution.py:343
  160.3 5.4 %experts.6 = (bf16[128,1536]{1,0:T(8,128)(2,1)S(1)}, bf16[128,1536]{1,0:T(8,128)(2,1)S(1)}) custom-call(s32[2]{0:T(128)S(1)} %pad_add_fusion.3.where_ref, bf16[128,1536]{1,0:T(8,128)(2,1)S(1)} %copy-done.22, bf16[128,1536]{1,0:T(8,128)(2,1)S(1)} %collective-permute-done.31.refs_1_, bf16[256,128]{1,0:T(8,128)(2,1)S(1)} %copy-done.9, ...), custom_call_target="tpu_custom_call" | custom-call | tf_op jit(solution)/shard_map/experts/pallas_call | solution.py:343
  166.2 5.5 %experts.5 = (bf16[128,1536]{1,0:T(8,128)(2,1)S(1)}, bf16[128,1536]{1,0:T(8,128)(2,1)S(1)}) custom-call(s32[2]{0:T(128)S(1)} %pad_add_fusion.3.where_ref, bf16[128,1536]{1,0:T(8,128)(2,1)} %collective-permute-done.26.refs_0_, bf16[128,1536]{1,0:T(8,128)(2,1)S(1)} %collective-permute-done.27.refs_1_, bf16[256,128]{1,0:T(8,128)(2,1)S(1)} %copy-done.9, ...), custom_call_target="tpu_custom_call" | custom-call | tf_op jit(solution)/shard_map/experts/pallas_call | solution.py:343
  171.8 5.5 %experts.4 = (bf16[128,1536]{1,0:T(8,128)(2,1)S(1)}, bf16[128,1536]{1,0:T(8,128)(2,1)S(1)}) custom-call(s32[2]{0:T(128)S(1)} %pad_add_fusion.3.where_ref, bf16[128,1536]{1,0:T(8,128)(2,1)} %get-tuple-element.38.refs_0_, bf16[128,1536]{1,0:T(8,128)(2,1)S(1)} %collective-permute-done.18.refs_1_, bf16[256,128]{1,0:T(8,128)(2,1)S(1)} %copy-done.9, ...), custom_call_target="tpu_custom_call" | custom-call | tf_op jit(solution)/shard_map/experts/pallas_call | solution.py:343
  178.1 2.1 collective-permute-start.29
  180.2 9.8 %collective-permute-done.36 = bf16[128,1536]{1,0:T(8,128)(2,1)S(1)} collective-permute-done((bf16[128,1536]{1,0:T(8,128)(2,1)S(1)}, bf16[128,1536]{1,0:T(8,128)(2,1)S(1)}, u32[]{:S(2)}, u32[]{:S(2)}) %collective-permute-start.36) | collective-permute-done | bytes 393248 | tf_op jit(solution)/shard_map/ppermute | solution.py:32
  190.1 2.0 collective-permute-start.37
  192.2 12.3 %collective-permute-done.29 = bf16[128,1536]{1,0:T(8,128)(2,1)S(1)} collective-permute-done((bf16[128,1536]{1,0:T(8,128)(2,1)S(1)}, bf16[128,1536]{1,0:T(8,128)(2,1)S(1)}, u32[]{:S(2)}, u32[]{:S(2)}) %collective-permute-start.29) | collective-permute-done | bytes 393248 | tf_op jit(solution)/shard_map/ppermute | solution.py:32
  204.5 4.4 %collective-permute-done.37 = bf16[128,1536]{1,0:T(8,128)(2,1)S(1)} collective-permute-done((bf16[128,1536]{1,0:T(8,128)(2,1)S(1)}, bf16[128,1536]{1,0:T(8,128)(2,1)S(1)}, u32[]{:S(2)}, u32[]{:S(2)}) %collective-permute-start.37) | collective-permute-done | bytes 393248 | tf_op jit(solution)/shard_map/ppermute | solution.py:32
  (158 shorter events, 65.5 us)
Async XLA Ops:
  2.3 17.8 %collective-permute-start.2 = (bf16[272,512]{1,0:T(8,128)(2,1)S(1)}, bf16[272,512]{1,0:T(8,128)(2,1)S(1)}, u32[]{:S(2)}, u32[]{:S(2)}) collective-permute-start(bf16[272,512]{1,0:T(8,128)(2,1)S(1)} %fusion.1.refs_0_), channel_id=1, source_target_pairs={{0,2},{2,0},{4,6},{6,4},{8,10},{10,8},{12,14},{14,12},{16,18},{18,... | collective-permute-start | bytes 835592 | tf_op jit(solution)/shard_map/ppermute | solution.py:32
  2.8 20.1 %collective-permute-start.3 = (bf16[272,512]{1,0:T(8,128)(2,1)S(1)}, bf16[272,512]{1,0:T(8,128)(2,1)}, u32[]{:S(2)}, u32[]{:S(2)}) collective-permute-start(bf16[272,512]{1,0:T(8,128)(2,1)S(1)} %fusion.1.refs_0_), channel_id=1, source_target_pairs={{0,4},{2,6},{4,0},{6,2},{8,12},{10,14},{12,8},{14,10},{16,20},{18,... | collective-permute-start | bytes 835592 | tf_op jit(solution)/shard_map/ppermute | solution.py:32
  7.0 15.5 %collective-permute-start.9 = (bf16[272,512]{1,0:T(8,128)(2,1)S(1)}, bf16[272,512]{1,0:T(8,128)(2,1)}, u32[]{:S(2)}, u32[]{:S(2)}) collective-permute-start(bf16[272,512]{1,0:T(8,128)(2,1)S(1)} %fusion.1.refs_0_), channel_id=1, source_target_pairs={{0,16},{2,18},{4,20},{6,22},{8,24},{10,26},{12,28},{14,30},{16,0},... | collective-permute-start | bytes 835592 | tf_op jit(solution)/shard_map/ppermute | solution.py:32
  20.1 22.2 %collective-permute-start.6 = (bf16[272,512]{1,0:T(8,128)(2,1)}, bf16[272,512]{1,0:T(8,128)(2,1)}, u32[]{:S(2)}, u32[]{:S(2)}) collective-permute-start(bf16[272,512]{1,0:T(8,128)(2,1)} %collective-permute-done.5.refs_4_), channel_id=1, source_target_pairs={{0,2},{2,0},{4,6},{6,4},{8,10},{10,8},{12,14},{14,12},{16,18},{18,... | collective-permute-start | bytes 835592 | tf_op jit(solution)/shard_map/ppermute | solution.py:32
  20.8 23.4 %collective-permute-start.7 = (bf16[272,512]{1,0:T(8,128)(2,1)}, bf16[272,512]{1,0:T(8,128)(2,1)}, u32[]{:S(2)}, u32[]{:S(2)}) collective-permute-start(bf16[272,512]{1,0:T(8,128)(2,1)} %collective-permute-done.5.refs_4_), channel_id=1, source_target_pairs={{0,4},{2,6},{4,0},{6,2},{8,12},{10,14},{12,8},{14,10},{16,20},{18,... | collective-permute-start | bytes 835592 | tf_op jit(solution)/shard_map/ppermute | solution.py:32
  22.4 23.6 %collective-permute-start.11 = (bf16[272,512]{1,0:T(8,128)(2,1)}, bf16[272,512]{1,0:T(8,128)(2,1)}, u32[]{:S(2)}, u32[]{:S(2)}) collective-permute-start(bf16[272,512]{1,0:T(8,128)(2,1)} %collective-permute-done.9.refs_8_), channel_id=1, source_target_pairs={{0,4},{2,6},{4,0},{6,2},{8,12},{10,14},{12,8},{14,10},{16,20},{18,... | collective-permute-start | bytes 835592 | tf_op jit(solution)/shard_map/ppermute | solution.py:32
  29.2 18.3 %collective-permute-start.10 = (bf16[272,512]{1,0:T(8,128)(2,1)}, bf16[272,512]{1,0:T(8,128)(2,1)}, u32[]{:S(2)}, u32[]{:S(2)}) collective-permute-start(bf16[272,512]{1,0:T(8,128)(2,1)} %collective-permute-done.9.refs_8_), channel_id=1, source_target_pairs={{0,2},{2,0},{4,6},{6,4},{8,10},{10,8},{12,14},{14,12},{16,18},{18,... | collective-permute-start | bytes 835592 | tf_op jit(solution)/shard_map/ppermute | solution.py:32
  31.7 16.2 %collective-permute-start.15 = (bf16[272,512]{1,0:T(8,128)(2,1)}, bf16[272,512]{1,0:T(8,128)(2,1)}, u32[]{:S(2)}, u32[]{:S(2)}) collective-permute-start(bf16[272,512]{1,0:T(8,128)(2,1)} %collective-permute-done.13.refs_12_), channel_id=1, source_target_pairs={{0,4},{2,6},{4,0},{6,2},{8,12},{10,14},{12,8},{14,10},{16,20},{18,... | collective-permute-start | bytes 835592 | tf_op jit(solution)/shard_map/ppermute | solution.py:32
  50.1 50.4 %collective-permute-start.19 = (bf16[1,1536,256]{2,1,0:T(8,128)(2,1)}, bf16[1,1536,256]{2,1,0:T(8,128)(2,1)}, u32[]{:S(2)}, u32[]{:S(2)}) collective-permute-start(bf16[1,1536,256]{2,1,0:T(8,128)(2,1)} %get-tuple-element.41), channel_id=1, source_target_pairs={{0,4},{2,6},{4,0},{6,2},{8,12},{10,14},{12,8},{14,10},{16,20},{18,... | collective-permute-start | bytes 2359304 | tf_op jit(solution)/shard_map/ppermute | solution.py:32
  51.9 50.1 %collective-permute-start.20 = (bf16[1,1536,256]{2,1,0:T(8,128)(2,1)}, bf16[1,1536,256]{2,1,0:T(8,128)(2,1)}, u32[]{:S(2)}, u32[]{:S(2)}) collective-permute-start(bf16[1,1536,256]{2,1,0:T(8,128)(2,1)} %get-tuple-element.42), channel_id=1, source_target_pairs={{0,4},{2,6},{4,0},{6,2},{8,12},{10,14},{12,8},{14,10},{16,20},{18,... | collective-permute-start | bytes 2359304 | tf_op jit(solution)/shard_map/ppermute | solution.py:32
  52.1 51.9 %collective-permute-start.21 = (bf16[1,256,1536]{2,1,0:T(8,128)(2,1)}, bf16[1,256,1536]{2,1,0:T(8,128)(2,1)}, u32[]{:S(2)}, u32[]{:S(2)}) collective-permute-start(bf16[1,256,1536]{2,1,0:T(8,128)(2,1)} %constant_dynamic-slice_fusion), channel_id=1, source_target_pairs={{0,4},{2,6},{4,0},{6,2},{8,12},{10,14},{12,8},{14,10},{16,20},{18,... | collective-permute-start | bytes 2359304 | tf_op jit(solution)/shard_map/ppermute | solution.py:32
  97.8 20.4 %collective-permute-start.30 = (bf16[128,1536]{1,0:T(8,128)(2,1)}, bf16[128,1536]{1,0:T(8,128)(2,1)S(1)}, u32[]{:S(2)}, u32[]{:S(2)}) collective-permute-start(bf16[128,1536]{1,0:T(8,128)(2,1)} %get-tuple-element.38.refs_0_), channel_id=1, source_target_pairs={{0,16},{2,18},{4,20},{6,22},{8,24},{10,26},{12,28},{14,30},{16,0},... | collective-permute-start | bytes 1179656 | tf_op jit(solution)/shard_map/ppermute | solution.py:32
  100.5 38.2 %collective-permute-start.22 = (bf16[1,1536,256]{2,1,0:T(8,128)(2,1)}, bf16[1,1536,256]{2,1,0:T(8,128)(2,1)}, u32[]{:S(2)}, u32[]{:S(2)}) collective-permute-start(bf16[1,1536,256]{2,1,0:T(8,128)(2,1)} %collective-permute-done.19.refs_6_), channel_id=1, source_target_pairs={{0,1},{1,0},{2,3},{3,2},{4,5},{5,4},{6,7},{7,6},{8,9},{9,8},{10,11... | collective-permute-start | bytes 2359304 | tf_op jit(solution)/shard_map/ppermute | solution.py:32
  102.0 37.2 %collective-permute-start.23 = (bf16[1,1536,256]{2,1,0:T(8,128)(2,1)}, bf16[1,1536,256]{2,1,0:T(8,128)(2,1)}, u32[]{:S(2)}, u32[]{:S(2)}) collective-permute-start(bf16[1,1536,256]{2,1,0:T(8,128)(2,1)} %collective-permute-done.20.refs_7_), channel_id=1, source_target_pairs={{0,1},{1,0},{2,3},{3,2},{4,5},{5,4},{6,7},{7,6},{8,9},{9,8},{10,11... | collective-permute-start | bytes 2359304 | tf_op jit(solution)/shard_map/ppermute | solution.py:32
  104.0 48.3 %collective-permute-start.24 = (bf16[1,256,1536]{2,1,0:T(8,128)(2,1)}, bf16[1,256,1536]{2,1,0:T(8,128)(2,1)}, u32[]{:S(2)}, u32[]{:S(2)}) collective-permute-start(bf16[1,256,1536]{2,1,0:T(8,128)(2,1)} %collective-permute-done.21.refs_8_), channel_id=1, source_target_pairs={{0,1},{1,0},{2,3},{3,2},{4,5},{5,4},{6,7},{7,6},{8,9},{9,8},{10,11... | collective-permute-start | bytes 2359304 | tf_op jit(solution)/shard_map/ppermute | solution.py:32
  119.0 19.6 %collective-permute-start.26 = (bf16[128,1536]{1,0:T(8,128)(2,1)}, bf16[128,1536]{1,0:T(8,128)(2,1)}, u32[]{:S(2)}, u32[]{:S(2)}) collective-permute-start(bf16[128,1536]{1,0:T(8,128)(2,1)} %get-tuple-element.38.refs_0_), channel_id=1, source_target_pairs={{0,8},{2,10},{4,12},{6,14},{8,0},{10,2},{12,4},{14,6},{16,24},{18,... | collective-permute-start | bytes 1179656 | tf_op jit(solution)/shard_map/ppermute | solution.py:32
  131.0 21.2 %collective-permute-start.34 = (bf16[128,1536]{1,0:T(8,128)(2,1)}, bf16[128,1536]{1,0:T(8,128)(2,1)}, u32[]{:S(2)}, u32[]{:S(2)}) collective-permute-start(bf16[128,1536]{1,0:T(8,128)(2,1)} %collective-permute-done.33.refs_0_), channel_id=1, source_target_pairs={{0,2},{2,0},{4,6},{6,4},{8,10},{10,8},{12,14},{14,12},{16,18},{18,... | collective-permute-start | bytes 1179656 | tf_op jit(solution)/shard_map/ppermute | solution.py:32
  138.6 21.7 %collective-permute-start.31 = (bf16[128,1536]{1,0:T(8,128)(2,1)}, bf16[128,1536]{1,0:T(8,128)(2,1)S(1)}, u32[]{:S(2)}, u32[]{:S(2)}) collective-permute-start(bf16[128,1536]{1,0:T(8,128)(2,1)} %copy-done.21), channel_id=1, source_target_pairs={{0,2},{2,0},{4,6},{6,4},{8,10},{10,8},{12,14},{14,12},{16,18},{18,... | collective-permute-start | bytes 1179656 | tf_op jit(solution)/shard_map/ppermute | solution.py:32
  138.6 27.6 %collective-permute-start.27 = (bf16[128,1536]{1,0:T(8,128)(2,1)}, bf16[128,1536]{1,0:T(8,128)(2,1)S(1)}, u32[]{:S(2)}, u32[]{:S(2)}) collective-permute-start(bf16[128,1536]{1,0:T(8,128)(2,1)} %collective-permute-done.26.refs_0_), channel_id=1, source_target_pairs={{0,2},{2,0},{4,6},{6,4},{8,10},{10,8},{12,14},{14,12},{16,18},{18,... | collective-permute-start | bytes 1179656 | tf_op jit(solution)/shard_map/ppermute | solution.py:32
  139.2 32.7 %collective-permute-start.18 = (bf16[128,1536]{1,0:T(8,128)(2,1)}, bf16[128,1536]{1,0:T(8,128)(2,1)S(1)}, u32[]{:S(2)}, u32[]{:S(2)}) collective-permute-start(bf16[128,1536]{1,0:T(8,128)(2,1)} %get-tuple-element.38.refs_0_), channel_id=1, source_target_pairs={{0,2},{2,0},{4,6},{6,4},{8,10},{10,8},{12,14},{14,12},{16,18},{18,... | collective-permute-start | bytes 1179656 | tf_op jit(solution)/shard_map/ppermute | solution.py:32
  160.2 17.7 %collective-permute-start.35 = (bf16[128,1536]{1,0:T(8,128)(2,1)S(1)}, bf16[128,1536]{1,0:T(8,128)(2,1)S(1)}, u32[]{:S(2)}, u32[]{:S(2)}) collective-permute-start(bf16[128,1536]{1,0:T(8,128)(2,1)S(1)} %get-tuple-element.51), channel_id=1, source_target_pairs={{0,2},{2,0},{4,6},{6,4},{8,10},{10,8},{12,14},{14,12},{16,18},{18,... | collective-permute-start | bytes 1179656 | tf_op jit(solution)/shard_map/ppermute | solution.py:32
  177.3 14.9 %collective-permute-start.25 = (bf16[128,1536]{1,0:T(8,128)(2,1)S(1)}, bf16[128,1536]{1,0:T(8,128)(2,1)S(1)}, u32[]{:S(2)}, u32[]{:S(2)}) collective-permute-start(bf16[128,1536]{1,0:T(8,128)(2,1)S(1)} %get-tuple-element.45), channel_id=1, source_target_pairs={{0,2},{2,0},{4,6},{6,4},{8,10},{10,8},{12,14},{14,12},{16,18},{18,... | collective-permute-start | bytes 1179656 | tf_op jit(solution)/shard_map/ppermute | solution.py:32
  178.1 26.3 %collective-permute-start.29 = (bf16[128,1536]{1,0:T(8,128)(2,1)S(1)}, bf16[128,1536]{1,0:T(8,128)(2,1)S(1)}, u32[]{:S(2)}, u32[]{:S(2)}) collective-permute-start(bf16[128,1536]{1,0:T(8,128)(2,1)S(1)} %add_convert_fusion.3), channel_id=1, source_target_pairs={{0,8},{2,10},{4,12},{6,14},{8,0},{10,2},{12,4},{14,6},{16,24},{18,... | collective-permute-start | bytes 1179656 | tf_op jit(solution)/shard_map/ppermute | solution.py:32
  190.1 18.7 %collective-permute-start.37 = (bf16[128,1536]{1,0:T(8,128)(2,1)S(1)}, bf16[128,1536]{1,0:T(8,128)(2,1)S(1)}, u32[]{:S(2)}, u32[]{:S(2)}) collective-permute-start(bf16[128,1536]{1,0:T(8,128)(2,1)S(1)} %add_convert_fusion.1), channel_id=1, source_target_pairs={{0,16},{2,18},{4,20},{6,22},{8,24},{10,26},{12,28},{14,30},{16,0},... | collective-permute-start | bytes 1179656 | tf_op jit(solution)/shard_map/ppermute | solution.py:32
  (42 other events, 323.5 us)

commit v4 on v3

v4 whole, which is shorter than its diff:
```python
import functools

import jax
import jax.numpy as jnp
import numpy as np
from jax import lax
from jax.experimental import pallas as pl
from jax.experimental.pallas import tpu as pltpu
from jax.sharding import PartitionSpec as P

D = 1536
HEADS = 24
KVH = 8
HD = 64
FFE = 512
TOPK = 8
PREFIX = 2048
GROUPS = 2
PAGE = 16
QPG = HEADS // KVH
BLOCK = 64


EPSILON = 1e-06
ROPE_BASE = 10000.0
MASKED = -1e30

LANES = 128


def crossed(array, axis, flip):
    count = lax.axis_size(axis)
    return lax.ppermute(array, axis, [(i, i ^ flip) for i in range(count)])


def spread(own, axis, bits):
    slots = {0: own}
    for bit in bits:
        for d in sorted(slots):
            slots[d | bit] = crossed(slots[d], axis, bit)
    return slots


def spread_by_stages(own, axis, bits, also):
    slots = {0: own}
    for stage in range(1, len(bits) + 1):
        coming = {}
        for d in slots:
            low = [bit for bit in bits if bit & d]
            for bit in bits[bits.index(low[-1]) + 1 if low else 0 :]:
                if bin(d).count("1") == stage - 1:
                    coming[d | bit] = crossed(slots[d], axis, bit)
        names = sorted(coming)
        came = lax.optimization_barrier([coming[d] for d in names] + (also if stage == 1 else []))
        slots.update(zip(names, came))
        also = came[len(names) :] if stage == 1 else also
    return slots, also


def folded(parts, axis, bits):
    parts = dict(parts)
    for bit in bits:
        for d in sorted(parts, reverse=True):
            if d & bit:
                came = crossed(parts.pop(d).astype(jnp.bfloat16), axis, bit)
                parts[d ^ bit] = parts[d ^ bit].astype(jnp.float32) + came.astype(jnp.float32)
    return parts[0]


def bits_of(count):
    return [1 << i for i in reversed(range(count.bit_length() - 1))]


VMEM = pl.BlockSpec(memory_space=pltpu.VMEM)
SMEM = pl.BlockSpec(memory_space=pltpu.SMEM)
TAIL = 16
ATT = 16


def params(mib):
    return pltpu.CompilerParams(vmem_limit_bytes=mib << 20)


def spent(flops):
    return pl.CostEstimate(flops=flops, transcendentals=0, bytes_accessed=0)


def pinned(array):
    return pltpu.with_memory_space_constraint(array, pltpu.VMEM)


def project_kernel(
    slots,
    kv_dev,
    where_ref,
    requests_ref,
    mask_ref,
    frequency_ref,
    gain_ref,
    weight_ref,
    *refs,
):
    state_refs = refs[:slots]
    query_ref, kv_ref, column_ref, row_ref, first_ref = refs[slots:]
    row_index, head_index = where_ref[0], where_ref[1]
    piece = state_refs[0].shape[0]
    rows = piece * slots
    real = jnp.float32
    rounded = jnp.bfloat16

    table = requests_ref[...]
    turned_table = jnp.transpose(table)
    width = table.shape[1]
    across = lax.broadcasted_iota(jnp.int32, (width, width), 1)
    along = lax.broadcasted_iota(jnp.int32, (width, width), 0)
    ends = jnp.sum(jnp.where(along <= across, turned_table[:, 0:1], 0.0), axis=0, keepdims=True)
    ends_up = jnp.sum(jnp.where(across <= along, table[0:1], 0.0), axis=1, keepdims=True)
    starts, starts_up = ends - table[0:1], ends_up - turned_table[:, 0:1]

    def offsets(shape, axis):
        place = lax.broadcasted_iota(jnp.int32, shape, axis)
        shift = jnp.zeros(shape, jnp.int32)
        for k in range(slots):
            shift = jnp.where(place // piece == k, ((head_index ^ k) - k) * piece, shift)
        return place + shift

    local, local_up = offsets((1, rows), 1), offsets((rows, 1), 0)
    across = lax.broadcasted_iota(jnp.int32, (rows, rows), 1).astype(real)
    along = lax.broadcasted_iota(jnp.int32, (rows, rows), 0).astype(real)
    lane = lax.broadcasted_iota(jnp.int32, (rows, LANES), 1)

    def tables(behind):
        first = (row_index - behind) * rows
        ids, ids_up = (local + first).astype(real), (local_up + first).astype(real)
        holds = (starts_up <= ids) & (ids < ends_up)
        holds_up = (starts <= ids_up) & (ids_up < ends)
        number = lax.broadcasted_iota(jnp.int32, (width, 1), 0).astype(real)
        request = jnp.sum(jnp.where(holds, number, 0.0), axis=0, keepdims=True)
        start = jnp.sum(jnp.where(holds, starts_up, 0.0), axis=0, keepdims=True)
        group = jnp.sum(jnp.where(holds, turned_table[:, 1:2], 0.0), axis=0, keepdims=True)
        group_up = jnp.sum(jnp.where(holds_up, table[1:2], 0.0), axis=1, keepdims=True)
        key = group * (2.0 * rows) + lax.broadcasted_iota(jnp.int32, (1, rows), 1).astype(real)
        key_up = group_up * (2.0 * rows) + lax.broadcasted_iota(jnp.int32, (rows, 1), 0).astype(real)
        rank = jnp.sum(jnp.where(key_up < key, 1.0, 0.0), axis=0, keepdims=True)
        rank_up = jnp.sum(jnp.where(key < key_up, 1.0, 0.0), axis=1, keepdims=True)
        place = rank == along

        def arranged(values):
            return jnp.sum(jnp.where(place, values, 0.0), axis=1, keepdims=True)

        marks = []
        for k in range(slots):
            block = (row_index - behind) * slots + (head_index ^ k)
            mark = mask_ref[pl.ds(jnp.maximum(block, 0), 1), :]
            marks.append(jnp.where(block >= 0, mark, 0))
        mark = jnp.concatenate(marks, axis=1)
        open_request = arranged(jnp.where(mark == 1, request, -1.0))
        ids = arranged(ids)
        columns = jnp.where(lane == 0, open_request, jnp.where(lane == 1, ids, 0.0))
        return columns, ids, arranged(request), arranged(start), place, rank_up, group

    before = tables(1)[0]
    columns, ids, request, start, place, rank_up, group = tables(0)
    columns = jnp.where(lane == 2, request, jnp.where(lane == 3, rank_up, columns))
    column_ref[...] = columns
    row_ref[:, :rows] = jnp.transpose(before)[:8]
    row_ref[:, rows:] = jnp.transpose(columns)[:8]
    first_ref[0] = jnp.sum(jnp.where(group == 0.0, 1.0, 0.0)).astype(jnp.int32)
    angles = (PREFIX + ids - start) * frequency_ref[...]
    cosine = jnp.cos(angles)
    sine = jnp.where(lane % HD < HD // 2, -1.0, 1.0) * jnp.sin(angles)

    states = jnp.concatenate([ref[...] for ref in state_refs], axis=0).astype(real)
    scale = lax.rsqrt(jnp.mean(states * states, axis=-1, keepdims=True) + EPSILON)
    normed = (states * scale * gain_ref[...]).astype(rounded)
    chosen = jnp.where(place, 1.0, 0.0).astype(rounded)
    normed = jnp.dot(chosen, normed, preferred_element_type=real).astype(rounded)
    projected = jnp.dot(normed, weight_ref[...], preferred_element_type=real)
    low = lane < HD
    first = lane % HD < HD // 2

    def tile(number):
        return projected[:, number * LANES : (number + 1) * LANES]

    @functools.cache
    def turned(number):
        plain = tile(number)
        partner = jnp.where(
            first, pltpu.roll(plain, LANES - HD // 2, 1), pltpu.roll(plain, HD // 2, 1)
        )
        return plain * cosine + partner * sine

    for j in range(kv_dev):
        unit = j * (QPG + 2)
        for i in range(QPG):
            query = turned((unit + i) // 2)
            if (unit + i) % 2:
                query = pltpu.roll(query, HD, 1)
            query_ref[j, i] = jnp.where(low, query * HD ** (-0.5), 0.0).astype(rounded)
        key, value = turned((unit + QPG) // 2), tile((unit + QPG + 1) // 2)
        if (unit + QPG) % 2:
            key, value = pltpu.roll(key, HD, 1), pltpu.roll(value, HD, 1)
        kv_ref[:, j * LANES : (j + 1) * LANES] = jnp.where(low, key, value).astype(rounded)


def scored(queries, keys):
    return lax.dot_general(
        queries, keys, (((1,), (1,)), ((), ())), preferred_element_type=jnp.float32
    )


def attend_kernel(
    shards,
    heads_at,
    slots,
    scalar_ref,
    first_ref,
    place_ref,
    query_ref,
    prior_ref,
    own_ref,
    column_ref,
    row_ref,
    *refs,
):
    shard_refs = refs[:shards]
    out_refs = refs[shards : shards + slots]
    routes_ref, pool_ref, peak_ref, total_ref, sum_ref, arrived, told = refs[shards + slots :]
    me = scalar_ref[0]
    in_first = first_ref[0]
    first_head, kv_dev = heads_at
    mine = slice(first_head * LANES, (first_head + kv_dev) * LANES)
    rows = query_ref.shape[2]
    blocks = rows // BLOCK
    shard_rows = shard_refs[0].shape[0] - TAIL
    shard_pages = shard_rows // PAGE

    for d in range(shards):
        def start(j, carry, d=d):
            page = (me ^ d) * shard_pages + j
            pltpu.make_async_copy(
                shard_refs[d].at[pl.ds(pl.multiple_of(j * PAGE, PAGE), PAGE), mine],
                pool_ref.at[pl.ds(pl.multiple_of(place_ref[page] * PAGE, PAGE), PAGE), :],
                arrived,
            ).start()
            return carry

        lax.fori_loop(0, shard_pages, start, 0, unroll=True)
        pltpu.make_async_copy(
            shard_refs[d].at[shard_rows : shard_rows + TAIL, : routes_ref.shape[1]],
            routes_ref.at[d * TAIL : (d + 1) * TAIL, :],
            told,
        ).start()

    def near(b, carry):
        at = pl.ds(pl.multiple_of(b * BLOCK, BLOCK), BLOCK)
        column = column_ref[at, :]
        row = row_ref[...]
        allowed = (row[0:1] == column[:, 2:3]) & (row[1:2] <= column[:, 1:2])
        allowed = jnp.concatenate([allowed.astype(jnp.float32)] * QPG, axis=0) > 0.0
        for j in range(kv_dev):
            queries = query_ref[first_head + j, :, at, :].reshape(QPG * BLOCK, LANES)
            columns = slice((first_head + j) * LANES, (first_head + j + 1) * LANES)
            keys = jnp.concatenate([prior_ref[:, columns], own_ref[:, columns]], axis=0)
            scores = jnp.where(allowed, scored(queries, keys), MASKED)
            peak = jnp.max(scores, axis=-1, keepdims=True)
            weights = jnp.where(allowed, jnp.exp(scores - peak), 0.0)
            total = jnp.sum(weights, axis=-1, keepdims=True)
            mixed = jnp.dot(
                weights.astype(jnp.bfloat16), keys, preferred_element_type=jnp.float32
            )
            shape = (QPG, BLOCK, LANES)
            peak_ref[j, :, at, :] = jnp.broadcast_to(peak, mixed.shape).reshape(shape)
            total_ref[j, :, at, :] = jnp.broadcast_to(total, mixed.shape).reshape(shape)
            sum_ref[j, :, at, :] = mixed.reshape(shape)
        return carry

    lax.fori_loop(0, blocks, near, 0)
    pltpu.make_async_copy(pool_ref, pool_ref, arrived).wait()
    pltpu.make_async_copy(routes_ref, routes_ref, told).wait()

    group_rows = pool_ref.shape[0] // GROUPS
    full = (in_first + BLOCK - 1) // BLOCK
    skip = in_first // BLOCK

    def far(item, carry):
        group = (item >= full).astype(jnp.int32)
        b = jnp.where(item < full, item, item - full + skip)
        at = pl.ds(pl.multiple_of(b * BLOCK, BLOCK), BLOCK)
        keys_at = pl.ds(pl.multiple_of(group * group_rows, group_rows), group_rows)
        line = lax.broadcasted_iota(jnp.int32, (QPG, BLOCK, LANES), 1) + b * BLOCK
        chosen = (line >= in_first) == (group == 1)
        shape = (QPG, BLOCK, LANES)
        for j in range(kv_dev):
            queries = query_ref[first_head + j, :, at, :].reshape(QPG * BLOCK, LANES)
            keys = pool_ref[keys_at, j * LANES : (j + 1) * LANES]
            scores = scored(queries, keys)
            here = jnp.max(scores, axis=-1, keepdims=True)
            weights = jnp.exp(scores - here)
            total = jnp.sum(weights, axis=-1, keepdims=True)
            mixed = jnp.dot(
                weights.astype(jnp.bfloat16), keys, preferred_element_type=jnp.float32
            ).reshape(shape)
            here = jnp.broadcast_to(here, (QPG * BLOCK, LANES)).reshape(shape)
            total = jnp.broadcast_to(total, (QPG * BLOCK, LANES)).reshape(shape)
            before = peak_ref[j, :, at, :]
            peak = jnp.maximum(before, here)
            keep, gain = jnp.exp(before - peak), jnp.exp(here - peak)
            joint_total = total_ref[j, :, at, :] * keep + total * gain
            joint_sum = sum_ref[j, :, at, :] * keep + mixed * gain
            total_ref[j, :, at, :] = jnp.where(chosen, joint_total, total_ref[j, :, at, :])
            sum_ref[j, :, at, :] = jnp.where(chosen, joint_sum, sum_ref[j, :, at, :])
        return carry

    lax.fori_loop(0, full + blocks - skip, far, 0)

    place = lax.broadcasted_iota(jnp.int32, (rows, rows), 1).astype(jnp.float32)
    back = jnp.where(column_ref[...][:, 3:4] == place, 1.0, 0.0).astype(jnp.bfloat16)
    lane = lax.broadcasted_iota(jnp.int32, (rows, LANES), 1)
    piece = rows // slots
    heads = [
        sum_ref[j, i] / total_ref[j, i] for j in range(kv_dev) for i in range(QPG)
    ]
    for h in range(0, len(heads), 2):
        pair = pltpu.roll(heads[h], HD, 1)
        if h + 1 < len(heads):
            pair = jnp.where(lane < HD, pair, heads[h + 1])
        pair = jnp.dot(
            back, pair.astype(jnp.bfloat16), preferred_element_type=jnp.float32
        ).astype(jnp.bfloat16)
        width = min(LANES, len(heads) * HD - h * HD)
        for k in range(slots):
            out_refs[k][:, h * HD : h * HD + width] = pair[k * piece : (k + 1) * piece, :width]


def close_kernel(slots, scalar_ref, hidden_ref, weight_ref, gain_ref, *refs):
    branch_ref, mid_ref, mixed_ref = refs[-3:]
    context_refs = refs[:-3]
    pieces = len(context_refs) // slots
    head_width = sum(ref.shape[1] for ref in context_refs[:pieces])
    total = None
    for k in range(slots):
        first = (scalar_ref[1] ^ k) * head_width
        for ref in context_refs[k * pieces : (k + 1) * pieces]:
            width = ref.shape[1]
            part = jnp.dot(
                ref[...],
                weight_ref[pl.ds(pl.multiple_of(first, HD), width), :],
                preferred_element_type=jnp.float32,
            )
            first = first + width
            total = part if total is None else total + part
    branch = total.astype(jnp.bfloat16)
    branch_ref[...] = branch
    mid = (hidden_ref[...].astype(jnp.float32) + branch.astype(jnp.float32)).astype(jnp.bfloat16)
    mid_ref[...] = mid
    wide = mid.astype(jnp.float32)
    scale = lax.rsqrt(jnp.mean(wide * wide, axis=-1, keepdims=True) + EPSILON)
    mixed_ref[...] = (wide * scale * gain_ref[...]).astype(jnp.bfloat16)


def expert_kernel(offsets, swap, parts, where_ref, *refs):
    count = len(offsets)
    state_refs = refs[:count]
    routes_ref, router_ref, up_ref, down_ref = refs[count : count + 4]
    swapped = refs[count + 4 : count + 4 + 2 * parts]
    other_ref = refs[count + 4 + 2 * parts]
    out_refs = refs[count + 5 + 2 * parts :]
    rows = state_refs[0].shape[0]
    lanes = router_ref.shape[0]
    experts_here = up_ref.shape[0]
    states = jnp.concatenate([ref[...] for ref in state_refs], axis=0)
    lane = lax.broadcasted_iota(jnp.int32, (rows, lanes), 1)
    hits = []
    for d in offsets:
        routes = routes_ref[d * TAIL : (d + 1) * TAIL, :].astype(jnp.float32)
        routes = jnp.transpose(routes).astype(jnp.int32)
        hit = jnp.zeros((rows, lanes), jnp.float32)
        for k in range(TOPK):
            hit = jnp.where(lane == routes[:, k : k + 1], 1.0, hit)
        hits.append(hit)
    hit = jnp.concatenate(hits, axis=0) > 0.0
    logits = scored(states, router_ref[...])
    logits = jnp.where(hit, logits, MASKED)
    peak = jnp.max(logits, axis=-1, keepdims=True)
    shares = jnp.where(hit, jnp.exp(logits - peak), 0.0)
    shares = shares / jnp.sum(shares, axis=-1, keepdims=True)
    lane = lax.broadcasted_iota(jnp.int32, shares.shape, 1)

    def gate_of(expert):
        return jnp.sum(jnp.where(lane == expert, shares, 0.0), axis=-1, keepdims=True)

    def through(lead, rest, down):
        activated = (lead / (1.0 + jnp.exp(-lead)) * rest).astype(jnp.bfloat16)
        return jnp.dot(activated, down, preferred_element_type=jnp.float32)

    result = None
    for x in range(experts_here):
        joined = jnp.dot(states, up_ref[x], preferred_element_type=jnp.float32)
        part = through(joined[:, :FFE], joined[:, FFE:], down_ref[x])
        part = gate_of(where_ref[0] * experts_here + x) * part
        result = part if result is None else result + part
    for x in range(experts_here):
        total = None
        for k in range(parts):
            lead_ref, rest_ref = swapped[2 * k : 2 * k + 2]
            share = lead_ref.shape[2]
            first = pl.multiple_of((where_ref[1] ^ k) * share, share)
            lead = jnp.dot(states, lead_ref[x], preferred_element_type=jnp.float32)
            rest = jnp.dot(states, rest_ref[x], preferred_element_type=jnp.float32)
            part = through(lead, rest, other_ref[x, pl.ds(first, share), :])
            total = part if total is None else total + part
        result = result + gate_of((where_ref[0] ^ swap) * experts_here + x) * total
    for i in range(count):
        out_refs[i][...] = result[i * rows : (i + 1) * rows].astype(jnp.bfloat16)


def run_experts(slots, offsets, where, swap, routes, router, w_gate_up, w_down, swapped):
    count = len(offsets)
    outs = pl.pallas_call(
        functools.partial(expert_kernel, offsets, swap, len(swapped) // 2),
        out_shape=[jax.ShapeDtypeStruct(slots[d].shape, jnp.bfloat16) for d in offsets],
        in_specs=[SMEM] + [VMEM] * (count + 4 + len(swapped)),
        out_specs=[VMEM] * count,
        compiler_params=params(28),
        cost_estimate=spent(count * 128 * D * FFE * 6 * 4),
        name="experts",
    )(where, *[slots[d] for d in offsets], routes, router, w_gate_up, w_down, *swapped)
    return dict(zip(offsets, outs))


def share_kernel(where_ref, up_ref, lead_ref, rest_ref, done):
    share = lead_ref.shape[2]
    at = pl.multiple_of(where_ref[1] * share, share)
    copies = [
        pltpu.make_async_copy(up_ref.at[:, :, pl.ds(at, share)], lead_ref, done.at[0]),
        pltpu.make_async_copy(up_ref.at[:, :, pl.ds(FFE + at, share)], rest_ref, done.at[1]),
    ]
    for copy in copies:
        copy.start()
    for copy in copies:
        copy.wait()


def shares_of(place_here, n_head, w_gate_up):
    share = FFE // n_head
    if share % LANES:
        first = place_here[1] * share
        return (
            lax.dynamic_slice_in_dim(w_gate_up, first, share, 2),
            lax.dynamic_slice_in_dim(w_gate_up, FFE + first, share, 2),
        )
    whole = pl.BlockSpec(memory_space=pltpu.HBM)
    return pl.pallas_call(
        share_kernel,
        out_shape=[pltpu.HBM((w_gate_up.shape[0], D, share), jnp.bfloat16)] * 2,
        in_specs=[SMEM, whole],
        out_specs=[whole] * 2,
        scratch_shapes=[pltpu.SemaphoreType.DMA((2,))],
        compiler_params=params(2),
        name="shares",
    )(place_here, w_gate_up)


def per_device(
    hidden,
    attn_gain,
    w_qkv,
    kv_cache,
    page_table,
    lengths,
    request_group,
    key_mask,
    o_weight,
    moe_gain,
    router,
    routes,
    w_gate_up,
    w_down,
):
    n_tok = lax.axis_size("tok")
    n_head = lax.axis_size("head")
    tok_dev = hidden.shape[0]
    row_tokens = tok_dev * n_head
    kv_dev = w_qkv.shape[1] // ((QPG + 2) * HD)
    row_index = lax.axis_index("tok")
    head_index = lax.axis_index("head")

    place_here = jnp.stack([row_index, head_index]).astype(jnp.int32)
    hidden, kv_cache, routes, place_here = lax.optimization_barrier(
        (hidden, kv_cache, routes, place_here)
    )
    states = spread(hidden, "head", bits_of(n_head))
    told = jnp.pad(
        routes.T.astype(jnp.bfloat16),
        ((0, TAIL - TOPK), (0, kv_cache.shape[1] - tok_dev)),
    )
    swap = min(2, n_tok // 2)
    walk = [bit for bit in bits_of(n_tok) if bit != swap]
    shards = spread(jnp.concatenate([kv_cache, told], axis=0), "tok", bits_of(n_tok))

    tied, _ = lax.optimization_barrier((place_here, shards[swap]))
    lead, rest = shares_of(tied, n_head, w_gate_up)
    lead = crossed(lead, "tok", swap)

    requests = jnp.stack([lengths, request_group]).astype(jnp.float32)
    requests = jnp.pad(requests, ((0, 6), (0, -requests.shape[1] % LANES)))
    half = HD // 2
    frequency = np.float32(ROPE_BASE) ** (-2.0 * np.arange(half, dtype=np.float32) / HD)
    frequency = np.tile(frequency.astype(np.float32), LANES // half)[None, :]
    n_pages = page_table.shape[0]
    pages = jnp.arange(n_pages, dtype=jnp.int32)
    place = jnp.sum(
        jnp.where(page_table[:, None] == pages[None, :], pages[:, None], 0), axis=0
    )
    columns = w_qkv.shape[1]
    queries, own_kv, column_table, row_table, in_first = pl.pallas_call(
        functools.partial(project_kernel, n_head, kv_dev),
        out_shape=[
            pltpu.VMEM((kv_dev, QPG, row_tokens, LANES), jnp.bfloat16),
            jax.ShapeDtypeStruct((row_tokens, kv_dev * LANES), jnp.bfloat16),
            pltpu.VMEM((row_tokens, LANES), jnp.float32),
            pltpu.VMEM((8, 2 * row_tokens), jnp.float32),
            jax.ShapeDtypeStruct((1,), jnp.int32),
        ],
        in_specs=[SMEM] + [VMEM] * (5 + n_head),
        out_specs=[VMEM] * 4 + [SMEM],
        compiler_params=params(32 if row_tokens <= 256 else 60),
        cost_estimate=spent(row_tokens * D * columns * 4),
        name="project",
    )(
        place_here,
        requests,
        key_mask.reshape(-1, tok_dev),
        frequency,
        attn_gain[None, :],
        pinned(jnp.pad(w_qkv, ((0, 0), (0, -columns % LANES)))),
        *[states[k] for k in range(n_head)],
    )
    prior_kv = lax.ppermute(own_kv, "tok", [(i, i + 1) for i in range(n_tok - 1)])
    pool_rows = kv_cache.shape[0] * n_tok
    rest, down, prior_kv = lax.optimization_barrier((rest, w_down, prior_kv))
    rest = crossed(rest, "tok", swap)
    down = crossed(down, "tok", swap)
    leads = spread(lead, "head", bits_of(n_head))
    queries, *leads = lax.optimization_barrier((queries, *[leads[k] for k in range(n_head)]))
    halves = [(0, kv_dev)]
    pieces = [[] for _ in range(n_head)]
    for heads_at in halves:
        count = heads_at[1]
        *contexts, all_routes = pl.pallas_call(
            functools.partial(attend_kernel, n_tok, heads_at, n_head),
            out_shape=[pltpu.VMEM((tok_dev, count * QPG * HD), jnp.bfloat16)] * n_head
            + [pltpu.VMEM((n_tok * TAIL, tok_dev), jnp.bfloat16)],
            in_specs=[SMEM] * 3 + [VMEM] * 5 + [pl.BlockSpec(memory_space=pltpu.HBM)] * n_tok,
            out_specs=[VMEM] * (n_head + 1),
            scratch_shapes=[pltpu.VMEM((pool_rows, count * LANES), jnp.bfloat16)]
            + [pltpu.VMEM((count, QPG, row_tokens, LANES), jnp.float32)] * 3
            + [pltpu.SemaphoreType.DMA] * 2,
            compiler_params=params(28),
            cost_estimate=spent(count * QPG * row_tokens * pool_rows * LANES * ATT),
            name="attend",
        )(
            place_here,
            in_first,
            place,
            queries,
            prior_kv,
            own_kv,
            column_table,
            row_table,
            *[shards[d] for d in range(n_tok)],
        )
        for k in range(n_head):
            pieces[k].append(crossed(contexts[k], "head", k) if k else contexts[0])
    rest, *ends = lax.optimization_barrier((rest, *[listed[0] for listed in pieces]))
    pieces = [[end] for end in ends]
    rests = spread(rest, "head", bits_of(n_head))
    attn_sum, mid_states, mixed = pl.pallas_call(
        functools.partial(close_kernel, n_head),
        out_shape=[jax.ShapeDtypeStruct(hidden.shape, jnp.bfloat16)] * 3,
        in_specs=[SMEM] + [VMEM] * (3 + n_head * len(halves)),
        out_specs=[VMEM] * 3,
        compiler_params=params(20),
        cost_estimate=spent(tok_dev * D * D * 4),
        name="close",
    )(
        place_here,
        hidden,
        pinned(o_weight),
        moe_gain[None, :],
        *[piece for listed in pieces for piece in listed],
    )

    slots, swapped = spread_by_stages(mixed, "tok", walk, [w[k] for k in range(n_head) for w in (leads, rests)] + [down])
    order = sorted(slots)
    w_gate_up, w_down, *swapped = [pinned(w) for w in (w_gate_up, w_down, *swapped)]
    parts = {}
    for first in range(0, len(order), 2):
        parts.update(
            run_experts(
                slots,
                order[first : first + 2],
                place_here,
                swap,
                all_routes,
                router.T,
                w_gate_up,
                w_down,
                swapped,
            )
        )
    routed_sum = folded(parts, "tok", walk[::-1]).astype(jnp.float32)
    layer_out = (mid_states.astype(jnp.float32) + routed_sum).astype(jnp.bfloat16)
    return (attn_sum, layer_out)


def solution(mesh):
    return jax.shard_map(
        per_device,
        mesh=mesh,
        in_specs=(
            P(("tok", "head"), None),
            P(),
            P(None, "head"),
            P("tok", "head"),
            P(),
            P(),
            P(),
            P(),
            P(),
            P(),
            P(),
            P(("tok", "head"), None),
            P("tok", None, None),
            P("tok", None, None),
        ),
        out_specs=(P(("tok", "head"), None), P(("tok", "head"), None)),
        check_vma=False,
    )
```

time: 211 us -> 179 us (0.85)
  local copies, waits for them, and re-layouts: 33.3 us -> 4.09 us
  other arithmetic: 11.8 us -> 3.22 us
  starting transfers between devices: 35.1 us -> 39.8 us
    unnamed x57 -> x32, local copies, waits for them, and re-layouts: 21.9 us -> 4.07 us
    ppermute x37 -> x36, starting transfers between devices: 33.1 us -> 38.5 us  [crossed(): return lax.ppermute(array, axis, [(i, i ^ flip) for i in range(count)])]
    broadcast_in_dim x3 -> x0, local copies, waits for them, and re-layouts: 3.68 us -> none  [the longest x1 1.47 us: per_device(): request[:, None]]
    dynamic_slice x2 -> x0, local copies, waits for them, and re-layouts: 3.44 us -> none  [the longest x1 2.08 us: per_device(): down = lax.dynamic_slice_in_dim(w_down, head_index * share, share, 1)]
    pallas_call x5 -> x6, Pallas kernels: 43.1 us -> 43.8 us  [the longest x1 25.7 us: per_device(): pl.pallas_call(functools.partial(attend_kernel, n_tok, heads_at, n_head),...]
    ppermute x37 -> x36, waiting for transfers between devices: 81.4 us -> 81.5 us  [crossed(): return lax.ppermute(array, axis, [(i, i ^ flip) for i in range(count)])]
  transfers between devices with their start and end apart: 38 -> 37, of which waited for: 12 -> 14; matrix products, arithmetic and copies ran while one was open for 11% -> 0% of each run, Pallas kernels for 23% -> 26%
where the time goes in v4:
time: 179 us
  waiting for transfers between devices  81.8 us (46%)
  Pallas kernels  49.2 us (27%)
  starting transfers between devices  39.8 us (22%)
  local copies, waits for them, and re-layouts  4.09 us (2%)
  other arithmetic  3.22 us (2%)
    ppermute x36, waiting for transfers between devices, crossed(): return lax.ppermute(array, axis, [(i, i ^ flip) for i in range(count)])  81.5 us
    ppermute x36, starting transfers between devices, crossed(): return lax.ppermute(array, axis, [(i, i ^ flip) for i in range(count)])  38.5 us
    pallas_call x1, Pallas kernels, per_device(): pl.pallas_call(functools.partial(attend_kernel, n_tok, heads_at, n_head),...  25.7 us
    pallas_call x4, Pallas kernels, run_experts(): pl.pallas_call(functools.partial(expert_kernel, offsets, swap, len(swappe...  16.4 us
    unnamed x32, local copies, waits for them, and re-layouts  4.07 us
  transfers between devices with their start and end apart: 37, of which 14 were waited for; matrix products, arithmetic and copies ran while one was open for 0% of the time, Pallas kernels for 26%

profile of v4, /device:TPU:0, one launch (start us, length us, event | category | flops | bytes accessed | tf_op | source)
XLA Modules:
  0.0 179.0 jit_solution(16882631675130890262)
XLA Ops:
  2.5 3.0 %collective-permute-start = (bf16[272,512]{1,0:T(8,128)(2,1)S(1)}, bf16[272,512]{1,0:T(8,128)(2,1)S(1)}, u32[]{:S(2)}, u32[]{:S(2)}) collective-permute-start(bf16[272,512]{1,0:T(8,128)(2,1)S(1)} %fusion.1.refs_0_), channel_id=1, source_target_pairs={{0,4},{2,6},{4,0},{6,2},{8,12},{10,14},{12,8},{14,10},{16,20},{18,... | collective-permute-start | bytes 835592 | tf_op jit(solution)/shard_map/ppermute | solution.py:33
  5.5 6.7 %collective-permute-done.refs_2_ = bf16[272,512]{1,0:T(8,128)(2,1)S(1)} collective-permute-done((bf16[272,512]{1,0:T(8,128)(2,1)S(1)}, bf16[272,512]{1,0:T(8,128)(2,1)S(1)}, u32[]{:S(2)}, u32[]{:S(2)}) %collective-permute-start) | collective-permute-done | bytes 278560 | tf_op jit(solution)/shard_map/ppermute | solution.py:33
  17.6 2.6 %collective-permute-start.12 = (bf16[272,512]{1,0:T(8,128)(2,1)S(1)}, bf16[272,512]{1,0:T(8,128)(2,1)S(1)}, u32[]{:S(2)}, u32[]{:S(2)}) collective-permute-start(bf16[272,512]{1,0:T(8,128)(2,1)S(1)} %fusion.1.refs_0_), channel_id=1, source_target_pairs={{0,16},{2,18},{4,20},{6,22},{8,24},{10,26},{12,28},{14,30},{16,0},... | collective-permute-start | bytes 835592 | tf_op jit(solution)/shard_map/ppermute | solution.py:33
  23.3 11.5 %collective-permute-done.4.refs_6_ = bf16[1,1536,256]{2,1,0:T(8,128)(2,1)S(1)} collective-permute-done((bf16[1,1536,256]{2,1,0:T(8,128)(2,1)}, bf16[1,1536,256]{2,1,0:T(8,128)(2,1)S(1)}, u32[]{:S(2)}, u32[]{:S(2)}) %collective-permute-start.4) | collective-permute-done | bytes 786464 | tf_op jit(solution)/shard_map/ppermute | solution.py:33
  40.1 2.7 %collective-permute-done.16.refs_12_ = bf16[272,512]{1,0:T(8,128)(2,1)S(1)} collective-permute-done((bf16[272,512]{1,0:T(8,128)(2,1)S(1)}, bf16[272,512]{1,0:T(8,128)(2,1)S(1)}, u32[]{:S(2)}, u32[]{:S(2)}) %collective-permute-start.16) | collective-permute-done | bytes 278560 | tf_op jit(solution)/shard_map/ppermute | solution.py:33
  42.8 3.3 %collective-permute-done.14.refs_10_ = bf16[272,512]{1,0:T(8,128)(2,1)S(1)} collective-permute-done((bf16[272,512]{1,0:T(8,128)(2,1)S(1)}, bf16[272,512]{1,0:T(8,128)(2,1)S(1)}, u32[]{:S(2)}, u32[]{:S(2)}) %collective-permute-start.14) | collective-permute-done | bytes 278560 | tf_op jit(solution)/shard_map/ppermute | solution.py:33
  46.1 2.5 %collective-permute-start.18 = (bf16[272,512]{1,0:T(8,128)(2,1)S(1)}, bf16[272,512]{1,0:T(8,128)(2,1)S(1)}, u32[]{:S(2)}, u32[]{:S(2)}) collective-permute-start(bf16[272,512]{1,0:T(8,128)(2,1)S(1)} %collective-permute-done.16.refs_12_), channel_id=1, source_target_pairs={{0,4},{2,6},{4,0},{6,2},{8,12},{10,14},{12,8},{14,10},{16,20},{18,... | collective-permute-start | bytes 835592 | tf_op jit(solution)/shard_map/ppermute | solution.py:33
  48.6 2.1 %copy-done.3 = bf16[1536,1280]{1,0:T(8,128)(2,1)S(1)} copy-done((bf16[1536,1280]{1,0:T(8,128)(2,1)S(1)}, bf16[1536,1280]{1,0:T(8,128)(2,1)}, u32[]{:S(2)}) %copy-start.3) | copy-done | bytes 3932184
  50.7 3.2 %project.1 = (bf16[4,3,256,128]{3,2,1,0:T(8,128)(2,1)S(1)}, bf16[256,512]{1,0:T(8,128)(2,1)S(1)}, f32[256,128]{1,0:T(8,128)S(1)}, f32[8,512]{1,0:T(8,128)S(1)}, s32[1]{0:T(128)}) custom-call(s32[2]{0:T(128)S(1)} %pad_add_fusion.where_ref.scalar_ref, f32[8,128]{1,0:T(8,128)S(1)} %pad.9.requests_ref, s32[32,128]{1,0:T(8,128)S(1)} %bitcast.14, ...), custom_call_target="tpu_custom_call" | custom-call | flops 2013265920 | tf_op jit(solution)/shard_map/project/pallas_call | solution.py:517
  56.4 2.9 %collective-permute-start.15 = (bf16[272,512]{1,0:T(8,128)(2,1)S(1)}, bf16[272,512]{1,0:T(8,128)(2,1)S(1)}, u32[]{:S(2)}, u32[]{:S(2)}) collective-permute-start(bf16[272,512]{1,0:T(8,128)(2,1)S(1)} %collective-permute-done.14.refs_10_), channel_id=1, source_target_pairs={{0,2},{2,0},{4,6},{6,4},{8,10},{10,8},{12,14},{14,12},{16,18},{18,... | collective-permute-start | bytes 835592 | tf_op jit(solution)/shard_map/ppermute | solution.py:33
  60.0 2.5 %collective-permute-start.3 = (bf16[1,1536,256]{2,1,0:T(8,128)(2,1)S(1)}, bf16[1,1536,256]{2,1,0:T(8,128)(2,1)S(1)}, u32[]{:S(2)}, u32[]{:S(2)}) collective-permute-start(bf16[1,1536,256]{2,1,0:T(8,128)(2,1)S(1)} %copy-done.13), channel_id=1, source_target_pairs={{0,4},{2,6},{4,0},{6,2},{8,12},{10,14},{12,8},{14,10},{16,20},{18,... | collective-permute-start | bytes 2359304 | tf_op jit(solution)/shard_map/ppermute | solution.py:33
  62.6 25.7 %attend.1 = (bf16[128,768]{1,0:T(8,128)(2,1)S(1)}, bf16[128,768]{1,0:T(8,128)(2,1)S(1)}, bf16[256,128]{1,0:T(8,128)(2,1)S(1)}) custom-call(s32[2]{0:T(128)S(1)} %pad_add_fusion.where_ref.scalar_ref, s32[1]{0:T(128)} %get-tuple-element.56.first_ref, s32[256]{0:T(256)S(1)} %select_reduce_fusion.place_ref, ...), custom_call_target="tpu_custom_call" | custom-call | flops 25769803776 | tf_op jit(solution)/shard_map/attend/pallas_call | solution.py:551
  88.9 6.5 %collective-permute-done.20.refs_1_ = bf16[128,768]{1,0:T(8,128)(2,1)S(1)} collective-permute-done((bf16[128,768]{1,0:T(8,128)(2,1)S(1)}, bf16[128,768]{1,0:T(8,128)(2,1)S(1)}, u32[]{:S(2)}, u32[]{:S(2)}) %collective-permute-start.20) | collective-permute-done | bytes 196640 | tf_op jit(solution)/shard_map/ppermute | solution.py:33
  98.0 7.9 %collective-permute-start.23 = (bf16[128,1536]{1,0:T(8,128)(2,1)S(1)}, bf16[128,1536]{1,0:T(8,128)(2,1)S(1)}, u32[]{:S(2)}, u32[]{:S(2)}) collective-permute-start(bf16[128,1536]{1,0:T(8,128)(2,1)S(1)} %get-tuple-element.69.refs_0_), channel_id=1, source_target_pairs={{0,16},{2,18},{4,20},{6,22},{8,24},{10,26},{12,28},{14,30},{16,0},... | collective-permute-start | bytes 1179656 | tf_op jit(solution)/shard_map/ppermute | solution.py:33
  106.4 7.9 %collective-permute-done.25.refs_10_ = bf16[1,512,1536]{2,1,0:T(8,128)(2,1)S(1)} collective-permute-done((bf16[1,512,1536]{2,1,0:T(8,128)(2,1)S(1)}, bf16[1,512,1536]{2,1,0:T(8,128)(2,1)S(1)}, u32[]{:S(2)}, u32[]{:S(2)}) %collective-permute-start.25) | collective-permute-done | bytes 1572896 | tf_op jit(solution)/shard_map/ppermute | solution.py:33
  114.3 8.1 %collective-permute-done.23.refs_0_ = bf16[128,1536]{1,0:T(8,128)(2,1)S(1)} collective-permute-done((bf16[128,1536]{1,0:T(8,128)(2,1)S(1)}, bf16[128,1536]{1,0:T(8,128)(2,1)S(1)}, u32[]{:S(2)}, u32[]{:S(2)}) %collective-permute-start.23) | collective-permute-done | bytes 393248 | tf_op jit(solution)/shard_map/ppermute | solution.py:33
  124.7 4.0 %experts.4 = (bf16[128,1536]{1,0:T(8,128)(2,1)S(1)}, bf16[128,1536]{1,0:T(8,128)(2,1)S(1)}) custom-call(s32[2]{0:T(128)S(1)} %pad_add_fusion.where_ref.scalar_ref, bf16[128,1536]{1,0:T(8,128)(2,1)S(1)} %get-tuple-element.69.refs_0_, bf16[128,1536]{1,0:T(8,128)(2,1)S(1)} %collective-permute-done.21.refs_1_, bf16[256,128]{1,0:T(8,128)(2,1)S(1)} %get-tuple-element.75.refs_2_, ...), custom_call_target="tpu_custom_call" | custom-call | flops 4831838208 | tf_op jit(solution)/shard_map/experts/pallas_call | solution.py:420
  128.8 4.6 %collective-permute-done.29.refs_0_ = bf16[128,1536]{1,0:T(8,128)(2,1)S(1)} collective-permute-done((bf16[128,1536]{1,0:T(8,128)(2,1)S(1)}, bf16[128,1536]{1,0:T(8,128)(2,1)S(1)}, u32[]{:S(2)}, u32[]{:S(2)}) %collective-permute-start.29) | collective-permute-done | bytes 393248 | tf_op jit(solution)/shard_map/ppermute | solution.py:33
  133.4 4.0 %experts.6 = (bf16[128,1536]{1,0:T(8,128)(2,1)S(1)}, bf16[128,1536]{1,0:T(8,128)(2,1)S(1)}) custom-call(s32[2]{0:T(128)S(1)} %pad_add_fusion.where_ref.scalar_ref, bf16[128,1536]{1,0:T(8,128)(2,1)S(1)} %collective-permute-done.23.refs_0_, bf16[128,1536]{1,0:T(8,128)(2,1)S(1)} %collective-permute-done.28.refs_1_, ...), custom_call_target="tpu_custom_call" | custom-call | flops 4831838208 | tf_op jit(solution)/shard_map/experts/pallas_call | solution.py:420
  138.0 4.0 %experts.7 = (bf16[128,1536]{1,0:T(8,128)(2,1)S(1)}, bf16[128,1536]{1,0:T(8,128)(2,1)S(1)}) custom-call(s32[2]{0:T(128)S(1)} %pad_add_fusion.where_ref.scalar_ref, bf16[128,1536]{1,0:T(8,128)(2,1)S(1)} %collective-permute-done.29.refs_0_, bf16[128,1536]{1,0:T(8,128)(2,1)S(1)} %collective-permute-done.33.refs_1_, ...), custom_call_target="tpu_custom_call" | custom-call | flops 4831838208 | tf_op jit(solution)/shard_map/experts/pallas_call | solution.py:420
  142.2 4.2 %experts.5 = (bf16[128,1536]{1,0:T(8,128)(2,1)S(1)}, bf16[128,1536]{1,0:T(8,128)(2,1)S(1)}) custom-call(s32[2]{0:T(128)S(1)} %pad_add_fusion.where_ref.scalar_ref, bf16[128,1536]{1,0:T(8,128)(2,1)S(1)} %collective-permute-done.22.refs_0_, bf16[128,1536]{1,0:T(8,128)(2,1)S(1)} %collective-permute-done.27.refs_1_, ...), custom_call_target="tpu_custom_call" | custom-call | flops 4831838208 | tf_op jit(solution)/shard_map/experts/pallas_call | solution.py:420
  149.3 9.8 %collective-permute-done.35 = bf16[128,1536]{1,0:T(8,128)(2,1)S(1)} collective-permute-done((bf16[128,1536]{1,0:T(8,128)(2,1)S(1)}, bf16[128,1536]{1,0:T(8,128)(2,1)S(1)}, u32[]{:S(2)}, u32[]{:S(2)}) %collective-permute-start.35) | collective-permute-done | bytes 393248 | tf_op jit(solution)/shard_map/ppermute | solution.py:33
  159.8 12.3 %collective-permute-done.31 = bf16[128,1536]{1,0:T(8,128)(2,1)S(1)} collective-permute-done((bf16[128,1536]{1,0:T(8,128)(2,1)S(1)}, bf16[128,1536]{1,0:T(8,128)(2,1)S(1)}, u32[]{:S(2)}, u32[]{:S(2)}) %collective-permute-start.31) | collective-permute-done | bytes 393248 | tf_op jit(solution)/shard_map/ppermute | solution.py:33
  172.1 5.9 %collective-permute-done.36 = bf16[128,1536]{1,0:T(8,128)(2,1)S(1)} collective-permute-done((bf16[128,1536]{1,0:T(8,128)(2,1)S(1)}, bf16[128,1536]{1,0:T(8,128)(2,1)S(1)}, u32[]{:S(2)}, u32[]{:S(2)}) %collective-permute-start.36) | collective-permute-done | bytes 393248 | tf_op jit(solution)/shard_map/ppermute | solution.py:33
  (103 shorter events, 30.0 us)
Async XLA Ops:
  2.5 9.7 %collective-permute-start = (bf16[272,512]{1,0:T(8,128)(2,1)S(1)}, bf16[272,512]{1,0:T(8,128)(2,1)S(1)}, u32[]{:S(2)}, u32[]{:S(2)}) collective-permute-start(bf16[272,512]{1,0:T(8,128)(2,1)S(1)} %fusion.1.refs_0_), channel_id=1, source_target_pairs={{0,4},{2,6},{4,0},{6,2},{8,12},{10,14},{12,8},{14,10},{16,20},{18,... | collective-permute-start | bytes 835592 | tf_op jit(solution)/shard_map/ppermute | solution.py:33
  15.8 19.0 %collective-permute-start.4 = (bf16[1,1536,256]{2,1,0:T(8,128)(2,1)}, bf16[1,1536,256]{2,1,0:T(8,128)(2,1)S(1)}, u32[]{:S(2)}, u32[]{:S(2)}) collective-permute-start(bf16[1,1536,256]{2,1,0:T(8,128)(2,1)} %get-tuple-element.58), channel_id=1, source_target_pairs={{0,4},{2,6},{4,0},{6,2},{8,12},{10,14},{12,8},{14,10},{16,20},{18,... | collective-permute-start | bytes 2359304 | tf_op jit(solution)/shard_map/ppermute | solution.py:33
  17.6 18.7 %collective-permute-start.12 = (bf16[272,512]{1,0:T(8,128)(2,1)S(1)}, bf16[272,512]{1,0:T(8,128)(2,1)S(1)}, u32[]{:S(2)}, u32[]{:S(2)}) collective-permute-start(bf16[272,512]{1,0:T(8,128)(2,1)S(1)} %fusion.1.refs_0_), channel_id=1, source_target_pairs={{0,16},{2,18},{4,20},{6,22},{8,24},{10,26},{12,28},{14,30},{16,0},... | collective-permute-start | bytes 835592 | tf_op jit(solution)/shard_map/ppermute | solution.py:33
  20.2 17.6 %collective-permute-start.8 = (bf16[272,512]{1,0:T(8,128)(2,1)S(1)}, bf16[272,512]{1,0:T(8,128)(2,1)S(1)}, u32[]{:S(2)}, u32[]{:S(2)}) collective-permute-start(bf16[272,512]{1,0:T(8,128)(2,1)S(1)} %fusion.1.refs_0_), channel_id=1, source_target_pairs={{0,8},{2,10},{4,12},{6,14},{8,0},{10,2},{12,4},{14,6},{16,24},{18,... | collective-permute-start | bytes 835592 | tf_op jit(solution)/shard_map/ppermute | solution.py:33
  21.8 17.7 %collective-permute-start.1 = (bf16[128,1536]{1,0:T(8,128)(2,1)S(1)}, bf16[128,1536]{1,0:T(8,128)(2,1)S(1)}, u32[]{:S(2)}, u32[]{:S(2)}) collective-permute-start(bf16[128,1536]{1,0:T(8,128)(2,1)S(1)} %copy-done.2), channel_id=1, source_target_pairs={{0,1},{1,0},{2,3},{3,2},{4,5},{5,4},{6,7},{7,6},{8,9},{9,8},{10,11... | collective-permute-start | bytes 1179656 | tf_op jit(solution)/shard_map/ppermute | solution.py:33
  23.3 16.0 %collective-permute-start.6 = (bf16[272,512]{1,0:T(8,128)(2,1)S(1)}, bf16[272,512]{1,0:T(8,128)(2,1)S(1)}, u32[]{:S(2)}, u32[]{:S(2)}) collective-permute-start(bf16[272,512]{1,0:T(8,128)(2,1)S(1)} %fusion.1.refs_0_), channel_id=1, source_target_pairs={{0,2},{2,0},{4,6},{6,4},{8,10},{10,8},{12,14},{14,12},{16,18},{18,... | collective-permute-start | bytes 835592 | tf_op jit(solution)/shard_map/ppermute | solution.py:33
  34.8 24.5 %collective-permute-start.5 = (bf16[1,1536,256]{2,1,0:T(8,128)(2,1)S(1)}, bf16[1,1536,256]{2,1,0:T(8,128)(2,1)S(1)}, u32[]{:S(2)}, u32[]{:S(2)}) collective-permute-start(bf16[1,1536,256]{2,1,0:T(8,128)(2,1)S(1)} %collective-permute-done.4.refs_6_), channel_id=1, source_target_pairs={{0,1},{1,0},{2,3},{3,2},{4,5},{5,4},{6,7},{7,6},{8,9},{9,8},{10,11... | collective-permute-start | bytes 2359304 | tf_op jit(solution)/shard_map/ppermute | solution.py:33
  39.3 14.6 %collective-permute-start.13 = (bf16[272,512]{1,0:T(8,128)(2,1)S(1)}, bf16[272,512]{1,0:T(8,128)(2,1)S(1)}, u32[]{:S(2)}, u32[]{:S(2)}) collective-permute-start(bf16[272,512]{1,0:T(8,128)(2,1)S(1)} %collective-permute-done.12.refs_8_), channel_id=1, source_target_pairs={{0,2},{2,0},{4,6},{6,4},{8,10},{10,8},{12,14},{14,12},{16,18},{18,... | collective-permute-start | bytes 835592 | tf_op jit(solution)/shard_map/ppermute | solution.py:33
  39.5 15.8 %collective-permute-start.10 = (bf16[272,512]{1,0:T(8,128)(2,1)S(1)}, bf16[272,512]{1,0:T(8,128)(2,1)S(1)}, u32[]{:S(2)}, u32[]{:S(2)}) collective-permute-start(bf16[272,512]{1,0:T(8,128)(2,1)S(1)} %collective-permute-done.8.refs_4_), channel_id=1, source_target_pairs={{0,4},{2,6},{4,0},{6,2},{8,12},{10,14},{12,8},{14,10},{16,20},{18,... | collective-permute-start | bytes 835592 | tf_op jit(solution)/shard_map/ppermute | solution.py:33
  42.8 13.3 %collective-permute-start.9 = (bf16[272,512]{1,0:T(8,128)(2,1)S(1)}, bf16[272,512]{1,0:T(8,128)(2,1)S(1)}, u32[]{:S(2)}, u32[]{:S(2)}) collective-permute-start(bf16[272,512]{1,0:T(8,128)(2,1)S(1)} %collective-permute-done.8.refs_4_), channel_id=1, source_target_pairs={{0,2},{2,0},{4,6},{6,4},{8,10},{10,8},{12,14},{14,12},{16,18},{18,... | collective-permute-start | bytes 835592 | tf_op jit(solution)/shard_map/ppermute | solution.py:33
  46.1 13.2 %collective-permute-start.18 = (bf16[272,512]{1,0:T(8,128)(2,1)S(1)}, bf16[272,512]{1,0:T(8,128)(2,1)S(1)}, u32[]{:S(2)}, u32[]{:S(2)}) collective-permute-start(bf16[272,512]{1,0:T(8,128)(2,1)S(1)} %collective-permute-done.16.refs_12_), channel_id=1, source_target_pairs={{0,4},{2,6},{4,0},{6,2},{8,12},{10,14},{12,8},{14,10},{16,20},{18,... | collective-permute-start | bytes 835592 | tf_op jit(solution)/shard_map/ppermute | solution.py:33
  60.0 29.0 %collective-permute-start.3 = (bf16[1,1536,256]{2,1,0:T(8,128)(2,1)S(1)}, bf16[1,1536,256]{2,1,0:T(8,128)(2,1)S(1)}, u32[]{:S(2)}, u32[]{:S(2)}) collective-permute-start(bf16[1,1536,256]{2,1,0:T(8,128)(2,1)S(1)} %copy-done.13), channel_id=1, source_target_pairs={{0,4},{2,6},{4,0},{6,2},{8,12},{10,14},{12,8},{14,10},{16,20},{18,... | collective-permute-start | bytes 2359304 | tf_op jit(solution)/shard_map/ppermute | solution.py:33
  62.5 51.8 %collective-permute-start.25 = (bf16[1,512,1536]{2,1,0:T(8,128)(2,1)S(1)}, bf16[1,512,1536]{2,1,0:T(8,128)(2,1)S(1)}, u32[]{:S(2)}, u32[]{:S(2)}) collective-permute-start(bf16[1,512,1536]{2,1,0:T(8,128)(2,1)S(1)} %copy-done.4), channel_id=1, source_target_pairs={{0,4},{2,6},{4,0},{6,2},{8,12},{10,14},{12,8},{14,10},{16,20},{18,... | collective-permute-start | bytes 4718600 | tf_op jit(solution)/shard_map/ppermute | solution.py:33
  95.4 28.4 %collective-permute-start.24 = (bf16[1,1536,256]{2,1,0:T(8,128)(2,1)S(1)}, bf16[1,1536,256]{2,1,0:T(8,128)(2,1)S(1)}, u32[]{:S(2)}, u32[]{:S(2)}) collective-permute-start(bf16[1,1536,256]{2,1,0:T(8,128)(2,1)S(1)} %collective-permute-done.3.refs_7_), channel_id=1, source_target_pairs={{0,1},{1,0},{2,3},{3,2},{4,5},{5,4},{6,7},{7,6},{8,9},{9,8},{10,11... | collective-permute-start | bytes 2359304 | tf_op jit(solution)/shard_map/ppermute | solution.py:33
  98.0 24.3 %collective-permute-start.23 = (bf16[128,1536]{1,0:T(8,128)(2,1)S(1)}, bf16[128,1536]{1,0:T(8,128)(2,1)S(1)}, u32[]{:S(2)}, u32[]{:S(2)}) collective-permute-start(bf16[128,1536]{1,0:T(8,128)(2,1)S(1)} %get-tuple-element.69.refs_0_), channel_id=1, source_target_pairs={{0,16},{2,18},{4,20},{6,22},{8,24},{10,26},{12,28},{14,30},{16,0},... | collective-permute-start | bytes 1179656 | tf_op jit(solution)/shard_map/ppermute | solution.py:33
  106.0 17.8 %collective-permute-start.22 = (bf16[128,1536]{1,0:T(8,128)(2,1)S(1)}, bf16[128,1536]{1,0:T(8,128)(2,1)S(1)}, u32[]{:S(2)}, u32[]{:S(2)}) collective-permute-start(bf16[128,1536]{1,0:T(8,128)(2,1)S(1)} %get-tuple-element.69.refs_0_), channel_id=1, source_target_pairs={{0,8},{2,10},{4,12},{6,14},{8,0},{10,2},{12,4},{14,6},{16,24},{18,... | collective-permute-start | bytes 1179656 | tf_op jit(solution)/shard_map/ppermute | solution.py:33
  106.4 17.3 %collective-permute-start.21 = (bf16[128,1536]{1,0:T(8,128)(2,1)S(1)}, bf16[128,1536]{1,0:T(8,128)(2,1)S(1)}, u32[]{:S(2)}, u32[]{:S(2)}) collective-permute-start(bf16[128,1536]{1,0:T(8,128)(2,1)S(1)} %get-tuple-element.69.refs_0_), channel_id=1, source_target_pairs={{0,2},{2,0},{4,6},{6,4},{8,10},{10,8},{12,14},{14,12},{16,18},{18,... | collective-permute-start | bytes 1179656 | tf_op jit(solution)/shard_map/ppermute | solution.py:33
  123.8 9.7 %collective-permute-start.29 = (bf16[128,1536]{1,0:T(8,128)(2,1)S(1)}, bf16[128,1536]{1,0:T(8,128)(2,1)S(1)}, u32[]{:S(2)}, u32[]{:S(2)}) collective-permute-start(bf16[128,1536]{1,0:T(8,128)(2,1)S(1)} %collective-permute-done.23.refs_0_), channel_id=1, source_target_pairs={{0,8},{2,10},{4,12},{6,14},{8,0},{10,2},{12,4},{14,6},{16,24},{18,... | collective-permute-start | bytes 1179656 | tf_op jit(solution)/shard_map/ppermute | solution.py:33
  124.2 9.2 %collective-permute-start.28 = (bf16[128,1536]{1,0:T(8,128)(2,1)S(1)}, bf16[128,1536]{1,0:T(8,128)(2,1)S(1)}, u32[]{:S(2)}, u32[]{:S(2)}) collective-permute-start(bf16[128,1536]{1,0:T(8,128)(2,1)S(1)} %collective-permute-done.23.refs_0_), channel_id=1, source_target_pairs={{0,2},{2,0},{4,6},{6,4},{8,10},{10,8},{12,14},{14,12},{16,18},{18,... | collective-permute-start | bytes 1179656 | tf_op jit(solution)/shard_map/ppermute | solution.py:33
  128.7 31.0 %collective-permute-start.26 = (bf16[128,1536]{1,0:T(8,128)(2,1)S(1)}, bf16[128,1536]{1,0:T(8,128)(2,1)S(1)}, u32[]{:S(2)}, u32[]{:S(2)}) collective-permute-start(bf16[128,1536]{1,0:T(8,128)(2,1)S(1)} %get-tuple-element.82), channel_id=1, source_target_pairs={{0,2},{2,0},{4,6},{6,4},{8,10},{10,8},{12,14},{14,12},{16,18},{18,... | collective-permute-start | bytes 1179656 | tf_op jit(solution)/shard_map/ppermute | solution.py:33
  137.5 11.9 %collective-permute-start.32 = (bf16[128,1536]{1,0:T(8,128)(2,1)S(1)}, bf16[128,1536]{1,0:T(8,128)(2,1)S(1)}, u32[]{:S(2)}, u32[]{:S(2)}) collective-permute-start(bf16[128,1536]{1,0:T(8,128)(2,1)S(1)} %get-tuple-element.90), channel_id=1, source_target_pairs={{0,2},{2,0},{4,6},{6,4},{8,10},{10,8},{12,14},{14,12},{16,18},{18,... | collective-permute-start | bytes 1179656 | tf_op jit(solution)/shard_map/ppermute | solution.py:33
  147.1 12.0 %collective-permute-start.35 = (bf16[128,1536]{1,0:T(8,128)(2,1)S(1)}, bf16[128,1536]{1,0:T(8,128)(2,1)S(1)}, u32[]{:S(2)}, u32[]{:S(2)}) collective-permute-start(bf16[128,1536]{1,0:T(8,128)(2,1)S(1)} %add_convert_fusion.2), channel_id=1, source_target_pairs={{0,8},{2,10},{4,12},{6,14},{8,0},{10,2},{12,4},{14,6},{16,24},{18,... | collective-permute-start | bytes 1179656 | tf_op jit(solution)/shard_map/ppermute | solution.py:33
  148.4 23.7 %collective-permute-start.31 = (bf16[128,1536]{1,0:T(8,128)(2,1)S(1)}, bf16[128,1536]{1,0:T(8,128)(2,1)S(1)}, u32[]{:S(2)}, u32[]{:S(2)}) collective-permute-start(bf16[128,1536]{1,0:T(8,128)(2,1)S(1)} %add_convert_fusion.3), channel_id=1, source_target_pairs={{0,8},{2,10},{4,12},{6,14},{8,0},{10,2},{12,4},{14,6},{16,24},{18,... | collective-permute-start | bytes 1179656 | tf_op jit(solution)/shard_map/ppermute | solution.py:33
  159.3 18.7 %collective-permute-start.36 = (bf16[128,1536]{1,0:T(8,128)(2,1)S(1)}, bf16[128,1536]{1,0:T(8,128)(2,1)S(1)}, u32[]{:S(2)}, u32[]{:S(2)}) collective-permute-start(bf16[128,1536]{1,0:T(8,128)(2,1)S(1)} %add_convert_fusion.1), channel_id=1, source_target_pairs={{0,16},{2,18},{4,20},{6,22},{8,24},{10,26},{12,28},{14,30},{16,0},... | collective-permute-start | bytes 1179656 | tf_op jit(solution)/shard_map/ppermute | solution.py:33
  (29 other events, 515.9 us)

commit v5 on v4

--- a/solution.py
+++ b/solution.py
@@ -225,7 +225,7 @@
 ):
     shard_refs = refs[:shards]
     out_refs = refs[shards : shards + slots]
-    routes_ref, pool_ref, peak_ref, total_ref, sum_ref, arrived, told = refs[shards + slots :]
+    routes_ref, stage_ref, pool_ref, peak_ref, total_ref, sum_ref, arrived = refs[shards + slots :]
     me = scalar_ref[0]
     in_first = first_ref[0]
     first_head, kv_dev = heads_at
@@ -236,21 +236,7 @@
     shard_pages = shard_rows // PAGE
 
     for d in range(shards):
-        def start(j, carry, d=d):
-            page = (me ^ d) * shard_pages + j
-            pltpu.make_async_copy(
-                shard_refs[d].at[pl.ds(pl.multiple_of(j * PAGE, PAGE), PAGE), mine],
-                pool_ref.at[pl.ds(pl.multiple_of(place_ref[page] * PAGE, PAGE), PAGE), :],
-                arrived,
-            ).start()
-            return carry
-
-        lax.fori_loop(0, shard_pages, start, 0, unroll=True)
-        pltpu.make_async_copy(
-            shard_refs[d].at[shard_rows : shard_rows + TAIL, : routes_ref.shape[1]],
-            routes_ref.at[d * TAIL : (d + 1) * TAIL, :],
-            told,
-        ).start()
+        pltpu.make_async_copy(shard_refs[d].at[:, mine], stage_ref.at[d], arrived).start()
 
     def near(b, carry):
         at = pl.ds(pl.multiple_of(b * BLOCK, BLOCK), BLOCK)
@@ -276,8 +262,14 @@
         return carry
 
     lax.fori_loop(0, blocks, near, 0)
-    pltpu.make_async_copy(pool_ref, pool_ref, arrived).wait()
-    pltpu.make_async_copy(routes_ref, routes_ref, told).wait()
+    pltpu.make_async_copy(stage_ref, stage_ref, arrived).wait()
+    for d in range(shards):
+        for j in range(shard_pages):
+            at = pl.multiple_of(place_ref[(me ^ d) * shard_pages + j] * PAGE, PAGE)
+            pool_ref[pl.ds(at, PAGE), :] = stage_ref[d, j * PAGE : (j + 1) * PAGE, :]
+        routes_ref[d * TAIL : (d + 1) * TAIL, :] = stage_ref[
+            d, shard_rows : shard_rows + TAIL, : routes_ref.shape[1]
+        ]
 
     group_rows = pool_ref.shape[0] // GROUPS
     full = (in_first + BLOCK - 1) // BLOCK
@@ -554,10 +546,13 @@
             + [pltpu.VMEM((n_tok * TAIL, tok_dev), jnp.bfloat16)],
             in_specs=[SMEM] * 3 + [VMEM] * 5 + [pl.BlockSpec(memory_space=pltpu.HBM)] * n_tok,
             out_specs=[VMEM] * (n_head + 1),
-            scratch_shapes=[pltpu.VMEM((pool_rows, count * LANES), jnp.bfloat16)]
+            scratch_shapes=[
+                pltpu.VMEM((n_tok, kv_cache.shape[0] + TAIL, count * LANES), jnp.bfloat16),
+                pltpu.VMEM((pool_rows, count * LANES), jnp.bfloat16),
+            ]
             + [pltpu.VMEM((count, QPG, row_tokens, LANES), jnp.float32)] * 3
-            + [pltpu.SemaphoreType.DMA] * 2,
-            compiler_params=params(28),
+            + [pltpu.SemaphoreType.DMA],
+            compiler_params=params(34),
             cost_estimate=spent(count * QPG * row_tokens * pool_rows * LANES * ATT),
             name="attend",
         )(

time: 179 us -> 173 us (0.966)
  starting transfers between devices: 39.8 us -> 47.8 us
  waiting for transfers between devices: 81.8 us -> 74.1 us
  Pallas kernels: 49.2 us -> 43 us
    ppermute x36, starting transfers between devices: 38.5 us -> 46.5 us  [crossed(): return lax.ppermute(array, axis, [(i, i ^ flip) for i in range(count)])]
    ppermute x36, waiting for transfers between devices: 81.5 us -> 73.9 us  [crossed(): return lax.ppermute(array, axis, [(i, i ^ flip) for i in range(count)])]
    pallas_call x1, Pallas kernels: 25.7 us -> 19.6 us  [per_device(): pl.pallas_call(functools.partial(attend_kernel, n_tok, heads_at, n_head),...]
  transfers between devices with their start and end apart: 37 -> 37, of which waited for: 14 -> 11; matrix products, arithmetic and copies ran while one was open for 0% -> 0% of each run, Pallas kernels for 26% -> 24%
where the time goes in v5:
time: 173 us
  waiting for transfers between devices  74.1 us (43%)
  starting transfers between devices  47.8 us (28%)
  Pallas kernels  43 us (25%)
  local copies, waits for them, and re-layouts  4.09 us (2%)
  other arithmetic  3.26 us (2%)
    ppermute x36, waiting for transfers between devices, crossed(): return lax.ppermute(array, axis, [(i, i ^ flip) for i in range(count)])  73.9 us
    ppermute x36, starting transfers between devices, crossed(): return lax.ppermute(array, axis, [(i, i ^ flip) for i in range(count)])  46.5 us
    pallas_call x1, Pallas kernels, per_device(): pl.pallas_call(functools.partial(attend_kernel, n_tok, heads_at, n_head),...  19.6 us
    pallas_call x4, Pallas kernels, run_experts(): pl.pallas_call(functools.partial(expert_kernel, offsets, swap, len(swappe...  16.3 us
    unnamed x32, local copies, waits for them, and re-layouts  4.07 us
  transfers between devices with their start and end apart: 37, of which 11 were waited for; matrix products, arithmetic and copies ran while one was open for 0% of the time, Pallas kernels for 24%

profile of v5, /device:TPU:0, one launch (start us, length us, event | category | flops | bytes accessed | tf_op | source)
XLA Modules:
  0.0 173.2 jit_solution(17345949769365064576)
XLA Ops:
  2.5 3.0 %collective-permute-start = (bf16[272,512]{1,0:T(8,128)(2,1)S(1)}, bf16[272,512]{1,0:T(8,128)(2,1)S(1)}, u32[]{:S(2)}, u32[]{:S(2)}) collective-permute-start(bf16[272,512]{1,0:T(8,128)(2,1)S(1)} %fusion.1.refs_0_), channel_id=1, source_target_pairs={{0,4},{2,6},{4,0},{6,2},{8,12},{10,14},{12,8},{14,10},{16,20},{18,... | collective-permute-start | bytes 835592 | tf_op jit(solution)/shard_map/ppermute | solution.py:33
  5.5 6.7 %collective-permute-done.refs_2_ = bf16[272,512]{1,0:T(8,128)(2,1)S(1)} collective-permute-done((bf16[272,512]{1,0:T(8,128)(2,1)S(1)}, bf16[272,512]{1,0:T(8,128)(2,1)S(1)}, u32[]{:S(2)}, u32[]{:S(2)}) %collective-permute-start) | collective-permute-done | bytes 278560 | tf_op jit(solution)/shard_map/ppermute | solution.py:33
  17.6 2.6 %collective-permute-start.12 = (bf16[272,512]{1,0:T(8,128)(2,1)S(1)}, bf16[272,512]{1,0:T(8,128)(2,1)S(1)}, u32[]{:S(2)}, u32[]{:S(2)}) collective-permute-start(bf16[272,512]{1,0:T(8,128)(2,1)S(1)} %fusion.1.refs_0_), channel_id=1, source_target_pairs={{0,16},{2,18},{4,20},{6,22},{8,24},{10,26},{12,28},{14,30},{16,0},... | collective-permute-start | bytes 835592 | tf_op jit(solution)/shard_map/ppermute | solution.py:33
  23.3 11.5 %collective-permute-done.4.refs_6_ = bf16[1,1536,256]{2,1,0:T(8,128)(2,1)S(1)} collective-permute-done((bf16[1,1536,256]{2,1,0:T(8,128)(2,1)}, bf16[1,1536,256]{2,1,0:T(8,128)(2,1)S(1)}, u32[]{:S(2)}, u32[]{:S(2)}) %collective-permute-start.4) | collective-permute-done | bytes 786464 | tf_op jit(solution)/shard_map/ppermute | solution.py:33
  40.1 2.7 %collective-permute-done.16.refs_12_ = bf16[272,512]{1,0:T(8,128)(2,1)S(1)} collective-permute-done((bf16[272,512]{1,0:T(8,128)(2,1)S(1)}, bf16[272,512]{1,0:T(8,128)(2,1)S(1)}, u32[]{:S(2)}, u32[]{:S(2)}) %collective-permute-start.16) | collective-permute-done | bytes 278560 | tf_op jit(solution)/shard_map/ppermute | solution.py:33
  42.8 3.3 %collective-permute-done.14.refs_10_ = bf16[272,512]{1,0:T(8,128)(2,1)S(1)} collective-permute-done((bf16[272,512]{1,0:T(8,128)(2,1)S(1)}, bf16[272,512]{1,0:T(8,128)(2,1)S(1)}, u32[]{:S(2)}, u32[]{:S(2)}) %collective-permute-start.14) | collective-permute-done | bytes 278560 | tf_op jit(solution)/shard_map/ppermute | solution.py:33
  46.1 2.5 %collective-permute-start.18 = (bf16[272,512]{1,0:T(8,128)(2,1)S(1)}, bf16[272,512]{1,0:T(8,128)(2,1)S(1)}, u32[]{:S(2)}, u32[]{:S(2)}) collective-permute-start(bf16[272,512]{1,0:T(8,128)(2,1)S(1)} %collective-permute-done.16.refs_12_), channel_id=1, source_target_pairs={{0,4},{2,6},{4,0},{6,2},{8,12},{10,14},{12,8},{14,10},{16,20},{18,... | collective-permute-start | bytes 835592 | tf_op jit(solution)/shard_map/ppermute | solution.py:33
  50.7 3.2 %project.1 = (bf16[4,3,256,128]{3,2,1,0:T(8,128)(2,1)S(1)}, bf16[256,512]{1,0:T(8,128)(2,1)S(1)}, f32[256,128]{1,0:T(8,128)S(1)}, f32[8,512]{1,0:T(8,128)S(1)}, s32[1]{0:T(128)}) custom-call(s32[2]{0:T(128)S(1)} %pad_add_fusion.where_ref.scalar_ref, f32[8,128]{1,0:T(8,128)S(1)} %pad.9.requests_ref, s32[32,128]{1,0:T(8,128)S(1)} %bitcast.14, ...), custom_call_target="tpu_custom_call" | custom-call | flops 2013265920 | tf_op jit(solution)/shard_map/project/pallas_call | solution.py:509
  56.4 2.9 %collective-permute-start.15 = (bf16[272,512]{1,0:T(8,128)(2,1)S(1)}, bf16[272,512]{1,0:T(8,128)(2,1)S(1)}, u32[]{:S(2)}, u32[]{:S(2)}) collective-permute-start(bf16[272,512]{1,0:T(8,128)(2,1)S(1)} %collective-permute-done.14.refs_10_), channel_id=1, source_target_pairs={{0,2},{2,0},{4,6},{6,4},{8,10},{10,8},{12,14},{14,12},{16,18},{18,... | collective-permute-start | bytes 835592 | tf_op jit(solution)/shard_map/ppermute | solution.py:33
  60.0 2.5 %collective-permute-start.3 = (bf16[1,1536,256]{2,1,0:T(8,128)(2,1)S(1)}, bf16[1,1536,256]{2,1,0:T(8,128)(2,1)S(1)}, u32[]{:S(2)}, u32[]{:S(2)}) collective-permute-start(bf16[1,1536,256]{2,1,0:T(8,128)(2,1)S(1)} %copy-done.13), channel_id=1, source_target_pairs={{0,4},{2,6},{4,0},{6,2},{8,12},{10,14},{12,8},{14,10},{16,20},{18,... | collective-permute-start | bytes 2359304 | tf_op jit(solution)/shard_map/ppermute | solution.py:33
  62.6 19.6 %attend.1 = (bf16[128,768]{1,0:T(8,128)(2,1)S(1)}, bf16[128,768]{1,0:T(8,128)(2,1)S(1)}, bf16[256,128]{1,0:T(8,128)(2,1)S(1)}) custom-call(s32[2]{0:T(128)S(1)} %pad_add_fusion.where_ref.scalar_ref, s32[1]{0:T(128)} %get-tuple-element.56.first_ref, s32[256]{0:T(256)S(1)} %select_reduce_fusion.place_ref, ...), custom_call_target="tpu_custom_call" | custom-call | flops 25769803776 | tf_op jit(solution)/shard_map/attend/pallas_call | solution.py:543
  82.8 6.5 %collective-permute-done.20.refs_1_ = bf16[128,768]{1,0:T(8,128)(2,1)S(1)} collective-permute-done((bf16[128,768]{1,0:T(8,128)(2,1)S(1)}, bf16[128,768]{1,0:T(8,128)(2,1)S(1)}, u32[]{:S(2)}, u32[]{:S(2)}) %collective-permute-start.20) | collective-permute-done | bytes 196640 | tf_op jit(solution)/shard_map/ppermute | solution.py:33
  91.9 8.1 %collective-permute-start.23 = (bf16[128,1536]{1,0:T(8,128)(2,1)S(1)}, bf16[128,1536]{1,0:T(8,128)(2,1)S(1)}, u32[]{:S(2)}, u32[]{:S(2)}) collective-permute-start(bf16[128,1536]{1,0:T(8,128)(2,1)S(1)} %get-tuple-element.69.refs_0_), channel_id=1, source_target_pairs={{0,16},{2,18},{4,20},{6,22},{8,24},{10,26},{12,28},{14,30},{16,0},... | collective-permute-start | bytes 1179656 | tf_op jit(solution)/shard_map/ppermute | solution.py:33
  100.3 14.0 %collective-permute-done.25.refs_10_ = bf16[1,512,1536]{2,1,0:T(8,128)(2,1)S(1)} collective-permute-done((bf16[1,512,1536]{2,1,0:T(8,128)(2,1)S(1)}, bf16[1,512,1536]{2,1,0:T(8,128)(2,1)S(1)}, u32[]{:S(2)}, u32[]{:S(2)}) %collective-permute-start.25) | collective-permute-done | bytes 1572896 | tf_op jit(solution)/shard_map/ppermute | solution.py:33
  114.3 3.1 %collective-permute-start.29 = (bf16[128,1536]{1,0:T(8,128)(2,1)S(1)}, bf16[128,1536]{1,0:T(8,128)(2,1)S(1)}, u32[]{:S(2)}, u32[]{:S(2)}) collective-permute-start(bf16[128,1536]{1,0:T(8,128)(2,1)S(1)} %collective-permute-done.23.refs_0_), channel_id=1, source_target_pairs={{0,8},{2,10},{4,12},{6,14},{8,0},{10,2},{12,4},{14,6},{16,24},{18,... | collective-permute-start | bytes 1179656 | tf_op jit(solution)/shard_map/ppermute | solution.py:33
  118.0 4.0 %experts.4 = (bf16[128,1536]{1,0:T(8,128)(2,1)S(1)}, bf16[128,1536]{1,0:T(8,128)(2,1)S(1)}) custom-call(s32[2]{0:T(128)S(1)} %pad_add_fusion.where_ref.scalar_ref, bf16[128,1536]{1,0:T(8,128)(2,1)S(1)} %get-tuple-element.69.refs_0_, bf16[128,1536]{1,0:T(8,128)(2,1)S(1)} %collective-permute-done.21.refs_1_, bf16[256,128]{1,0:T(8,128)(2,1)S(1)} %get-tuple-element.75.refs_2_, ...), custom_call_target="tpu_custom_call" | custom-call | flops 4831838208 | tf_op jit(solution)/shard_map/experts/pallas_call | solution.py:412
  122.1 4.3 %collective-permute-done.29.refs_0_ = bf16[128,1536]{1,0:T(8,128)(2,1)S(1)} collective-permute-done((bf16[128,1536]{1,0:T(8,128)(2,1)S(1)}, bf16[128,1536]{1,0:T(8,128)(2,1)S(1)}, u32[]{:S(2)}, u32[]{:S(2)}) %collective-permute-start.29) | collective-permute-done | bytes 393248 | tf_op jit(solution)/shard_map/ppermute | solution.py:33
  126.4 4.0 %experts.6 = (bf16[128,1536]{1,0:T(8,128)(2,1)S(1)}, bf16[128,1536]{1,0:T(8,128)(2,1)S(1)}) custom-call(s32[2]{0:T(128)S(1)} %pad_add_fusion.where_ref.scalar_ref, bf16[128,1536]{1,0:T(8,128)(2,1)S(1)} %collective-permute-done.23.refs_0_, bf16[128,1536]{1,0:T(8,128)(2,1)S(1)} %collective-permute-done.28.refs_1_, ...), custom_call_target="tpu_custom_call" | custom-call | flops 4831838208 | tf_op jit(solution)/shard_map/experts/pallas_call | solution.py:412
  131.0 4.0 %experts.7 = (bf16[128,1536]{1,0:T(8,128)(2,1)S(1)}, bf16[128,1536]{1,0:T(8,128)(2,1)S(1)}) custom-call(s32[2]{0:T(128)S(1)} %pad_add_fusion.where_ref.scalar_ref, bf16[128,1536]{1,0:T(8,128)(2,1)S(1)} %collective-permute-done.29.refs_0_, bf16[128,1536]{1,0:T(8,128)(2,1)S(1)} %collective-permute-done.33.refs_1_, ...), custom_call_target="tpu_custom_call" | custom-call | flops 4831838208 | tf_op jit(solution)/shard_map/experts/pallas_call | solution.py:412
  135.2 4.2 %experts.5 = (bf16[128,1536]{1,0:T(8,128)(2,1)S(1)}, bf16[128,1536]{1,0:T(8,128)(2,1)S(1)}) custom-call(s32[2]{0:T(128)S(1)} %pad_add_fusion.where_ref.scalar_ref, bf16[128,1536]{1,0:T(8,128)(2,1)S(1)} %collective-permute-done.22.refs_0_, bf16[128,1536]{1,0:T(8,128)(2,1)S(1)} %collective-permute-done.27.refs_1_, ...), custom_call_target="tpu_custom_call" | custom-call | flops 4831838208 | tf_op jit(solution)/shard_map/experts/pallas_call | solution.py:412
  143.2 8.9 %collective-permute-done.35 = bf16[128,1536]{1,0:T(8,128)(2,1)S(1)} collective-permute-done((bf16[128,1536]{1,0:T(8,128)(2,1)S(1)}, bf16[128,1536]{1,0:T(8,128)(2,1)S(1)}, u32[]{:S(2)}, u32[]{:S(2)}) %collective-permute-start.35) | collective-permute-done | bytes 393248 | tf_op jit(solution)/shard_map/ppermute | solution.py:33
  152.2 3.9 %collective-permute-start.36 = (bf16[128,1536]{1,0:T(8,128)(2,1)S(1)}, bf16[128,1536]{1,0:T(8,128)(2,1)S(1)}, u32[]{:S(2)}, u32[]{:S(2)}) collective-permute-start(bf16[128,1536]{1,0:T(8,128)(2,1)S(1)} %add_convert_fusion.1), channel_id=1, source_target_pairs={{0,16},{2,18},{4,20},{6,22},{8,24},{10,26},{12,28},{14,30},{16,0},... | collective-permute-start | bytes 1179656 | tf_op jit(solution)/shard_map/ppermute | solution.py:33
  156.2 11.1 %collective-permute-done.31 = bf16[128,1536]{1,0:T(8,128)(2,1)S(1)} collective-permute-done((bf16[128,1536]{1,0:T(8,128)(2,1)S(1)}, bf16[128,1536]{1,0:T(8,128)(2,1)S(1)}, u32[]{:S(2)}, u32[]{:S(2)}) %collective-permute-start.31) | collective-permute-done | bytes 393248 | tf_op jit(solution)/shard_map/ppermute | solution.py:33
  167.3 4.9 %collective-permute-done.36 = bf16[128,1536]{1,0:T(8,128)(2,1)S(1)} collective-permute-done((bf16[128,1536]{1,0:T(8,128)(2,1)S(1)}, bf16[128,1536]{1,0:T(8,128)(2,1)S(1)}, u32[]{:S(2)}, u32[]{:S(2)}) %collective-permute-start.36) | collective-permute-done | bytes 393248 | tf_op jit(solution)/shard_map/ppermute | solution.py:33
  (103 shorter events, 30.6 us)
Async XLA Ops:
  2.5 9.7 %collective-permute-start = (bf16[272,512]{1,0:T(8,128)(2,1)S(1)}, bf16[272,512]{1,0:T(8,128)(2,1)S(1)}, u32[]{:S(2)}, u32[]{:S(2)}) collective-permute-start(bf16[272,512]{1,0:T(8,128)(2,1)S(1)} %fusion.1.refs_0_), channel_id=1, source_target_pairs={{0,4},{2,6},{4,0},{6,2},{8,12},{10,14},{12,8},{14,10},{16,20},{18,... | collective-permute-start | bytes 835592 | tf_op jit(solution)/shard_map/ppermute | solution.py:33
  15.8 19.0 %collective-permute-start.4 = (bf16[1,1536,256]{2,1,0:T(8,128)(2,1)}, bf16[1,1536,256]{2,1,0:T(8,128)(2,1)S(1)}, u32[]{:S(2)}, u32[]{:S(2)}) collective-permute-start(bf16[1,1536,256]{2,1,0:T(8,128)(2,1)} %get-tuple-element.58), channel_id=1, source_target_pairs={{0,4},{2,6},{4,0},{6,2},{8,12},{10,14},{12,8},{14,10},{16,20},{18,... | collective-permute-start | bytes 2359304 | tf_op jit(solution)/shard_map/ppermute | solution.py:33
  17.6 18.7 %collective-permute-start.12 = (bf16[272,512]{1,0:T(8,128)(2,1)S(1)}, bf16[272,512]{1,0:T(8,128)(2,1)S(1)}, u32[]{:S(2)}, u32[]{:S(2)}) collective-permute-start(bf16[272,512]{1,0:T(8,128)(2,1)S(1)} %fusion.1.refs_0_), channel_id=1, source_target_pairs={{0,16},{2,18},{4,20},{6,22},{8,24},{10,26},{12,28},{14,30},{16,0},... | collective-permute-start | bytes 835592 | tf_op jit(solution)/shard_map/ppermute | solution.py:33
  20.2 17.6 %collective-permute-start.8 = (bf16[272,512]{1,0:T(8,128)(2,1)S(1)}, bf16[272,512]{1,0:T(8,128)(2,1)S(1)}, u32[]{:S(2)}, u32[]{:S(2)}) collective-permute-start(bf16[272,512]{1,0:T(8,128)(2,1)S(1)} %fusion.1.refs_0_), channel_id=1, source_target_pairs={{0,8},{2,10},{4,12},{6,14},{8,0},{10,2},{12,4},{14,6},{16,24},{18,... | collective-permute-start | bytes 835592 | tf_op jit(solution)/shard_map/ppermute | solution.py:33
  21.8 17.7 %collective-permute-start.1 = (bf16[128,1536]{1,0:T(8,128)(2,1)S(1)}, bf16[128,1536]{1,0:T(8,128)(2,1)S(1)}, u32[]{:S(2)}, u32[]{:S(2)}) collective-permute-start(bf16[128,1536]{1,0:T(8,128)(2,1)S(1)} %copy-done.2), channel_id=1, source_target_pairs={{0,1},{1,0},{2,3},{3,2},{4,5},{5,4},{6,7},{7,6},{8,9},{9,8},{10,11... | collective-permute-start | bytes 1179656 | tf_op jit(solution)/shard_map/ppermute | solution.py:33
  23.3 16.0 %collective-permute-start.6 = (bf16[272,512]{1,0:T(8,128)(2,1)S(1)}, bf16[272,512]{1,0:T(8,128)(2,1)S(1)}, u32[]{:S(2)}, u32[]{:S(2)}) collective-permute-start(bf16[272,512]{1,0:T(8,128)(2,1)S(1)} %fusion.1.refs_0_), channel_id=1, source_target_pairs={{0,2},{2,0},{4,6},{6,4},{8,10},{10,8},{12,14},{14,12},{16,18},{18,... | collective-permute-start | bytes 835592 | tf_op jit(solution)/shard_map/ppermute | solution.py:33
  34.8 24.5 %collective-permute-start.5 = (bf16[1,1536,256]{2,1,0:T(8,128)(2,1)S(1)}, bf16[1,1536,256]{2,1,0:T(8,128)(2,1)S(1)}, u32[]{:S(2)}, u32[]{:S(2)}) collective-permute-start(bf16[1,1536,256]{2,1,0:T(8,128)(2,1)S(1)} %collective-permute-done.4.refs_6_), channel_id=1, source_target_pairs={{0,1},{1,0},{2,3},{3,2},{4,5},{5,4},{6,7},{7,6},{8,9},{9,8},{10,11... | collective-permute-start | bytes 2359304 | tf_op jit(solution)/shard_map/ppermute | solution.py:33
  39.3 14.6 %collective-permute-start.13 = (bf16[272,512]{1,0:T(8,128)(2,1)S(1)}, bf16[272,512]{1,0:T(8,128)(2,1)S(1)}, u32[]{:S(2)}, u32[]{:S(2)}) collective-permute-start(bf16[272,512]{1,0:T(8,128)(2,1)S(1)} %collective-permute-done.12.refs_8_), channel_id=1, source_target_pairs={{0,2},{2,0},{4,6},{6,4},{8,10},{10,8},{12,14},{14,12},{16,18},{18,... | collective-permute-start | bytes 835592 | tf_op jit(solution)/shard_map/ppermute | solution.py:33
  39.5 15.8 %collective-permute-start.10 = (bf16[272,512]{1,0:T(8,128)(2,1)S(1)}, bf16[272,512]{1,0:T(8,128)(2,1)S(1)}, u32[]{:S(2)}, u32[]{:S(2)}) collective-permute-start(bf16[272,512]{1,0:T(8,128)(2,1)S(1)} %collective-permute-done.8.refs_4_), channel_id=1, source_target_pairs={{0,4},{2,6},{4,0},{6,2},{8,12},{10,14},{12,8},{14,10},{16,20},{18,... | collective-permute-start | bytes 835592 | tf_op jit(solution)/shard_map/ppermute | solution.py:33
  42.8 13.3 %collective-permute-start.9 = (bf16[272,512]{1,0:T(8,128)(2,1)S(1)}, bf16[272,512]{1,0:T(8,128)(2,1)S(1)}, u32[]{:S(2)}, u32[]{:S(2)}) collective-permute-start(bf16[272,512]{1,0:T(8,128)(2,1)S(1)} %collective-permute-done.8.refs_4_), channel_id=1, source_target_pairs={{0,2},{2,0},{4,6},{6,4},{8,10},{10,8},{12,14},{14,12},{16,18},{18,... | collective-permute-start | bytes 835592 | tf_op jit(solution)/shard_map/ppermute | solution.py:33
  46.1 13.2 %collective-permute-start.18 = (bf16[272,512]{1,0:T(8,128)(2,1)S(1)}, bf16[272,512]{1,0:T(8,128)(2,1)S(1)}, u32[]{:S(2)}, u32[]{:S(2)}) collective-permute-start(bf16[272,512]{1,0:T(8,128)(2,1)S(1)} %collective-permute-done.16.refs_12_), channel_id=1, source_target_pairs={{0,4},{2,6},{4,0},{6,2},{8,12},{10,14},{12,8},{14,10},{16,20},{18,... | collective-permute-start | bytes 835592 | tf_op jit(solution)/shard_map/ppermute | solution.py:33
  60.0 22.8 %collective-permute-start.3 = (bf16[1,1536,256]{2,1,0:T(8,128)(2,1)S(1)}, bf16[1,1536,256]{2,1,0:T(8,128)(2,1)S(1)}, u32[]{:S(2)}, u32[]{:S(2)}) collective-permute-start(bf16[1,1536,256]{2,1,0:T(8,128)(2,1)S(1)} %copy-done.13), channel_id=1, source_target_pairs={{0,4},{2,6},{4,0},{6,2},{8,12},{10,14},{12,8},{14,10},{16,20},{18,... | collective-permute-start | bytes 2359304 | tf_op jit(solution)/shard_map/ppermute | solution.py:33
  62.5 51.8 %collective-permute-start.25 = (bf16[1,512,1536]{2,1,0:T(8,128)(2,1)S(1)}, bf16[1,512,1536]{2,1,0:T(8,128)(2,1)S(1)}, u32[]{:S(2)}, u32[]{:S(2)}) collective-permute-start(bf16[1,512,1536]{2,1,0:T(8,128)(2,1)S(1)} %copy-done.4), channel_id=1, source_target_pairs={{0,4},{2,6},{4,0},{6,2},{8,12},{10,14},{12,8},{14,10},{16,20},{18,... | collective-permute-start | bytes 4718600 | tf_op jit(solution)/shard_map/ppermute | solution.py:33
  89.2 25.1 %collective-permute-start.24 = (bf16[1,1536,256]{2,1,0:T(8,128)(2,1)S(1)}, bf16[1,1536,256]{2,1,0:T(8,128)(2,1)S(1)}, u32[]{:S(2)}, u32[]{:S(2)}) collective-permute-start(bf16[1,1536,256]{2,1,0:T(8,128)(2,1)S(1)} %collective-permute-done.3.refs_7_), channel_id=1, source_target_pairs={{0,1},{1,0},{2,3},{3,2},{4,5},{5,4},{6,7},{7,6},{8,9},{9,8},{10,11... | collective-permute-start | bytes 2359304 | tf_op jit(solution)/shard_map/ppermute | solution.py:33
  91.9 22.4 %collective-permute-start.23 = (bf16[128,1536]{1,0:T(8,128)(2,1)S(1)}, bf16[128,1536]{1,0:T(8,128)(2,1)S(1)}, u32[]{:S(2)}, u32[]{:S(2)}) collective-permute-start(bf16[128,1536]{1,0:T(8,128)(2,1)S(1)} %get-tuple-element.69.refs_0_), channel_id=1, source_target_pairs={{0,16},{2,18},{4,20},{6,22},{8,24},{10,26},{12,28},{14,30},{16,0},... | collective-permute-start | bytes 1179656 | tf_op jit(solution)/shard_map/ppermute | solution.py:33
  100.0 14.3 %collective-permute-start.22 = (bf16[128,1536]{1,0:T(8,128)(2,1)S(1)}, bf16[128,1536]{1,0:T(8,128)(2,1)S(1)}, u32[]{:S(2)}, u32[]{:S(2)}) collective-permute-start(bf16[128,1536]{1,0:T(8,128)(2,1)S(1)} %get-tuple-element.69.refs_0_), channel_id=1, source_target_pairs={{0,8},{2,10},{4,12},{6,14},{8,0},{10,2},{12,4},{14,6},{16,24},{18,... | collective-permute-start | bytes 1179656 | tf_op jit(solution)/shard_map/ppermute | solution.py:33
  100.3 14.1 %collective-permute-start.21 = (bf16[128,1536]{1,0:T(8,128)(2,1)S(1)}, bf16[128,1536]{1,0:T(8,128)(2,1)S(1)}, u32[]{:S(2)}, u32[]{:S(2)}) collective-permute-start(bf16[128,1536]{1,0:T(8,128)(2,1)S(1)} %get-tuple-element.69.refs_0_), channel_id=1, source_target_pairs={{0,2},{2,0},{4,6},{6,4},{8,10},{10,8},{12,14},{14,12},{16,18},{18,... | collective-permute-start | bytes 1179656 | tf_op jit(solution)/shard_map/ppermute | solution.py:33
  114.3 12.1 %collective-permute-start.29 = (bf16[128,1536]{1,0:T(8,128)(2,1)S(1)}, bf16[128,1536]{1,0:T(8,128)(2,1)S(1)}, u32[]{:S(2)}, u32[]{:S(2)}) collective-permute-start(bf16[128,1536]{1,0:T(8,128)(2,1)S(1)} %collective-permute-done.23.refs_0_), channel_id=1, source_target_pairs={{0,8},{2,10},{4,12},{6,14},{8,0},{10,2},{12,4},{14,6},{16,24},{18,... | collective-permute-start | bytes 1179656 | tf_op jit(solution)/shard_map/ppermute | solution.py:33
  117.5 8.9 %collective-permute-start.28 = (bf16[128,1536]{1,0:T(8,128)(2,1)S(1)}, bf16[128,1536]{1,0:T(8,128)(2,1)S(1)}, u32[]{:S(2)}, u32[]{:S(2)}) collective-permute-start(bf16[128,1536]{1,0:T(8,128)(2,1)S(1)} %collective-permute-done.23.refs_0_), channel_id=1, source_target_pairs={{0,2},{2,0},{4,6},{6,4},{8,10},{10,8},{12,14},{14,12},{16,18},{18,... | collective-permute-start | bytes 1179656 | tf_op jit(solution)/shard_map/ppermute | solution.py:33
  122.0 34.2 %collective-permute-start.26 = (bf16[128,1536]{1,0:T(8,128)(2,1)S(1)}, bf16[128,1536]{1,0:T(8,128)(2,1)S(1)}, u32[]{:S(2)}, u32[]{:S(2)}) collective-permute-start(bf16[128,1536]{1,0:T(8,128)(2,1)S(1)} %get-tuple-element.82), channel_id=1, source_target_pairs={{0,2},{2,0},{4,6},{6,4},{8,10},{10,8},{12,14},{14,12},{16,18},{18,... | collective-permute-start | bytes 1179656 | tf_op jit(solution)/shard_map/ppermute | solution.py:33
  130.5 12.8 %collective-permute-start.32 = (bf16[128,1536]{1,0:T(8,128)(2,1)S(1)}, bf16[128,1536]{1,0:T(8,128)(2,1)S(1)}, u32[]{:S(2)}, u32[]{:S(2)}) collective-permute-start(bf16[128,1536]{1,0:T(8,128)(2,1)S(1)} %get-tuple-element.90), channel_id=1, source_target_pairs={{0,2},{2,0},{4,6},{6,4},{8,10},{10,8},{12,14},{14,12},{16,18},{18,... | collective-permute-start | bytes 1179656 | tf_op jit(solution)/shard_map/ppermute | solution.py:33
  140.1 12.0 %collective-permute-start.35 = (bf16[128,1536]{1,0:T(8,128)(2,1)S(1)}, bf16[128,1536]{1,0:T(8,128)(2,1)S(1)}, u32[]{:S(2)}, u32[]{:S(2)}) collective-permute-start(bf16[128,1536]{1,0:T(8,128)(2,1)S(1)} %add_convert_fusion.2), channel_id=1, source_target_pairs={{0,8},{2,10},{4,12},{6,14},{8,0},{10,2},{12,4},{14,6},{16,24},{18,... | collective-permute-start | bytes 1179656 | tf_op jit(solution)/shard_map/ppermute | solution.py:33
  142.0 25.3 %collective-permute-start.31 = (bf16[128,1536]{1,0:T(8,128)(2,1)S(1)}, bf16[128,1536]{1,0:T(8,128)(2,1)S(1)}, u32[]{:S(2)}, u32[]{:S(2)}) collective-permute-start(bf16[128,1536]{1,0:T(8,128)(2,1)S(1)} %add_convert_fusion.3), channel_id=1, source_target_pairs={{0,8},{2,10},{4,12},{6,14},{8,0},{10,2},{12,4},{14,6},{16,24},{18,... | collective-permute-start | bytes 1179656 | tf_op jit(solution)/shard_map/ppermute | solution.py:33
  152.2 19.9 %collective-permute-start.36 = (bf16[128,1536]{1,0:T(8,128)(2,1)S(1)}, bf16[128,1536]{1,0:T(8,128)(2,1)S(1)}, u32[]{:S(2)}, u32[]{:S(2)}) collective-permute-start(bf16[128,1536]{1,0:T(8,128)(2,1)S(1)} %add_convert_fusion.1), channel_id=1, source_target_pairs={{0,16},{2,18},{4,20},{6,22},{8,24},{10,26},{12,28},{14,30},{16,0},... | collective-permute-start | bytes 1179656 | tf_op jit(solution)/shard_map/ppermute | solution.py:33
  (29 other events, 496.8 us)

commit v6 on v5

--- a/solution.py
+++ b/solution.py
@@ -491,7 +491,7 @@
     walk = [bit for bit in bits_of(n_tok) if bit != swap]
     shards = spread(jnp.concatenate([kv_cache, told], axis=0), "tok", bits_of(n_tok))
 
-    tied, _ = lax.optimization_barrier((place_here, shards[swap]))
+    tied, _ = lax.optimization_barrier((place_here, shards[1]))
     lead, rest = shares_of(tied, n_head, w_gate_up)
     lead = crossed(lead, "tok", swap)
 

time: 173 us -> 169 us (0.977)
  waiting for transfers between devices: 74.1 us -> 68 us
    ppermute x36, waiting for transfers between devices: 73.9 us -> 67.9 us  [crossed(): return lax.ppermute(array, axis, [(i, i ^ flip) for i in range(count)])]
  transfers between devices with their start and end apart: 37 -> 37, of which waited for: 11 -> 13; matrix products, arithmetic and copies ran while one was open for 0% -> 0% of each run, Pallas kernels for 24% -> 24%
where the time goes in v6:
time: 169 us
  waiting for transfers between devices  68 us (40%)
  starting transfers between devices  49.4 us (29%)
  Pallas kernels  43 us (25%)
  local copies, waits for them, and re-layouts  4.09 us (2%)
  other arithmetic  3.26 us (2%)
    ppermute x36, waiting for transfers between devices, crossed(): return lax.ppermute(array, axis, [(i, i ^ flip) for i in range(count)])  67.9 us
    ppermute x36, starting transfers between devices, crossed(): return lax.ppermute(array, axis, [(i, i ^ flip) for i in range(count)])  48.1 us
    pallas_call x1, Pallas kernels, per_device(): pl.pallas_call(functools.partial(attend_kernel, n_tok, heads_at, n_head),...  19.6 us
    pallas_call x4, Pallas kernels, run_experts(): pl.pallas_call(functools.partial(expert_kernel, offsets, swap, len(swappe...  16.3 us
    unnamed x32, local copies, waits for them, and re-layouts  4.07 us
  transfers between devices with their start and end apart: 37, of which 13 were waited for; matrix products, arithmetic and copies ran while one was open for 0% of the time, Pallas kernels for 24%

profile of v6, /device:TPU:0, one launch (start us, length us, event | category | flops | bytes accessed | tf_op | source)
XLA Modules:
  0.0 168.7 jit_solution(9455225175172108754)
XLA Ops:
  7.8 2.9 %collective-permute-start.4 = (bf16[1,1536,256]{2,1,0:T(8,128)(2,1)}, bf16[1,1536,256]{2,1,0:T(8,128)(2,1)S(1)}, u32[]{:S(2)}, u32[]{:S(2)}) collective-permute-start(bf16[1,1536,256]{2,1,0:T(8,128)(2,1)} %get-tuple-element.58), channel_id=1, source_target_pairs={{0,4},{2,6},{4,0},{6,2},{8,12},{10,14},{12,8},{14,10},{16,20},{18,... | collective-permute-start | bytes 2359304 | tf_op jit(solution)/shard_map/ppermute | solution.py:33
  10.7 2.6 %collective-permute-start.12 = (bf16[272,512]{1,0:T(8,128)(2,1)S(1)}, bf16[272,512]{1,0:T(8,128)(2,1)S(1)}, u32[]{:S(2)}, u32[]{:S(2)}) collective-permute-start(bf16[272,512]{1,0:T(8,128)(2,1)S(1)} %fusion.1.refs_0_), channel_id=1, source_target_pairs={{0,16},{2,18},{4,20},{6,22},{8,24},{10,26},{12,28},{14,30},{16,0},... | collective-permute-start | bytes 835592 | tf_op jit(solution)/shard_map/ppermute | solution.py:33
  17.0 12.3 %collective-permute-done.4.refs_6_ = bf16[1,1536,256]{2,1,0:T(8,128)(2,1)S(1)} collective-permute-done((bf16[1,1536,256]{2,1,0:T(8,128)(2,1)}, bf16[1,1536,256]{2,1,0:T(8,128)(2,1)S(1)}, u32[]{:S(2)}, u32[]{:S(2)}) %collective-permute-start.4) | collective-permute-done | bytes 786464 | tf_op jit(solution)/shard_map/ppermute | solution.py:33
  29.3 2.1 %collective-permute-start.5 = (bf16[1,1536,256]{2,1,0:T(8,128)(2,1)S(1)}, bf16[1,1536,256]{2,1,0:T(8,128)(2,1)S(1)}, u32[]{:S(2)}, u32[]{:S(2)}) collective-permute-start(bf16[1,1536,256]{2,1,0:T(8,128)(2,1)S(1)} %collective-permute-done.4.refs_6_), channel_id=1, source_target_pairs={{0,1},{1,0},{2,3},{3,2},{4,5},{5,4},{6,7},{7,6},{8,9},{9,8},{10,11... | collective-permute-start | bytes 2359304 | tf_op jit(solution)/shard_map/ppermute | solution.py:33
  35.3 2.1 %collective-permute-start.10 = (bf16[272,512]{1,0:T(8,128)(2,1)S(1)}, bf16[272,512]{1,0:T(8,128)(2,1)S(1)}, u32[]{:S(2)}, u32[]{:S(2)}) collective-permute-start(bf16[272,512]{1,0:T(8,128)(2,1)S(1)} %collective-permute-done.8.refs_4_), channel_id=1, source_target_pairs={{0,4},{2,6},{4,0},{6,2},{8,12},{10,14},{12,8},{14,10},{16,20},{18,... | collective-permute-start | bytes 835592 | tf_op jit(solution)/shard_map/ppermute | solution.py:33
  38.2 4.4 %collective-permute-done.14.refs_10_ = bf16[272,512]{1,0:T(8,128)(2,1)S(1)} collective-permute-done((bf16[272,512]{1,0:T(8,128)(2,1)S(1)}, bf16[272,512]{1,0:T(8,128)(2,1)S(1)}, u32[]{:S(2)}, u32[]{:S(2)}) %collective-permute-start.14) | collective-permute-done | bytes 278560 | tf_op jit(solution)/shard_map/ppermute | solution.py:33
  44.0 2.1 %copy-done.3 = bf16[1536,1280]{1,0:T(8,128)(2,1)S(1)} copy-done((bf16[1536,1280]{1,0:T(8,128)(2,1)S(1)}, bf16[1536,1280]{1,0:T(8,128)(2,1)}, u32[]{:S(2)}) %copy-start.3) | copy-done | bytes 3932184
  46.2 3.2 %project.1 = (bf16[4,3,256,128]{3,2,1,0:T(8,128)(2,1)S(1)}, bf16[256,512]{1,0:T(8,128)(2,1)S(1)}, f32[256,128]{1,0:T(8,128)S(1)}, f32[8,512]{1,0:T(8,128)S(1)}, s32[1]{0:T(128)}) custom-call(s32[2]{0:T(128)S(1)} %pad_add_fusion.where_ref.scalar_ref, f32[8,128]{1,0:T(8,128)S(1)} %pad.9.requests_ref, s32[32,128]{1,0:T(8,128)S(1)} %bitcast.14, ...), custom_call_target="tpu_custom_call" | custom-call | flops 2013265920 | tf_op jit(solution)/shard_map/project/pallas_call | solution.py:509
  52.2 3.1 %collective-permute-start.15 = (bf16[272,512]{1,0:T(8,128)(2,1)S(1)}, bf16[272,512]{1,0:T(8,128)(2,1)S(1)}, u32[]{:S(2)}, u32[]{:S(2)}) collective-permute-start(bf16[272,512]{1,0:T(8,128)(2,1)S(1)} %collective-permute-done.14.refs_10_), channel_id=1, source_target_pairs={{0,2},{2,0},{4,6},{6,4},{8,10},{10,8},{12,14},{14,12},{16,18},{18,... | collective-permute-start | bytes 835592 | tf_op jit(solution)/shard_map/ppermute | solution.py:33
  55.9 2.5 %collective-permute-start.3 = (bf16[1,1536,256]{2,1,0:T(8,128)(2,1)S(1)}, bf16[1,1536,256]{2,1,0:T(8,128)(2,1)S(1)}, u32[]{:S(2)}, u32[]{:S(2)}) collective-permute-start(bf16[1,1536,256]{2,1,0:T(8,128)(2,1)S(1)} %copy-done.13), channel_id=1, source_target_pairs={{0,4},{2,6},{4,0},{6,2},{8,12},{10,14},{12,8},{14,10},{16,20},{18,... | collective-permute-start | bytes 2359304 | tf_op jit(solution)/shard_map/ppermute | solution.py:33
  58.6 19.6 %attend.1 = (bf16[128,768]{1,0:T(8,128)(2,1)S(1)}, bf16[128,768]{1,0:T(8,128)(2,1)S(1)}, bf16[256,128]{1,0:T(8,128)(2,1)S(1)}) custom-call(s32[2]{0:T(128)S(1)} %pad_add_fusion.where_ref.scalar_ref, s32[1]{0:T(128)} %get-tuple-element.56.first_ref, s32[256]{0:T(256)S(1)} %select_reduce_fusion.place_ref, ...), custom_call_target="tpu_custom_call" | custom-call | flops 25769803776 | tf_op jit(solution)/shard_map/attend/pallas_call | solution.py:543
  79.3 4.6 %collective-permute-done.20.refs_1_ = bf16[128,768]{1,0:T(8,128)(2,1)S(1)} collective-permute-done((bf16[128,768]{1,0:T(8,128)(2,1)S(1)}, bf16[128,768]{1,0:T(8,128)(2,1)S(1)}, u32[]{:S(2)}, u32[]{:S(2)}) %collective-permute-start.20) | collective-permute-done | bytes 196640 | tf_op jit(solution)/shard_map/ppermute | solution.py:33
  85.1 2.1 %close.1 = (bf16[128,1536]{1,0:T(8,128)(2,1)}, bf16[128,1536]{1,0:T(8,128)(2,1)S(1)}, bf16[128,1536]{1,0:T(8,128)(2,1)S(1)}) custom-call(s32[2]{0:T(128)S(1)} %pad_add_fusion.where_ref.scalar_ref, bf16[128,1536]{1,0:T(8,128)(2,1)S(1)} %copy-done.2, bf16[1536,1536]{1,0:T(8,128)(2,1)S(1)} %bitcast.9, f32[1,1536]{1,0:T(1,128)S(1)} %broadcast_in_dim.21.gain_ref, ...), custom_call_target="tpu_custom_call" | custom-call | flops 1207959552 | tf_op jit(solution)/shard_map/close/pallas_call | solution.py:574
  87.2 8.3 %collective-permute-start.23 = (bf16[128,1536]{1,0:T(8,128)(2,1)S(1)}, bf16[128,1536]{1,0:T(8,128)(2,1)S(1)}, u32[]{:S(2)}, u32[]{:S(2)}) collective-permute-start(bf16[128,1536]{1,0:T(8,128)(2,1)S(1)} %get-tuple-element.69.refs_0_), channel_id=1, source_target_pairs={{0,16},{2,18},{4,20},{6,22},{8,24},{10,26},{12,28},{14,30},{16,0},... | collective-permute-start | bytes 1179656 | tf_op jit(solution)/shard_map/ppermute | solution.py:33
  97.1 13.2 %collective-permute-done.25.refs_10_ = bf16[1,512,1536]{2,1,0:T(8,128)(2,1)S(1)} collective-permute-done((bf16[1,512,1536]{2,1,0:T(8,128)(2,1)S(1)}, bf16[1,512,1536]{2,1,0:T(8,128)(2,1)S(1)}, u32[]{:S(2)}, u32[]{:S(2)}) %collective-permute-start.25) | collective-permute-done | bytes 1572896 | tf_op jit(solution)/shard_map/ppermute | solution.py:33
  114.3 4.0 %experts.4 = (bf16[128,1536]{1,0:T(8,128)(2,1)S(1)}, bf16[128,1536]{1,0:T(8,128)(2,1)S(1)}) custom-call(s32[2]{0:T(128)S(1)} %pad_add_fusion.where_ref.scalar_ref, bf16[128,1536]{1,0:T(8,128)(2,1)S(1)} %get-tuple-element.69.refs_0_, bf16[128,1536]{1,0:T(8,128)(2,1)S(1)} %collective-permute-done.21.refs_1_, bf16[256,128]{1,0:T(8,128)(2,1)S(1)} %get-tuple-element.75.refs_2_, ...), custom_call_target="tpu_custom_call" | custom-call | flops 4831838208 | tf_op jit(solution)/shard_map/experts/pallas_call | solution.py:412
  118.4 3.8 %collective-permute-done.29.refs_0_ = bf16[128,1536]{1,0:T(8,128)(2,1)S(1)} collective-permute-done((bf16[128,1536]{1,0:T(8,128)(2,1)S(1)}, bf16[128,1536]{1,0:T(8,128)(2,1)S(1)}, u32[]{:S(2)}, u32[]{:S(2)}) %collective-permute-start.29) | collective-permute-done | bytes 393248 | tf_op jit(solution)/shard_map/ppermute | solution.py:33
  122.2 4.0 %experts.6 = (bf16[128,1536]{1,0:T(8,128)(2,1)S(1)}, bf16[128,1536]{1,0:T(8,128)(2,1)S(1)}) custom-call(s32[2]{0:T(128)S(1)} %pad_add_fusion.where_ref.scalar_ref, bf16[128,1536]{1,0:T(8,128)(2,1)S(1)} %collective-permute-done.23.refs_0_, bf16[128,1536]{1,0:T(8,128)(2,1)S(1)} %collective-permute-done.28.refs_1_, ...), custom_call_target="tpu_custom_call" | custom-call | flops 4831838208 | tf_op jit(solution)/shard_map/experts/pallas_call | solution.py:412
  126.9 4.0 %experts.7 = (bf16[128,1536]{1,0:T(8,128)(2,1)S(1)}, bf16[128,1536]{1,0:T(8,128)(2,1)S(1)}) custom-call(s32[2]{0:T(128)S(1)} %pad_add_fusion.where_ref.scalar_ref, bf16[128,1536]{1,0:T(8,128)(2,1)S(1)} %collective-permute-done.29.refs_0_, bf16[128,1536]{1,0:T(8,128)(2,1)S(1)} %collective-permute-done.33.refs_1_, ...), custom_call_target="tpu_custom_call" | custom-call | flops 4831838208 | tf_op jit(solution)/shard_map/experts/pallas_call | solution.py:412
  131.0 4.2 %experts.5 = (bf16[128,1536]{1,0:T(8,128)(2,1)S(1)}, bf16[128,1536]{1,0:T(8,128)(2,1)S(1)}) custom-call(s32[2]{0:T(128)S(1)} %pad_add_fusion.where_ref.scalar_ref, bf16[128,1536]{1,0:T(8,128)(2,1)S(1)} %collective-permute-done.22.refs_0_, bf16[128,1536]{1,0:T(8,128)(2,1)S(1)} %collective-permute-done.27.refs_1_, ...), custom_call_target="tpu_custom_call" | custom-call | flops 4831838208 | tf_op jit(solution)/shard_map/experts/pallas_call | solution.py:412
  139.1 8.9 %collective-permute-done.35 = bf16[128,1536]{1,0:T(8,128)(2,1)S(1)} collective-permute-done((bf16[128,1536]{1,0:T(8,128)(2,1)S(1)}, bf16[128,1536]{1,0:T(8,128)(2,1)S(1)}, u32[]{:S(2)}, u32[]{:S(2)}) %collective-permute-start.35) | collective-permute-done | bytes 393248 | tf_op jit(solution)/shard_map/ppermute | solution.py:33
  148.1 3.6 %collective-permute-start.36 = (bf16[128,1536]{1,0:T(8,128)(2,1)S(1)}, bf16[128,1536]{1,0:T(8,128)(2,1)S(1)}, u32[]{:S(2)}, u32[]{:S(2)}) collective-permute-start(bf16[128,1536]{1,0:T(8,128)(2,1)S(1)} %add_convert_fusion.1), channel_id=1, source_target_pairs={{0,16},{2,18},{4,20},{6,22},{8,24},{10,26},{12,28},{14,30},{16,0},... | collective-permute-start | bytes 1179656 | tf_op jit(solution)/shard_map/ppermute | solution.py:33
  151.7 11.4 %collective-permute-done.31 = bf16[128,1536]{1,0:T(8,128)(2,1)S(1)} collective-permute-done((bf16[128,1536]{1,0:T(8,128)(2,1)S(1)}, bf16[128,1536]{1,0:T(8,128)(2,1)S(1)}, u32[]{:S(2)}, u32[]{:S(2)}) %collective-permute-start.31) | collective-permute-done | bytes 393248 | tf_op jit(solution)/shard_map/ppermute | solution.py:33
  163.1 4.6 %collective-permute-done.36 = bf16[128,1536]{1,0:T(8,128)(2,1)S(1)} collective-permute-done((bf16[128,1536]{1,0:T(8,128)(2,1)S(1)}, bf16[128,1536]{1,0:T(8,128)(2,1)S(1)}, u32[]{:S(2)}, u32[]{:S(2)}) %collective-permute-start.36) | collective-permute-done | bytes 393248 | tf_op jit(solution)/shard_map/ppermute | solution.py:33
  (103 shorter events, 33.9 us)
Async XLA Ops:
  7.8 21.5 %collective-permute-start.4 = (bf16[1,1536,256]{2,1,0:T(8,128)(2,1)}, bf16[1,1536,256]{2,1,0:T(8,128)(2,1)S(1)}, u32[]{:S(2)}, u32[]{:S(2)}) collective-permute-start(bf16[1,1536,256]{2,1,0:T(8,128)(2,1)} %get-tuple-element.58), channel_id=1, source_target_pairs={{0,4},{2,6},{4,0},{6,2},{8,12},{10,14},{12,8},{14,10},{16,20},{18,... | collective-permute-start | bytes 2359304 | tf_op jit(solution)/shard_map/ppermute | solution.py:33
  10.7 20.6 %collective-permute-start.12 = (bf16[272,512]{1,0:T(8,128)(2,1)S(1)}, bf16[272,512]{1,0:T(8,128)(2,1)S(1)}, u32[]{:S(2)}, u32[]{:S(2)}) collective-permute-start(bf16[272,512]{1,0:T(8,128)(2,1)S(1)} %fusion.1.refs_0_), channel_id=1, source_target_pairs={{0,16},{2,18},{4,20},{6,22},{8,24},{10,26},{12,28},{14,30},{16,0},... | collective-permute-start | bytes 835592 | tf_op jit(solution)/shard_map/ppermute | solution.py:33
  13.3 19.6 %collective-permute-start.8 = (bf16[272,512]{1,0:T(8,128)(2,1)S(1)}, bf16[272,512]{1,0:T(8,128)(2,1)S(1)}, u32[]{:S(2)}, u32[]{:S(2)}) collective-permute-start(bf16[272,512]{1,0:T(8,128)(2,1)S(1)} %fusion.1.refs_0_), channel_id=1, source_target_pairs={{0,8},{2,10},{4,12},{6,14},{8,0},{10,2},{12,4},{14,6},{16,24},{18,... | collective-permute-start | bytes 835592 | tf_op jit(solution)/shard_map/ppermute | solution.py:33
  14.9 20.4 %collective-permute-start.1 = (bf16[128,1536]{1,0:T(8,128)(2,1)S(1)}, bf16[128,1536]{1,0:T(8,128)(2,1)S(1)}, u32[]{:S(2)}, u32[]{:S(2)}) collective-permute-start(bf16[128,1536]{1,0:T(8,128)(2,1)S(1)} %copy-done.2), channel_id=1, source_target_pairs={{0,1},{1,0},{2,3},{3,2},{4,5},{5,4},{6,7},{7,6},{8,9},{9,8},{10,11... | collective-permute-start | bytes 1179656 | tf_op jit(solution)/shard_map/ppermute | solution.py:33
  16.4 18.8 %collective-permute-start.6 = (bf16[272,512]{1,0:T(8,128)(2,1)S(1)}, bf16[272,512]{1,0:T(8,128)(2,1)S(1)}, u32[]{:S(2)}, u32[]{:S(2)}) collective-permute-start(bf16[272,512]{1,0:T(8,128)(2,1)S(1)} %fusion.1.refs_0_), channel_id=1, source_target_pairs={{0,4},{2,6},{4,0},{6,2},{8,12},{10,14},{12,8},{14,10},{16,20},{18,... | collective-permute-start | bytes 835592 | tf_op jit(solution)/shard_map/ppermute | solution.py:33
  29.3 26.0 %collective-permute-start.5 = (bf16[1,1536,256]{2,1,0:T(8,128)(2,1)S(1)}, bf16[1,1536,256]{2,1,0:T(8,128)(2,1)S(1)}, u32[]{:S(2)}, u32[]{:S(2)}) collective-permute-start(bf16[1,1536,256]{2,1,0:T(8,128)(2,1)S(1)} %collective-permute-done.4.refs_6_), channel_id=1, source_target_pairs={{0,1},{1,0},{2,3},{3,2},{4,5},{5,4},{6,7},{7,6},{8,9},{9,8},{10,11... | collective-permute-start | bytes 2359304 | tf_op jit(solution)/shard_map/ppermute | solution.py:33
  33.0 9.6 %collective-permute-start.14 = (bf16[272,512]{1,0:T(8,128)(2,1)S(1)}, bf16[272,512]{1,0:T(8,128)(2,1)S(1)}, u32[]{:S(2)}, u32[]{:S(2)}) collective-permute-start(bf16[272,512]{1,0:T(8,128)(2,1)S(1)} %collective-permute-done.12.refs_8_), channel_id=1, source_target_pairs={{0,4},{2,6},{4,0},{6,2},{8,12},{10,14},{12,8},{14,10},{16,20},{18,... | collective-permute-start | bytes 835592 | tf_op jit(solution)/shard_map/ppermute | solution.py:33
  35.2 14.2 %collective-permute-start.13 = (bf16[272,512]{1,0:T(8,128)(2,1)S(1)}, bf16[272,512]{1,0:T(8,128)(2,1)S(1)}, u32[]{:S(2)}, u32[]{:S(2)}) collective-permute-start(bf16[272,512]{1,0:T(8,128)(2,1)S(1)} %collective-permute-done.12.refs_8_), channel_id=1, source_target_pairs={{0,2},{2,0},{4,6},{6,4},{8,10},{10,8},{12,14},{14,12},{16,18},{18,... | collective-permute-start | bytes 835592 | tf_op jit(solution)/shard_map/ppermute | solution.py:33
  35.3 15.5 %collective-permute-start.10 = (bf16[272,512]{1,0:T(8,128)(2,1)S(1)}, bf16[272,512]{1,0:T(8,128)(2,1)S(1)}, u32[]{:S(2)}, u32[]{:S(2)}) collective-permute-start(bf16[272,512]{1,0:T(8,128)(2,1)S(1)} %collective-permute-done.8.refs_4_), channel_id=1, source_target_pairs={{0,4},{2,6},{4,0},{6,2},{8,12},{10,14},{12,8},{14,10},{16,20},{18,... | collective-permute-start | bytes 835592 | tf_op jit(solution)/shard_map/ppermute | solution.py:33
  38.2 13.9 %collective-permute-start.9 = (bf16[272,512]{1,0:T(8,128)(2,1)S(1)}, bf16[272,512]{1,0:T(8,128)(2,1)S(1)}, u32[]{:S(2)}, u32[]{:S(2)}) collective-permute-start(bf16[272,512]{1,0:T(8,128)(2,1)S(1)} %collective-permute-done.8.refs_4_), channel_id=1, source_target_pairs={{0,2},{2,0},{4,6},{6,4},{8,10},{10,8},{12,14},{14,12},{16,18},{18,... | collective-permute-start | bytes 835592 | tf_op jit(solution)/shard_map/ppermute | solution.py:33
  42.5 12.8 %collective-permute-start.18 = (bf16[272,512]{1,0:T(8,128)(2,1)S(1)}, bf16[272,512]{1,0:T(8,128)(2,1)S(1)}, u32[]{:S(2)}, u32[]{:S(2)}) collective-permute-start(bf16[272,512]{1,0:T(8,128)(2,1)S(1)} %collective-permute-done.16.refs_12_), channel_id=1, source_target_pairs={{0,4},{2,6},{4,0},{6,2},{8,12},{10,14},{12,8},{14,10},{16,20},{18,... | collective-permute-start | bytes 835592 | tf_op jit(solution)/shard_map/ppermute | solution.py:33
  55.9 23.4 %collective-permute-start.3 = (bf16[1,1536,256]{2,1,0:T(8,128)(2,1)S(1)}, bf16[1,1536,256]{2,1,0:T(8,128)(2,1)S(1)}, u32[]{:S(2)}, u32[]{:S(2)}) collective-permute-start(bf16[1,1536,256]{2,1,0:T(8,128)(2,1)S(1)} %copy-done.13), channel_id=1, source_target_pairs={{0,4},{2,6},{4,0},{6,2},{8,12},{10,14},{12,8},{14,10},{16,20},{18,... | collective-permute-start | bytes 2359304 | tf_op jit(solution)/shard_map/ppermute | solution.py:33
  58.5 51.8 %collective-permute-start.25 = (bf16[1,512,1536]{2,1,0:T(8,128)(2,1)S(1)}, bf16[1,512,1536]{2,1,0:T(8,128)(2,1)S(1)}, u32[]{:S(2)}, u32[]{:S(2)}) collective-permute-start(bf16[1,512,1536]{2,1,0:T(8,128)(2,1)S(1)} %copy-done.4), channel_id=1, source_target_pairs={{0,4},{2,6},{4,0},{6,2},{8,12},{10,14},{12,8},{14,10},{16,20},{18,... | collective-permute-start | bytes 4718600 | tf_op jit(solution)/shard_map/ppermute | solution.py:33
  84.0 28.3 %collective-permute-start.24 = (bf16[1,1536,256]{2,1,0:T(8,128)(2,1)S(1)}, bf16[1,1536,256]{2,1,0:T(8,128)(2,1)S(1)}, u32[]{:S(2)}, u32[]{:S(2)}) collective-permute-start(bf16[1,1536,256]{2,1,0:T(8,128)(2,1)S(1)} %collective-permute-done.3.refs_7_), channel_id=1, source_target_pairs={{0,1},{1,0},{2,3},{3,2},{4,5},{5,4},{6,7},{7,6},{8,9},{9,8},{10,11... | collective-permute-start | bytes 2359304 | tf_op jit(solution)/shard_map/ppermute | solution.py:33
  87.2 24.9 %collective-permute-start.23 = (bf16[128,1536]{1,0:T(8,128)(2,1)S(1)}, bf16[128,1536]{1,0:T(8,128)(2,1)S(1)}, u32[]{:S(2)}, u32[]{:S(2)}) collective-permute-start(bf16[128,1536]{1,0:T(8,128)(2,1)S(1)} %get-tuple-element.69.refs_0_), channel_id=1, source_target_pairs={{0,16},{2,18},{4,20},{6,22},{8,24},{10,26},{12,28},{14,30},{16,0},... | collective-permute-start | bytes 1179656 | tf_op jit(solution)/shard_map/ppermute | solution.py:33
  95.5 16.7 %collective-permute-start.22 = (bf16[128,1536]{1,0:T(8,128)(2,1)S(1)}, bf16[128,1536]{1,0:T(8,128)(2,1)S(1)}, u32[]{:S(2)}, u32[]{:S(2)}) collective-permute-start(bf16[128,1536]{1,0:T(8,128)(2,1)S(1)} %get-tuple-element.69.refs_0_), channel_id=1, source_target_pairs={{0,8},{2,10},{4,12},{6,14},{8,0},{10,2},{12,4},{14,6},{16,24},{18,... | collective-permute-start | bytes 1179656 | tf_op jit(solution)/shard_map/ppermute | solution.py:33
  97.1 15.2 %collective-permute-start.21 = (bf16[128,1536]{1,0:T(8,128)(2,1)S(1)}, bf16[128,1536]{1,0:T(8,128)(2,1)S(1)}, u32[]{:S(2)}, u32[]{:S(2)}) collective-permute-start(bf16[128,1536]{1,0:T(8,128)(2,1)S(1)} %get-tuple-element.69.refs_0_), channel_id=1, source_target_pairs={{0,2},{2,0},{4,6},{6,4},{8,10},{10,8},{12,14},{14,12},{16,18},{18,... | collective-permute-start | bytes 1179656 | tf_op jit(solution)/shard_map/ppermute | solution.py:33
  112.3 10.0 %collective-permute-start.29 = (bf16[128,1536]{1,0:T(8,128)(2,1)S(1)}, bf16[128,1536]{1,0:T(8,128)(2,1)S(1)}, u32[]{:S(2)}, u32[]{:S(2)}) collective-permute-start(bf16[128,1536]{1,0:T(8,128)(2,1)S(1)} %collective-permute-done.23.refs_0_), channel_id=1, source_target_pairs={{0,8},{2,10},{4,12},{6,14},{8,0},{10,2},{12,4},{14,6},{16,24},{18,... | collective-permute-start | bytes 1179656 | tf_op jit(solution)/shard_map/ppermute | solution.py:33
  113.8 8.5 %collective-permute-start.28 = (bf16[128,1536]{1,0:T(8,128)(2,1)S(1)}, bf16[128,1536]{1,0:T(8,128)(2,1)S(1)}, u32[]{:S(2)}, u32[]{:S(2)}) collective-permute-start(bf16[128,1536]{1,0:T(8,128)(2,1)S(1)} %collective-permute-done.23.refs_0_), channel_id=1, source_target_pairs={{0,2},{2,0},{4,6},{6,4},{8,10},{10,8},{12,14},{14,12},{16,18},{18,... | collective-permute-start | bytes 1179656 | tf_op jit(solution)/shard_map/ppermute | solution.py:33
  118.3 33.3 %collective-permute-start.26 = (bf16[128,1536]{1,0:T(8,128)(2,1)S(1)}, bf16[128,1536]{1,0:T(8,128)(2,1)S(1)}, u32[]{:S(2)}, u32[]{:S(2)}) collective-permute-start(bf16[128,1536]{1,0:T(8,128)(2,1)S(1)} %get-tuple-element.82), channel_id=1, source_target_pairs={{0,2},{2,0},{4,6},{6,4},{8,10},{10,8},{12,14},{14,12},{16,18},{18,... | collective-permute-start | bytes 1179656 | tf_op jit(solution)/shard_map/ppermute | solution.py:33
  126.3 12.8 %collective-permute-start.32 = (bf16[128,1536]{1,0:T(8,128)(2,1)S(1)}, bf16[128,1536]{1,0:T(8,128)(2,1)S(1)}, u32[]{:S(2)}, u32[]{:S(2)}) collective-permute-start(bf16[128,1536]{1,0:T(8,128)(2,1)S(1)} %get-tuple-element.90), channel_id=1, source_target_pairs={{0,2},{2,0},{4,6},{6,4},{8,10},{10,8},{12,14},{14,12},{16,18},{18,... | collective-permute-start | bytes 1179656 | tf_op jit(solution)/shard_map/ppermute | solution.py:33
  135.9 12.0 %collective-permute-start.35 = (bf16[128,1536]{1,0:T(8,128)(2,1)S(1)}, bf16[128,1536]{1,0:T(8,128)(2,1)S(1)}, u32[]{:S(2)}, u32[]{:S(2)}) collective-permute-start(bf16[128,1536]{1,0:T(8,128)(2,1)S(1)} %add_convert_fusion.2), channel_id=1, source_target_pairs={{0,8},{2,10},{4,12},{6,14},{8,0},{10,2},{12,4},{14,6},{16,24},{18,... | collective-permute-start | bytes 1179656 | tf_op jit(solution)/shard_map/ppermute | solution.py:33
  137.8 25.3 %collective-permute-start.31 = (bf16[128,1536]{1,0:T(8,128)(2,1)S(1)}, bf16[128,1536]{1,0:T(8,128)(2,1)S(1)}, u32[]{:S(2)}, u32[]{:S(2)}) collective-permute-start(bf16[128,1536]{1,0:T(8,128)(2,1)S(1)} %add_convert_fusion.3), channel_id=1, source_target_pairs={{0,8},{2,10},{4,12},{6,14},{8,0},{10,2},{12,4},{14,6},{16,24},{18,... | collective-permute-start | bytes 1179656 | tf_op jit(solution)/shard_map/ppermute | solution.py:33
  148.1 19.6 %collective-permute-start.36 = (bf16[128,1536]{1,0:T(8,128)(2,1)S(1)}, bf16[128,1536]{1,0:T(8,128)(2,1)S(1)}, u32[]{:S(2)}, u32[]{:S(2)}) collective-permute-start(bf16[128,1536]{1,0:T(8,128)(2,1)S(1)} %add_convert_fusion.1), channel_id=1, source_target_pairs={{0,16},{2,18},{4,20},{6,22},{8,24},{10,26},{12,28},{14,30},{16,0},... | collective-permute-start | bytes 1179656 | tf_op jit(solution)/shard_map/ppermute | solution.py:33
  (29 other events, 461.9 us)

commit v7 on v6

--- a/solution.py
+++ b/solution.py
@@ -250,7 +250,7 @@
             keys = jnp.concatenate([prior_ref[:, columns], own_ref[:, columns]], axis=0)
             scores = jnp.where(allowed, scored(queries, keys), MASKED)
             peak = jnp.max(scores, axis=-1, keepdims=True)
-            weights = jnp.where(allowed, jnp.exp(scores - peak), 0.0)
+            weights = jnp.exp(scores - peak)
             total = jnp.sum(weights, axis=-1, keepdims=True)
             mixed = jnp.dot(
                 weights.astype(jnp.bfloat16), keys, preferred_element_type=jnp.float32

time: 169 us -> 169 us (level)
  no operation moved by 1% of the time
where the time goes in v7:
time: 169 us
  waiting for transfers between devices  68.1 us (40%)
  starting transfers between devices  49.5 us (29%)
  Pallas kernels  42.8 us (25%)
  local copies, waits for them, and re-layouts  4.09 us (2%)
  other arithmetic  3.26 us (2%)
    ppermute x36, waiting for transfers between devices, crossed(): return lax.ppermute(array, axis, [(i, i ^ flip) for i in range(count)])  68.1 us
    ppermute x36, starting transfers between devices, crossed(): return lax.ppermute(array, axis, [(i, i ^ flip) for i in range(count)])  48.2 us
    pallas_call x1, Pallas kernels, per_device(): pl.pallas_call(functools.partial(attend_kernel, n_tok, heads_at, n_head),...  19.4 us
    pallas_call x4, Pallas kernels, run_experts(): pl.pallas_call(functools.partial(expert_kernel, offsets, swap, len(swappe...  16.3 us
    unnamed x32, local copies, waits for them, and re-layouts  4.07 us
  transfers between devices with their start and end apart: 37, of which 13 were waited for; matrix products, arithmetic and copies ran while one was open for 0% of the time, Pallas kernels for 24%

profile of v7, /device:TPU:0, one launch (start us, length us, event | category | flops | bytes accessed | tf_op | source)
XLA Modules:
  0.0 168.7 jit_solution(13717671621640221278)
XLA Ops:
  7.8 2.9 %collective-permute-start.4 = (bf16[1,1536,256]{2,1,0:T(8,128)(2,1)}, bf16[1,1536,256]{2,1,0:T(8,128)(2,1)S(1)}, u32[]{:S(2)}, u32[]{:S(2)}) collective-permute-start(bf16[1,1536,256]{2,1,0:T(8,128)(2,1)} %get-tuple-element.58), channel_id=1, source_target_pairs={{0,4},{2,6},{4,0},{6,2},{8,12},{10,14},{12,8},{14,10},{16,20},{18,... | collective-permute-start | bytes 2359304 | tf_op jit(solution)/shard_map/ppermute | solution.py:33
  10.7 2.6 %collective-permute-start.12 = (bf16[272,512]{1,0:T(8,128)(2,1)S(1)}, bf16[272,512]{1,0:T(8,128)(2,1)S(1)}, u32[]{:S(2)}, u32[]{:S(2)}) collective-permute-start(bf16[272,512]{1,0:T(8,128)(2,1)S(1)} %fusion.1.refs_0_), channel_id=1, source_target_pairs={{0,16},{2,18},{4,20},{6,22},{8,24},{10,26},{12,28},{14,30},{16,0},... | collective-permute-start | bytes 835592 | tf_op jit(solution)/shard_map/ppermute | solution.py:33
  17.0 12.3 %collective-permute-done.4.refs_6_ = bf16[1,1536,256]{2,1,0:T(8,128)(2,1)S(1)} collective-permute-done((bf16[1,1536,256]{2,1,0:T(8,128)(2,1)}, bf16[1,1536,256]{2,1,0:T(8,128)(2,1)S(1)}, u32[]{:S(2)}, u32[]{:S(2)}) %collective-permute-start.4) | collective-permute-done | bytes 786464 | tf_op jit(solution)/shard_map/ppermute | solution.py:33
  29.3 2.1 %collective-permute-start.5 = (bf16[1,1536,256]{2,1,0:T(8,128)(2,1)S(1)}, bf16[1,1536,256]{2,1,0:T(8,128)(2,1)S(1)}, u32[]{:S(2)}, u32[]{:S(2)}) collective-permute-start(bf16[1,1536,256]{2,1,0:T(8,128)(2,1)S(1)} %collective-permute-done.4.refs_6_), channel_id=1, source_target_pairs={{0,1},{1,0},{2,3},{3,2},{4,5},{5,4},{6,7},{7,6},{8,9},{9,8},{10,11... | collective-permute-start | bytes 2359304 | tf_op jit(solution)/shard_map/ppermute | solution.py:33
  35.3 2.1 %collective-permute-start.10 = (bf16[272,512]{1,0:T(8,128)(2,1)S(1)}, bf16[272,512]{1,0:T(8,128)(2,1)S(1)}, u32[]{:S(2)}, u32[]{:S(2)}) collective-permute-start(bf16[272,512]{1,0:T(8,128)(2,1)S(1)} %collective-permute-done.8.refs_4_), channel_id=1, source_target_pairs={{0,4},{2,6},{4,0},{6,2},{8,12},{10,14},{12,8},{14,10},{16,20},{18,... | collective-permute-start | bytes 835592 | tf_op jit(solution)/shard_map/ppermute | solution.py:33
  38.2 4.4 %collective-permute-done.14.refs_10_ = bf16[272,512]{1,0:T(8,128)(2,1)S(1)} collective-permute-done((bf16[272,512]{1,0:T(8,128)(2,1)S(1)}, bf16[272,512]{1,0:T(8,128)(2,1)S(1)}, u32[]{:S(2)}, u32[]{:S(2)}) %collective-permute-start.14) | collective-permute-done | bytes 278560 | tf_op jit(solution)/shard_map/ppermute | solution.py:33
  44.0 2.1 %copy-done.3 = bf16[1536,1280]{1,0:T(8,128)(2,1)S(1)} copy-done((bf16[1536,1280]{1,0:T(8,128)(2,1)S(1)}, bf16[1536,1280]{1,0:T(8,128)(2,1)}, u32[]{:S(2)}) %copy-start.3) | copy-done | bytes 3932184
  46.2 3.2 %project.1 = (bf16[4,3,256,128]{3,2,1,0:T(8,128)(2,1)S(1)}, bf16[256,512]{1,0:T(8,128)(2,1)S(1)}, f32[256,128]{1,0:T(8,128)S(1)}, f32[8,512]{1,0:T(8,128)S(1)}, s32[1]{0:T(128)}) custom-call(s32[2]{0:T(128)S(1)} %pad_add_fusion.where_ref.scalar_ref, f32[8,128]{1,0:T(8,128)S(1)} %pad.9.requests_ref, s32[32,128]{1,0:T(8,128)S(1)} %bitcast.14, ...), custom_call_target="tpu_custom_call" | custom-call | flops 2013265920 | tf_op jit(solution)/shard_map/project/pallas_call | solution.py:509
  52.2 3.1 %collective-permute-start.15 = (bf16[272,512]{1,0:T(8,128)(2,1)S(1)}, bf16[272,512]{1,0:T(8,128)(2,1)S(1)}, u32[]{:S(2)}, u32[]{:S(2)}) collective-permute-start(bf16[272,512]{1,0:T(8,128)(2,1)S(1)} %collective-permute-done.14.refs_10_), channel_id=1, source_target_pairs={{0,2},{2,0},{4,6},{6,4},{8,10},{10,8},{12,14},{14,12},{16,18},{18,... | collective-permute-start | bytes 835592 | tf_op jit(solution)/shard_map/ppermute | solution.py:33
  55.9 2.5 %collective-permute-start.3 = (bf16[1,1536,256]{2,1,0:T(8,128)(2,1)S(1)}, bf16[1,1536,256]{2,1,0:T(8,128)(2,1)S(1)}, u32[]{:S(2)}, u32[]{:S(2)}) collective-permute-start(bf16[1,1536,256]{2,1,0:T(8,128)(2,1)S(1)} %copy-done.13), channel_id=1, source_target_pairs={{0,4},{2,6},{4,0},{6,2},{8,12},{10,14},{12,8},{14,10},{16,20},{18,... | collective-permute-start | bytes 2359304 | tf_op jit(solution)/shard_map/ppermute | solution.py:33
  58.6 19.4 %attend.1 = (bf16[128,768]{1,0:T(8,128)(2,1)S(1)}, bf16[128,768]{1,0:T(8,128)(2,1)S(1)}, bf16[256,128]{1,0:T(8,128)(2,1)S(1)}) custom-call(s32[2]{0:T(128)S(1)} %pad_add_fusion.where_ref.scalar_ref, s32[1]{0:T(128)} %get-tuple-element.56.first_ref, s32[256]{0:T(256)S(1)} %select_reduce_fusion.place_ref, ...), custom_call_target="tpu_custom_call" | custom-call | flops 25769803776 | tf_op jit(solution)/shard_map/attend/pallas_call | solution.py:543
  79.2 4.6 %collective-permute-done.20.refs_1_ = bf16[128,768]{1,0:T(8,128)(2,1)S(1)} collective-permute-done((bf16[128,768]{1,0:T(8,128)(2,1)S(1)}, bf16[128,768]{1,0:T(8,128)(2,1)S(1)}, u32[]{:S(2)}, u32[]{:S(2)}) %collective-permute-start.20) | collective-permute-done | bytes 196640 | tf_op jit(solution)/shard_map/ppermute | solution.py:33
  84.9 2.1 %close.1 = (bf16[128,1536]{1,0:T(8,128)(2,1)}, bf16[128,1536]{1,0:T(8,128)(2,1)S(1)}, bf16[128,1536]{1,0:T(8,128)(2,1)S(1)}) custom-call(s32[2]{0:T(128)S(1)} %pad_add_fusion.where_ref.scalar_ref, bf16[128,1536]{1,0:T(8,128)(2,1)S(1)} %copy-done.2, bf16[1536,1536]{1,0:T(8,128)(2,1)S(1)} %bitcast.9, f32[1,1536]{1,0:T(1,128)S(1)} %broadcast_in_dim.21.gain_ref, ...), custom_call_target="tpu_custom_call" | custom-call | flops 1207959552 | tf_op jit(solution)/shard_map/close/pallas_call | solution.py:574
  87.0 8.3 %collective-permute-start.23 = (bf16[128,1536]{1,0:T(8,128)(2,1)S(1)}, bf16[128,1536]{1,0:T(8,128)(2,1)S(1)}, u32[]{:S(2)}, u32[]{:S(2)}) collective-permute-start(bf16[128,1536]{1,0:T(8,128)(2,1)S(1)} %get-tuple-element.69.refs_0_), channel_id=1, source_target_pairs={{0,16},{2,18},{4,20},{6,22},{8,24},{10,26},{12,28},{14,30},{16,0},... | collective-permute-start | bytes 1179656 | tf_op jit(solution)/shard_map/ppermute | solution.py:33
  96.9 13.4 %collective-permute-done.25.refs_10_ = bf16[1,512,1536]{2,1,0:T(8,128)(2,1)S(1)} collective-permute-done((bf16[1,512,1536]{2,1,0:T(8,128)(2,1)S(1)}, bf16[1,512,1536]{2,1,0:T(8,128)(2,1)S(1)}, u32[]{:S(2)}, u32[]{:S(2)}) %collective-permute-start.25) | collective-permute-done | bytes 1572896 | tf_op jit(solution)/shard_map/ppermute | solution.py:33
  114.1 4.0 %experts.4 = (bf16[128,1536]{1,0:T(8,128)(2,1)S(1)}, bf16[128,1536]{1,0:T(8,128)(2,1)S(1)}) custom-call(s32[2]{0:T(128)S(1)} %pad_add_fusion.where_ref.scalar_ref, bf16[128,1536]{1,0:T(8,128)(2,1)S(1)} %get-tuple-element.69.refs_0_, bf16[128,1536]{1,0:T(8,128)(2,1)S(1)} %collective-permute-done.21.refs_1_, bf16[256,128]{1,0:T(8,128)(2,1)S(1)} %get-tuple-element.75.refs_2_, ...), custom_call_target="tpu_custom_call" | custom-call | flops 4831838208 | tf_op jit(solution)/shard_map/experts/pallas_call | solution.py:412
  118.2 4.0 %collective-permute-done.29.refs_0_ = bf16[128,1536]{1,0:T(8,128)(2,1)S(1)} collective-permute-done((bf16[128,1536]{1,0:T(8,128)(2,1)S(1)}, bf16[128,1536]{1,0:T(8,128)(2,1)S(1)}, u32[]{:S(2)}, u32[]{:S(2)}) %collective-permute-start.29) | collective-permute-done | bytes 393248 | tf_op jit(solution)/shard_map/ppermute | solution.py:33
  122.2 4.0 %experts.6 = (bf16[128,1536]{1,0:T(8,128)(2,1)S(1)}, bf16[128,1536]{1,0:T(8,128)(2,1)S(1)}) custom-call(s32[2]{0:T(128)S(1)} %pad_add_fusion.where_ref.scalar_ref, bf16[128,1536]{1,0:T(8,128)(2,1)S(1)} %collective-permute-done.23.refs_0_, bf16[128,1536]{1,0:T(8,128)(2,1)S(1)} %collective-permute-done.28.refs_1_, ...), custom_call_target="tpu_custom_call" | custom-call | flops 4831838208 | tf_op jit(solution)/shard_map/experts/pallas_call | solution.py:412
  126.9 4.0 %experts.7 = (bf16[128,1536]{1,0:T(8,128)(2,1)S(1)}, bf16[128,1536]{1,0:T(8,128)(2,1)S(1)}) custom-call(s32[2]{0:T(128)S(1)} %pad_add_fusion.where_ref.scalar_ref, bf16[128,1536]{1,0:T(8,128)(2,1)S(1)} %collective-permute-done.29.refs_0_, bf16[128,1536]{1,0:T(8,128)(2,1)S(1)} %collective-permute-done.33.refs_1_, ...), custom_call_target="tpu_custom_call" | custom-call | flops 4831838208 | tf_op jit(solution)/shard_map/experts/pallas_call | solution.py:412
  131.0 4.2 %experts.5 = (bf16[128,1536]{1,0:T(8,128)(2,1)S(1)}, bf16[128,1536]{1,0:T(8,128)(2,1)S(1)}) custom-call(s32[2]{0:T(128)S(1)} %pad_add_fusion.where_ref.scalar_ref, bf16[128,1536]{1,0:T(8,128)(2,1)S(1)} %collective-permute-done.22.refs_0_, bf16[128,1536]{1,0:T(8,128)(2,1)S(1)} %collective-permute-done.27.refs_1_, ...), custom_call_target="tpu_custom_call" | custom-call | flops 4831838208 | tf_op jit(solution)/shard_map/experts/pallas_call | solution.py:412
  139.1 8.9 %collective-permute-done.35 = bf16[128,1536]{1,0:T(8,128)(2,1)S(1)} collective-permute-done((bf16[128,1536]{1,0:T(8,128)(2,1)S(1)}, bf16[128,1536]{1,0:T(8,128)(2,1)S(1)}, u32[]{:S(2)}, u32[]{:S(2)}) %collective-permute-start.35) | collective-permute-done | bytes 393248 | tf_op jit(solution)/shard_map/ppermute | solution.py:33
  148.1 3.6 %collective-permute-start.36 = (bf16[128,1536]{1,0:T(8,128)(2,1)S(1)}, bf16[128,1536]{1,0:T(8,128)(2,1)S(1)}, u32[]{:S(2)}, u32[]{:S(2)}) collective-permute-start(bf16[128,1536]{1,0:T(8,128)(2,1)S(1)} %add_convert_fusion.1), channel_id=1, source_target_pairs={{0,16},{2,18},{4,20},{6,22},{8,24},{10,26},{12,28},{14,30},{16,0},... | collective-permute-start | bytes 1179656 | tf_op jit(solution)/shard_map/ppermute | solution.py:33
  151.7 11.4 %collective-permute-done.31 = bf16[128,1536]{1,0:T(8,128)(2,1)S(1)} collective-permute-done((bf16[128,1536]{1,0:T(8,128)(2,1)S(1)}, bf16[128,1536]{1,0:T(8,128)(2,1)S(1)}, u32[]{:S(2)}, u32[]{:S(2)}) %collective-permute-start.31) | collective-permute-done | bytes 393248 | tf_op jit(solution)/shard_map/ppermute | solution.py:33
  163.1 4.6 %collective-permute-done.36 = bf16[128,1536]{1,0:T(8,128)(2,1)S(1)} collective-permute-done((bf16[128,1536]{1,0:T(8,128)(2,1)S(1)}, bf16[128,1536]{1,0:T(8,128)(2,1)S(1)}, u32[]{:S(2)}, u32[]{:S(2)}) %collective-permute-start.36) | collective-permute-done | bytes 393248 | tf_op jit(solution)/shard_map/ppermute | solution.py:33
  (103 shorter events, 33.7 us)
Async XLA Ops:
  7.8 21.5 %collective-permute-start.4 = (bf16[1,1536,256]{2,1,0:T(8,128)(2,1)}, bf16[1,1536,256]{2,1,0:T(8,128)(2,1)S(1)}, u32[]{:S(2)}, u32[]{:S(2)}) collective-permute-start(bf16[1,1536,256]{2,1,0:T(8,128)(2,1)} %get-tuple-element.58), channel_id=1, source_target_pairs={{0,4},{2,6},{4,0},{6,2},{8,12},{10,14},{12,8},{14,10},{16,20},{18,... | collective-permute-start | bytes 2359304 | tf_op jit(solution)/shard_map/ppermute | solution.py:33
  10.7 20.6 %collective-permute-start.12 = (bf16[272,512]{1,0:T(8,128)(2,1)S(1)}, bf16[272,512]{1,0:T(8,128)(2,1)S(1)}, u32[]{:S(2)}, u32[]{:S(2)}) collective-permute-start(bf16[272,512]{1,0:T(8,128)(2,1)S(1)} %fusion.1.refs_0_), channel_id=1, source_target_pairs={{0,16},{2,18},{4,20},{6,22},{8,24},{10,26},{12,28},{14,30},{16,0},... | collective-permute-start | bytes 835592 | tf_op jit(solution)/shard_map/ppermute | solution.py:33
  13.3 19.6 %collective-permute-start.8 = (bf16[272,512]{1,0:T(8,128)(2,1)S(1)}, bf16[272,512]{1,0:T(8,128)(2,1)S(1)}, u32[]{:S(2)}, u32[]{:S(2)}) collective-permute-start(bf16[272,512]{1,0:T(8,128)(2,1)S(1)} %fusion.1.refs_0_), channel_id=1, source_target_pairs={{0,8},{2,10},{4,12},{6,14},{8,0},{10,2},{12,4},{14,6},{16,24},{18,... | collective-permute-start | bytes 835592 | tf_op jit(solution)/shard_map/ppermute | solution.py:33
  14.9 20.4 %collective-permute-start.1 = (bf16[128,1536]{1,0:T(8,128)(2,1)S(1)}, bf16[128,1536]{1,0:T(8,128)(2,1)S(1)}, u32[]{:S(2)}, u32[]{:S(2)}) collective-permute-start(bf16[128,1536]{1,0:T(8,128)(2,1)S(1)} %copy-done.2), channel_id=1, source_target_pairs={{0,1},{1,0},{2,3},{3,2},{4,5},{5,4},{6,7},{7,6},{8,9},{9,8},{10,11... | collective-permute-start | bytes 1179656 | tf_op jit(solution)/shard_map/ppermute | solution.py:33
  16.4 18.8 %collective-permute-start.6 = (bf16[272,512]{1,0:T(8,128)(2,1)S(1)}, bf16[272,512]{1,0:T(8,128)(2,1)S(1)}, u32[]{:S(2)}, u32[]{:S(2)}) collective-permute-start(bf16[272,512]{1,0:T(8,128)(2,1)S(1)} %fusion.1.refs_0_), channel_id=1, source_target_pairs={{0,4},{2,6},{4,0},{6,2},{8,12},{10,14},{12,8},{14,10},{16,20},{18,... | collective-permute-start | bytes 835592 | tf_op jit(solution)/shard_map/ppermute | solution.py:33
  29.3 26.0 %collective-permute-start.5 = (bf16[1,1536,256]{2,1,0:T(8,128)(2,1)S(1)}, bf16[1,1536,256]{2,1,0:T(8,128)(2,1)S(1)}, u32[]{:S(2)}, u32[]{:S(2)}) collective-permute-start(bf16[1,1536,256]{2,1,0:T(8,128)(2,1)S(1)} %collective-permute-done.4.refs_6_), channel_id=1, source_target_pairs={{0,1},{1,0},{2,3},{3,2},{4,5},{5,4},{6,7},{7,6},{8,9},{9,8},{10,11... | collective-permute-start | bytes 2359304 | tf_op jit(solution)/shard_map/ppermute | solution.py:33
  33.0 9.6 %collective-permute-start.14 = (bf16[272,512]{1,0:T(8,128)(2,1)S(1)}, bf16[272,512]{1,0:T(8,128)(2,1)S(1)}, u32[]{:S(2)}, u32[]{:S(2)}) collective-permute-start(bf16[272,512]{1,0:T(8,128)(2,1)S(1)} %collective-permute-done.12.refs_8_), channel_id=1, source_target_pairs={{0,4},{2,6},{4,0},{6,2},{8,12},{10,14},{12,8},{14,10},{16,20},{18,... | collective-permute-start | bytes 835592 | tf_op jit(solution)/shard_map/ppermute | solution.py:33
  35.2 14.2 %collective-permute-start.13 = (bf16[272,512]{1,0:T(8,128)(2,1)S(1)}, bf16[272,512]{1,0:T(8,128)(2,1)S(1)}, u32[]{:S(2)}, u32[]{:S(2)}) collective-permute-start(bf16[272,512]{1,0:T(8,128)(2,1)S(1)} %collective-permute-done.12.refs_8_), channel_id=1, source_target_pairs={{0,2},{2,0},{4,6},{6,4},{8,10},{10,8},{12,14},{14,12},{16,18},{18,... | collective-permute-start | bytes 835592 | tf_op jit(solution)/shard_map/ppermute | solution.py:33
  35.3 15.5 %collective-permute-start.10 = (bf16[272,512]{1,0:T(8,128)(2,1)S(1)}, bf16[272,512]{1,0:T(8,128)(2,1)S(1)}, u32[]{:S(2)}, u32[]{:S(2)}) collective-permute-start(bf16[272,512]{1,0:T(8,128)(2,1)S(1)} %collective-permute-done.8.refs_4_), channel_id=1, source_target_pairs={{0,4},{2,6},{4,0},{6,2},{8,12},{10,14},{12,8},{14,10},{16,20},{18,... | collective-permute-start | bytes 835592 | tf_op jit(solution)/shard_map/ppermute | solution.py:33
  38.2 13.9 %collective-permute-start.9 = (bf16[272,512]{1,0:T(8,128)(2,1)S(1)}, bf16[272,512]{1,0:T(8,128)(2,1)S(1)}, u32[]{:S(2)}, u32[]{:S(2)}) collective-permute-start(bf16[272,512]{1,0:T(8,128)(2,1)S(1)} %collective-permute-done.8.refs_4_), channel_id=1, source_target_pairs={{0,2},{2,0},{4,6},{6,4},{8,10},{10,8},{12,14},{14,12},{16,18},{18,... | collective-permute-start | bytes 835592 | tf_op jit(solution)/shard_map/ppermute | solution.py:33
  42.5 12.8 %collective-permute-start.18 = (bf16[272,512]{1,0:T(8,128)(2,1)S(1)}, bf16[272,512]{1,0:T(8,128)(2,1)S(1)}, u32[]{:S(2)}, u32[]{:S(2)}) collective-permute-start(bf16[272,512]{1,0:T(8,128)(2,1)S(1)} %collective-permute-done.16.refs_12_), channel_id=1, source_target_pairs={{0,4},{2,6},{4,0},{6,2},{8,12},{10,14},{12,8},{14,10},{16,20},{18,... | collective-permute-start | bytes 835592 | tf_op jit(solution)/shard_map/ppermute | solution.py:33
  55.9 23.2 %collective-permute-start.3 = (bf16[1,1536,256]{2,1,0:T(8,128)(2,1)S(1)}, bf16[1,1536,256]{2,1,0:T(8,128)(2,1)S(1)}, u32[]{:S(2)}, u32[]{:S(2)}) collective-permute-start(bf16[1,1536,256]{2,1,0:T(8,128)(2,1)S(1)} %copy-done.13), channel_id=1, source_target_pairs={{0,4},{2,6},{4,0},{6,2},{8,12},{10,14},{12,8},{14,10},{16,20},{18,... | collective-permute-start | bytes 2359304 | tf_op jit(solution)/shard_map/ppermute | solution.py:33
  58.5 51.8 %collective-permute-start.25 = (bf16[1,512,1536]{2,1,0:T(8,128)(2,1)S(1)}, bf16[1,512,1536]{2,1,0:T(8,128)(2,1)S(1)}, u32[]{:S(2)}, u32[]{:S(2)}) collective-permute-start(bf16[1,512,1536]{2,1,0:T(8,128)(2,1)S(1)} %copy-done.4), channel_id=1, source_target_pairs={{0,4},{2,6},{4,0},{6,2},{8,12},{10,14},{12,8},{14,10},{16,20},{18,... | collective-permute-start | bytes 4718600 | tf_op jit(solution)/shard_map/ppermute | solution.py:33
  83.8 28.3 %collective-permute-start.24 = (bf16[1,1536,256]{2,1,0:T(8,128)(2,1)S(1)}, bf16[1,1536,256]{2,1,0:T(8,128)(2,1)S(1)}, u32[]{:S(2)}, u32[]{:S(2)}) collective-permute-start(bf16[1,1536,256]{2,1,0:T(8,128)(2,1)S(1)} %collective-permute-done.3.refs_7_), channel_id=1, source_target_pairs={{0,1},{1,0},{2,3},{3,2},{4,5},{5,4},{6,7},{7,6},{8,9},{9,8},{10,11... | collective-permute-start | bytes 2359304 | tf_op jit(solution)/shard_map/ppermute | solution.py:33
  87.0 24.9 %collective-permute-start.23 = (bf16[128,1536]{1,0:T(8,128)(2,1)S(1)}, bf16[128,1536]{1,0:T(8,128)(2,1)S(1)}, u32[]{:S(2)}, u32[]{:S(2)}) collective-permute-start(bf16[128,1536]{1,0:T(8,128)(2,1)S(1)} %get-tuple-element.69.refs_0_), channel_id=1, source_target_pairs={{0,16},{2,18},{4,20},{6,22},{8,24},{10,26},{12,28},{14,30},{16,0},... | collective-permute-start | bytes 1179656 | tf_op jit(solution)/shard_map/ppermute | solution.py:33
  95.4 16.7 %collective-permute-start.22 = (bf16[128,1536]{1,0:T(8,128)(2,1)S(1)}, bf16[128,1536]{1,0:T(8,128)(2,1)S(1)}, u32[]{:S(2)}, u32[]{:S(2)}) collective-permute-start(bf16[128,1536]{1,0:T(8,128)(2,1)S(1)} %get-tuple-element.69.refs_0_), channel_id=1, source_target_pairs={{0,8},{2,10},{4,12},{6,14},{8,0},{10,2},{12,4},{14,6},{16,24},{18,... | collective-permute-start | bytes 1179656 | tf_op jit(solution)/shard_map/ppermute | solution.py:33
  96.9 15.1 %collective-permute-start.21 = (bf16[128,1536]{1,0:T(8,128)(2,1)S(1)}, bf16[128,1536]{1,0:T(8,128)(2,1)S(1)}, u32[]{:S(2)}, u32[]{:S(2)}) collective-permute-start(bf16[128,1536]{1,0:T(8,128)(2,1)S(1)} %get-tuple-element.69.refs_0_), channel_id=1, source_target_pairs={{0,2},{2,0},{4,6},{6,4},{8,10},{10,8},{12,14},{14,12},{16,18},{18,... | collective-permute-start | bytes 1179656 | tf_op jit(solution)/shard_map/ppermute | solution.py:33
  112.1 10.2 %collective-permute-start.29 = (bf16[128,1536]{1,0:T(8,128)(2,1)S(1)}, bf16[128,1536]{1,0:T(8,128)(2,1)S(1)}, u32[]{:S(2)}, u32[]{:S(2)}) collective-permute-start(bf16[128,1536]{1,0:T(8,128)(2,1)S(1)} %collective-permute-done.23.refs_0_), channel_id=1, source_target_pairs={{0,8},{2,10},{4,12},{6,14},{8,0},{10,2},{12,4},{14,6},{16,24},{18,... | collective-permute-start | bytes 1179656 | tf_op jit(solution)/shard_map/ppermute | solution.py:33
  113.6 8.7 %collective-permute-start.28 = (bf16[128,1536]{1,0:T(8,128)(2,1)S(1)}, bf16[128,1536]{1,0:T(8,128)(2,1)S(1)}, u32[]{:S(2)}, u32[]{:S(2)}) collective-permute-start(bf16[128,1536]{1,0:T(8,128)(2,1)S(1)} %collective-permute-done.23.refs_0_), channel_id=1, source_target_pairs={{0,2},{2,0},{4,6},{6,4},{8,10},{10,8},{12,14},{14,12},{16,18},{18,... | collective-permute-start | bytes 1179656 | tf_op jit(solution)/shard_map/ppermute | solution.py:33
  118.1 33.5 %collective-permute-start.26 = (bf16[128,1536]{1,0:T(8,128)(2,1)S(1)}, bf16[128,1536]{1,0:T(8,128)(2,1)S(1)}, u32[]{:S(2)}, u32[]{:S(2)}) collective-permute-start(bf16[128,1536]{1,0:T(8,128)(2,1)S(1)} %get-tuple-element.82), channel_id=1, source_target_pairs={{0,2},{2,0},{4,6},{6,4},{8,10},{10,8},{12,14},{14,12},{16,18},{18,... | collective-permute-start | bytes 1179656 | tf_op jit(solution)/shard_map/ppermute | solution.py:33
  126.3 12.8 %collective-permute-start.32 = (bf16[128,1536]{1,0:T(8,128)(2,1)S(1)}, bf16[128,1536]{1,0:T(8,128)(2,1)S(1)}, u32[]{:S(2)}, u32[]{:S(2)}) collective-permute-start(bf16[128,1536]{1,0:T(8,128)(2,1)S(1)} %get-tuple-element.90), channel_id=1, source_target_pairs={{0,2},{2,0},{4,6},{6,4},{8,10},{10,8},{12,14},{14,12},{16,18},{18,... | collective-permute-start | bytes 1179656 | tf_op jit(solution)/shard_map/ppermute | solution.py:33
  135.9 12.0 %collective-permute-start.35 = (bf16[128,1536]{1,0:T(8,128)(2,1)S(1)}, bf16[128,1536]{1,0:T(8,128)(2,1)S(1)}, u32[]{:S(2)}, u32[]{:S(2)}) collective-permute-start(bf16[128,1536]{1,0:T(8,128)(2,1)S(1)} %add_convert_fusion.2), channel_id=1, source_target_pairs={{0,8},{2,10},{4,12},{6,14},{8,0},{10,2},{12,4},{14,6},{16,24},{18,... | collective-permute-start | bytes 1179656 | tf_op jit(solution)/shard_map/ppermute | solution.py:33
  137.8 25.3 %collective-permute-start.31 = (bf16[128,1536]{1,0:T(8,128)(2,1)S(1)}, bf16[128,1536]{1,0:T(8,128)(2,1)S(1)}, u32[]{:S(2)}, u32[]{:S(2)}) collective-permute-start(bf16[128,1536]{1,0:T(8,128)(2,1)S(1)} %add_convert_fusion.3), channel_id=1, source_target_pairs={{0,8},{2,10},{4,12},{6,14},{8,0},{10,2},{12,4},{14,6},{16,24},{18,... | collective-permute-start | bytes 1179656 | tf_op jit(solution)/shard_map/ppermute | solution.py:33
  148.1 19.6 %collective-permute-start.36 = (bf16[128,1536]{1,0:T(8,128)(2,1)S(1)}, bf16[128,1536]{1,0:T(8,128)(2,1)S(1)}, u32[]{:S(2)}, u32[]{:S(2)}) collective-permute-start(bf16[128,1536]{1,0:T(8,128)(2,1)S(1)} %add_convert_fusion.1), channel_id=1, source_target_pairs={{0,16},{2,18},{4,20},{6,22},{8,24},{10,26},{12,28},{14,30},{16,0},... | collective-permute-start | bytes 1179656 | tf_op jit(solution)/shard_map/ppermute | solution.py:33
  (29 other events, 461.4 us)
